TPU v7x, 768 devices: a whole 4x8x12 slice. The times are simulated.
768 devices in a mesh: grp: 8 (over y), slab: 12 (over z_lo, core), row: 8 (over x, z_hi).
Axes of the slice: x: 4, y: 8, z: 12 (z_hi: 2, z_lo: 6; z = z_hi * 6 + z_lo), core: 2. Of those that a mesh axis runs over, the one named last changes fastest.
Arguments:
- velocity: float32 [3, 384, 64, 1024], P(None, 'slab', 'grp', 'row'), may hold values from -6 to 6
- modes: float32 [196608, 512], P(('grp', 'slab', 'row')), may hold values from -6 to 6
- planes: int32 [64], replicated, may hold values from 0 to 383, as said below
- assign: int32 [12], replicated, may hold values from 0 to 11, each once
Outputs:
- advanced: float32 [3, 384, 64, 1024], P(None, 'slab', 'grp', 'row')
- basis: float32 [196608, 576], P(('grp', 'slab', 'row'))
- factor: float32 [576, 576], replicated
Inputs may be any that keep to these rules, and one draw needn't show every extreme that they name: `planes`: the 64 plane indices are distinct.
All inputs are finite; a program needn't handle non-finite values.
Results may differ from a plain program's by a relative error of at most 0.00005.
Values sent between devices are 32-bit elements; how exact they have to be, the bound alone decides.
No kernel may reach another device: no remote copies, remote signals or barrier semaphores. Data moves between devices by JAX's collectives and lax.ppermute only.
A program may use at most 32 MiB of HBM per device.

v0:
```python
import jax
import jax.numpy as jnp
from jax import lax
from jax.sharding import PartitionSpec as P

step_size = 0.05
viscosity = 1.0
third = 1.0 / 3.0
carry_back = -5.0 / 9.0
second_gain = 15.0 / 16.0


def padded(array, sides, width, wrap):
    for axis, dim in sides:
        devices, length = (lax.axis_size(axis), array.shape[dim])
        up = [(i, (i + 1) % devices) for i in range(devices if wrap else devices - 1)]
        down = [(j, i) for i, j in up]
        last = lax.slice_in_dim(array, length - width, length, axis=dim)
        initial = lax.slice_in_dim(array, 0, width, axis=dim)
        before = lax.ppermute(last, axis, up)
        after = lax.ppermute(initial, axis, down)
        array = jnp.concatenate([before, array, after], axis=dim)
    return array


def derivatives(parts):
    first = (parts[0] - 8.0 * parts[1] + 8.0 * parts[3] - parts[4]) / 12.0
    second = (-parts[0] + 16.0 * parts[1] - 30.0 * parts[2] + 16.0 * parts[3] - parts[4]) / 12.0
    return (first, second)


def tendency(field):
    wide = padded(field, (("grp", 2), ("slab", 1)), 2, True)
    walls = padded(field, (("row", 3),), 2, False)
    depth, across, height = (field.shape[1], field.shape[2], field.shape[3])
    along_z = [wide[:, k : k + depth, 2 : 2 + across, :] for k in range(5)]
    along_x = [wide[:, 2 : 2 + depth, k : k + across, :] for k in range(5)]
    along_y = [walls[:, :, :, k : k + height] for k in range(5)]
    dz_first, dz_second = derivatives(along_z)
    dx_first, dx_second = derivatives(along_x)
    dy_first, dy_second = derivatives(along_y)
    convect = field[0:1] * dx_first + field[1:2] * dy_first + field[2:3] * dz_first
    laplace = dx_second + dy_second + dz_second
    return viscosity * laplace - convect


def product(left, right):
    return jnp.dot(left, right, precision=lax.Precision.HIGHEST, preferred_element_type=jnp.float32)


def on_device(velocity, modes, planes, assign):
    count = planes.shape[0]
    slabs = lax.axis_size("slab")
    rows_total = modes.shape[0] * lax.axis_size("grp") * slabs * lax.axis_size("row")
    first_q = step_size * tendency(velocity)
    middle = velocity + third * first_q
    second_q = carry_back * first_q + step_size * tendency(middle)
    advanced = middle + second_gain * second_q
    depth = velocity.shape[1]
    local_z = planes - lax.axis_index("slab") * depth
    owned = (local_z >= 0) & (local_z < depth)
    picked = jnp.take(advanced, jnp.clip(local_z, 0, depth - 1), axis=1)
    picked = jnp.where(owned[None, :, None, None], picked, 0.0)
    picked = jnp.transpose(picked, (1, 0, 2, 3)).reshape(count, slabs, -1)
    arranged = jnp.take(picked, assign, axis=1)
    received = lax.psum_scatter(
        arranged.reshape(count, -1), "slab", scatter_dimension=1, tiled=True
    )
    snapshot_rows = received.T
    joined = jnp.concatenate([modes, snapshot_rows], axis=1)
    summed = lax.psum(product(joined.T, joined), ("grp", "slab", "row"))
    gram = summed / float(rows_total)
    lower = jnp.linalg.cholesky(gram)
    basis = jax.scipy.linalg.solve_triangular(lower, joined.T, lower=True).T
    return (advanced, basis, lower.T)


def solution(mesh):
    placed = (P(None, "slab", "grp", "row"), P(("grp", "slab", "row"), None), P(), P())
    return jax.shard_map(
        on_device,
        mesh=mesh,
        in_specs=placed,
        out_specs=(P(None, "slab", "grp", "row"), P(("grp", "slab", "row"), None), P()),
        check_vma=False,
    )
```

profile of v0, /device:TPU:1, one launch (start us, length us, event | category | flops | bytes accessed | tf_op | source)
XLA Modules:
  0.0 924.9 jit_solution(3039688649852246852)
XLA Ops:
  8.5 4.0 collective-permute-start
  12.5 3.8 collective-permute-start.1
  18.4 14.9 %collective-permute-start.2 = (f32[3,32,8,2]{3,2,1,0:T(8,128)}, f32[3,32,8,2]{3,2,1,0:T(8,128)S(1)}, u32[]{:S(2)}, u32[]{:S(2)}) collective-permute-start(f32[3,32,8,2]{3,2,1,0:T(8,128)} %get-tuple-element.49), channel_id=1, source_target_pairs={{0,1},{1,2},{2,3},{3,4},{4,5},{5,6},{6,7},{8,9},{9,10},{10,11},{11... | collective-permute-start | bytes 18440 | tf_op jit(solution)/shard_map/ppermute | solution.py:20
  36.6 30.6 %collective-permute-done.3 = f32[3,32,8,2]{3,2,1,0:T(8,128)S(1)} collective-permute-done((f32[3,32,8,2]{3,2,1,0:T(8,128)}, f32[3,32,8,2]{3,2,1,0:T(8,128)S(1)}, u32[]{:S(2)}, u32[]{:S(2)}) %collective-permute-start.3) | collective-permute-done | bytes 6176 | tf_op jit(solution)/shard_map/ppermute | solution.py:21
  67.3 21.9 %collective-permute-start.4 = (f32[3,2,12,128]{3,2,1,0:T(8,128)S(1)}, f32[3,2,12,128]{3,2,1,0:T(8,128)S(1)}, u32[]{:S(2)}, u32[]{:S(2)}) collective-permute-start(f32[3,2,12,128]{3,2,1,0:T(8,128)S(1)} %get-tuple-element.38), channel_id=1, source_target_pairs={{0,8},{8,16},{16,24},{24,32},{32,40},{40,48},{48,56},{56,64},{64,7... | collective-permute-start | bytes 110600 | tf_op jit(solution)/shard_map/ppermute | solution.py:20
  91.2 3.4 collective-permute-done.5
  97.6 4.6 collective-permute-start.7
  102.4 10.4 %collective-permute-start.8 = (f32[3,32,8,2]{3,2,1,0:T(8,128)S(1)}, f32[3,32,8,2]{3,2,1,0:T(8,128)S(1)}, u32[]{:S(2)}, u32[]{:S(2)}) collective-permute-start(f32[3,32,8,2]{3,2,1,0:T(8,128)S(1)} %get-tuple-element.43), channel_id=1, source_target_pairs={{0,1},{1,2},{2,3},{3,4},{4,5},{5,6},{6,7},{8,9},{9,10},{10,11},{11... | collective-permute-start | bytes 18440 | tf_op jit(solution)/shard_map/ppermute | solution.py:20
  116.1 5.7 collective-permute-start.11
  121.8 23.9 %collective-permute-done.9 = f32[3,32,8,2]{3,2,1,0:T(8,128)S(1)} collective-permute-done((f32[3,32,8,2]{3,2,1,0:T(8,128)S(1)}, f32[3,32,8,2]{3,2,1,0:T(8,128)S(1)}, u32[]{:S(2)}, u32[]{:S(2)}) %collective-permute-start.9) | collective-permute-done | bytes 6176 | tf_op jit(solution)/shard_map/ppermute | solution.py:21
  151.0 83.4 %reduce-scatter.2.cloned.1.call-done = f32[64,256]{1,0:T(8,128)} async-done(((f32[64,3072]{1,0:T(8,128)}), f32[64,256]{1,0:T(8,128)}) %reduce-scatter.2.cloned.1.call-update) | async-done | bytes 65552 | tf_op jit(solution)/shard_map/reduce_scatter | solution.py:66
  234.4 3.6 fusion.11
  238.8 476.9 %all-reduce.5.cloned.1.call-done = f32[576,576]{0,1:T(8,128)} async-done(((f32[576,576]{0,1:T(8,128)}), f32[576,576]{0,1:T(8,128)}) %all-reduce.5.cloned.1.call-update) | async-done | bytes 1327120 | tf_op jit(solution)/shard_map/psum | solution.py:71
  721.6 11.7 %cholesky.134 = f32[128,128]{1,0:T(8,128)S(1)} custom-call(f32[128,128]{1,0:T(8,128)S(1)} %cholesky.346), custom_call_target="Cholesky" | custom-call | tf_op jit(solution)/shard_map/jit(cholesky)/cholesky | solution.py:73
  733.9 10.4 %custom-call.39 = f32[1,128,128]{1,2,0:T(8,128)} custom-call(f32[1,128,128]{2,1,0:T(8,128)S(1)} %get-tuple-element.66), custom_call_target="InvertDiagBlocksLowerTriangular" | custom-call | tf_op jit(solution)/shard_map/jit(cholesky)/cholesky | solution.py:73
  747.4 13.3 %cholesky.274 = f32[128,128]{1,0:T(8,128)} custom-call(f32[128,128]{1,0:T(8,128)} %cholesky.350), custom_call_target="Cholesky" | custom-call | tf_op jit(solution)/shard_map/jit(cholesky)/cholesky | solution.py:73
  762.2 11.3 %custom-call.40 = f32[1,128,128]{1,2,0:T(8,128)} custom-call(f32[1,128,128]{2,1,0:T(8,128)} %get-tuple-element.63), custom_call_target="InvertDiagBlocksLowerTriangular" | custom-call | tf_op jit(solution)/shard_map/jit(cholesky)/cholesky | solution.py:73
  776.4 13.2 %cholesky.295 = f32[128,128]{1,0:T(8,128)} custom-call(f32[128,128]{1,0:T(8,128)} %cholesky.355), custom_call_target="Cholesky" | custom-call | tf_op jit(solution)/shard_map/jit(cholesky)/cholesky | solution.py:73
  791.7 11.3 %custom-call.41 = f32[1,128,128]{1,2,0:T(8,128)} custom-call(f32[1,128,128]{2,1,0:T(8,128)} %get-tuple-element.60), custom_call_target="InvertDiagBlocksLowerTriangular" | custom-call | tf_op jit(solution)/shard_map/jit(cholesky)/cholesky | solution.py:73
  805.9 13.4 %cholesky.314 = f32[128,128]{1,0:T(8,128)} custom-call(f32[128,128]{1,0:T(8,128)} %cholesky.360), custom_call_target="Cholesky" | custom-call | tf_op jit(solution)/shard_map/jit(cholesky)/cholesky | solution.py:73
  821.4 11.3 %custom-call.42 = f32[1,128,128]{1,2,0:T(8,128)} custom-call(f32[1,128,128]{2,1,0:T(8,128)} %get-tuple-element.57), custom_call_target="InvertDiagBlocksLowerTriangular" | custom-call | tf_op jit(solution)/shard_map/jit(cholesky)/cholesky | solution.py:73
  834.6 6.6 cholesky.334
  849.5 11.8 %while.1 = (s32[]{:T(128)}, f32[576,576]{1,0:T(8,128)}, s32[4,2]{0,1:T(2,128)S(1)}, f32[4,128,128]{2,1,0:T(8,128)S(1)}, s32[]{:T(128)}) while((s32[]{:T(128)}, f32[576,576]{1,0:T(8,128)}, s32[4,2]{0,1:T(2,128)S(1)}, f32[4,128,128]{2,1,0:T(8,128)S(1)}, s32[]{:T(128)}) %tuple.62), condition=%wide.while_cond, body=%wide.while_body.sunk | while | flops 2 | bytes 131189 | solution.py:74
  861.4 49.1 %custom-call.43 = f32[5,128,128]{1,2,0:T(8,128)S(1)} custom-call(f32[5,128,128]{2,1,0:T(8,128)S(1)} %pad_maximum_fusion.24), custom_call_target="InvertDiagBlocksLowerTriangular" | custom-call | tf_op jit(solution)/shard_map/jit(_solve_triangular)/triangular_solve | solution.py:74
  (141 shorter events, 68.1 us)
Async XLA Ops:
  7.2 28.0 %copy-start = (f32[3,32,8,128]{3,2,1,0:T(8,128)S(1)}, f32[3,32,8,128]{3,2,1,0:T(8,128)}, u32[]{:S(2)}) copy-start(f32[3,32,8,128]{3,2,1,0:T(8,128)} %param.4) | copy-start | bytes 1179652
  7.2 27.4 %copy-start.18 = (s32[12]{0:T(128)S(1)}, s32[12]{0:T(128)}, u32[]{:S(2)}) copy-start(s32[12]{0:T(128)} %param.7) | copy-start | bytes 148
  7.2 227.2 %reduce-scatter.2.cloned.1.call-start = ((), (), s32[]{:S(2)}) async-start(), calls=%async_computation.1 | async-start | bytes 851968 | tf_op jit(solution)/shard_map/reduce_scatter | solution.py:66
  8.5 58.8 %collective-permute-start = (f32[3,32,2,128]{3,2,1,0:T(2,128)S(1)}, f32[3,32,2,128]{3,2,1,0:T(2,128)S(1)}, u32[]{:S(2)}, u32[]{:S(2)}) collective-permute-start(f32[3,32,2,128]{3,2,1,0:T(2,128)S(1)} %get-tuple-element.51), channel_id=1, source_target_pairs={{0,96},{96,192},{192,288},{288,384},{384,480},{480,576},{576,672},... | collective-permute-start | bytes 294920 | tf_op jit(solution)/shard_map/ppermute | solution.py:20
  12.5 22.8 %copy-start.17 = (s32[64]{0:T(128)S(1)}, s32[64]{0:T(128)}, u32[]{:S(2)}) copy-start(s32[64]{0:T(128)} %param.6) | copy-start | bytes 772
  12.5 54.8 %collective-permute-start.1 = (f32[3,32,2,128]{3,2,1,0:T(2,128)S(1)}, f32[3,32,2,128]{3,2,1,0:T(2,128)S(1)}, u32[]{:S(2)}, u32[]{:S(2)}) collective-permute-start(f32[3,32,2,128]{3,2,1,0:T(2,128)S(1)} %get-tuple-element.52), channel_id=1, source_target_pairs={{96,0},{192,96},{288,192},{384,288},{480,384},{576,480},{672,576},... | collective-permute-start | bytes 294920 | tf_op jit(solution)/shard_map/ppermute | solution.py:21
  18.4 72.7 %collective-permute-start.2 = (f32[3,32,8,2]{3,2,1,0:T(8,128)}, f32[3,32,8,2]{3,2,1,0:T(8,128)S(1)}, u32[]{:S(2)}, u32[]{:S(2)}) collective-permute-start(f32[3,32,8,2]{3,2,1,0:T(8,128)} %get-tuple-element.49), channel_id=1, source_target_pairs={{0,1},{1,2},{2,3},{3,4},{4,5},{5,6},{6,7},{8,9},{9,10},{10,11},{11... | collective-permute-start | bytes 18440 | tf_op jit(solution)/shard_map/ppermute | solution.py:20
  33.3 33.9 %collective-permute-start.3 = (f32[3,32,8,2]{3,2,1,0:T(8,128)}, f32[3,32,8,2]{3,2,1,0:T(8,128)S(1)}, u32[]{:S(2)}, u32[]{:S(2)}) collective-permute-start(f32[3,32,8,2]{3,2,1,0:T(8,128)} %get-tuple-element.50), channel_id=1, source_target_pairs={{1,0},{2,1},{3,2},{4,3},{5,4},{6,5},{7,6},{9,8},{10,9},{11,10},{12... | collective-permute-start | bytes 18440 | tf_op jit(solution)/shard_map/ppermute | solution.py:21
  67.3 23.9 %collective-permute-start.4 = (f32[3,2,12,128]{3,2,1,0:T(8,128)S(1)}, f32[3,2,12,128]{3,2,1,0:T(8,128)S(1)}, u32[]{:S(2)}, u32[]{:S(2)}) collective-permute-start(f32[3,2,12,128]{3,2,1,0:T(8,128)S(1)} %get-tuple-element.38), channel_id=1, source_target_pairs={{0,8},{8,16},{16,24},{24,32},{32,40},{40,48},{48,56},{56,64},{64,7... | collective-permute-start | bytes 110600 | tf_op jit(solution)/shard_map/ppermute | solution.py:20
  89.2 5.4 collective-permute-start.5
  95.7 18.4 %collective-permute-start.6 = (f32[3,32,2,128]{3,2,1,0:T(2,128)S(1)}, f32[3,32,2,128]{3,2,1,0:T(2,128)S(1)}, u32[]{:S(2)}, u32[]{:S(2)}) collective-permute-start(f32[3,32,2,128]{3,2,1,0:T(2,128)S(1)} %get-tuple-element.45), channel_id=1, source_target_pairs={{0,96},{96,192},{192,288},{288,384},{384,480},{480,576},{576,672},... | collective-permute-start | bytes 294920 | tf_op jit(solution)/shard_map/ppermute | solution.py:20
  97.6 16.5 %collective-permute-start.7 = (f32[3,32,2,128]{3,2,1,0:T(2,128)S(1)}, f32[3,32,2,128]{3,2,1,0:T(2,128)S(1)}, u32[]{:S(2)}, u32[]{:S(2)}) collective-permute-start(f32[3,32,2,128]{3,2,1,0:T(2,128)S(1)} %get-tuple-element.46), channel_id=1, source_target_pairs={{96,0},{192,96},{288,192},{384,288},{480,384},{576,480},{672,576},... | collective-permute-start | bytes 294920 | tf_op jit(solution)/shard_map/ppermute | solution.py:21
  102.4 19.5 %collective-permute-start.8 = (f32[3,32,8,2]{3,2,1,0:T(8,128)S(1)}, f32[3,32,8,2]{3,2,1,0:T(8,128)S(1)}, u32[]{:S(2)}, u32[]{:S(2)}) collective-permute-start(f32[3,32,8,2]{3,2,1,0:T(8,128)S(1)} %get-tuple-element.43), channel_id=1, source_target_pairs={{0,1},{1,2},{2,3},{3,4},{4,5},{5,6},{6,7},{8,9},{9,10},{10,11},{11... | collective-permute-start | bytes 18440 | tf_op jit(solution)/shard_map/ppermute | solution.py:20
  112.8 32.9 %collective-permute-start.9 = (f32[3,32,8,2]{3,2,1,0:T(8,128)S(1)}, f32[3,32,8,2]{3,2,1,0:T(8,128)S(1)}, u32[]{:S(2)}, u32[]{:S(2)}) collective-permute-start(f32[3,32,8,2]{3,2,1,0:T(8,128)S(1)} %get-tuple-element.44), channel_id=1, source_target_pairs={{1,0},{2,1},{3,2},{4,3},{5,4},{6,5},{7,6},{9,8},{10,9},{11,10},{12... | collective-permute-start | bytes 18440 | tf_op jit(solution)/shard_map/ppermute | solution.py:21
  114.1 31.6 %collective-permute-start.10 = (f32[3,2,12,128]{3,2,1,0:T(8,128)S(1)}, f32[3,2,12,128]{3,2,1,0:T(8,128)S(1)}, u32[]{:S(2)}, u32[]{:S(2)}) collective-permute-start(f32[3,2,12,128]{3,2,1,0:T(8,128)S(1)} %get-tuple-element.36), channel_id=1, source_target_pairs={{0,8},{8,16},{16,24},{24,32},{32,40},{40,48},{48,56},{56,64},{64,7... | collective-permute-start | bytes 110600 | tf_op jit(solution)/shard_map/ppermute | solution.py:20
  116.1 29.7 %collective-permute-start.11 = (f32[3,2,12,128]{3,2,1,0:T(8,128)S(1)}, f32[3,2,12,128]{3,2,1,0:T(8,128)S(1)}, u32[]{:S(2)}, u32[]{:S(2)}) collective-permute-start(f32[3,2,12,128]{3,2,1,0:T(8,128)S(1)} %get-tuple-element.37), channel_id=1, source_target_pairs={{8,0},{16,8},{24,16},{32,24},{40,32},{48,40},{56,48},{64,56},{72,6... | collective-permute-start | bytes 110600 | tf_op jit(solution)/shard_map/ppermute | solution.py:21
  145.7 2.0 copy-start.15
  145.7 2.0 copy-start.16
  150.3 565.4 %all-reduce.5.cloned.1.call-start = ((), (), s32[]{:S(2)}) async-start(), calls=%async_computation.2 | async-start | bytes 2949120 | tf_op jit(solution)/shard_map/psum | solution.py:71
  234.4 4.3 copy-start.9
  718.3 2.0 copy-start.1
  721.5 23.8 %copy-start.3 = (f32[576,576]{1,0:T(8,128)S(1)}, f32[576,576]{1,0:T(8,128)}, u32[]{:S(2)}) copy-start(f32[576,576]{1,0:T(8,128)} %copy-done.2) | copy-start | bytes 3981316
  847.2 2.4 copy-start.11
  847.2 14.1 %copy-start.12 = (f32[128,64]{1,0:T(8,128)S(1)}, f32[128,64]{1,0:T(8,128)}, u32[]{:S(2)}) copy-start(f32[128,64]{1,0:T(8,128)} %pad_convert_fusion) | copy-start | bytes 98308
  (9 other events, 7.9 us)
Sparse Core Ops, SparseCore 0:
  150.4 83.9 reduce-scatter.1
  241.3 474.3 all-reduce.4
where the time goes:
time: 931 us; the launch traced here: 925 us
  waiting for transfers between devices  618 us (66%)
  other arithmetic  169 us (18%)
  starting transfers between devices  74.1 us (8%)
  local copies, waits for them, and re-layouts  30.1 us (3%)
  between operations  18.1 us (2%)
  matrix products  15.7 us (2%)
    psum x1, waiting for transfers between devices, on_device(): summed = lax.psum(product(joined.T, joined), ('grp', 'slab', 'row'))  477 us
    another operation x18, other arithmetic, on_device(): lower = jnp.linalg.cholesky(gram)  110 us
    reduce_scatter x1, waiting for transfers between devices, on_device(): lax.psum_scatter(arranged.reshape(count, -1), 'slab', scatter_dimension=1...  83.4 us
    ppermute x6, waiting for transfers between devices, padded(): after = lax.ppermute(initial, axis, down)  57.9 us
    ppermute x6, starting transfers between devices, padded(): before = lax.ppermute(last, axis, up)  55 us
    another operation x6, other arithmetic, on_device(): basis = jax.scipy.linalg.solve_triangular(lower, joined.T, lower=True).T  49.9 us
  transfers between devices with their start and end apart: 14, of which 5 were waited for; matrix products, arithmetic and copies ran while one was open for 1% of the time, Pallas kernels for 0%

commit v1 on v0

v1 whole, which is shorter than its diff:
```python
import jax
import jax.numpy as jnp
from jax import lax
from jax.experimental import pallas as pl
from jax.experimental.pallas import tpu as pltpu
from jax.sharding import PartitionSpec as P

step_size = 0.05
viscosity = 1.0
third = 1.0 / 3.0
carry_back = -5.0 / 9.0
second_gain = 15.0 / 16.0

ALL = ("grp", "slab", "row")
WIDE = 4
BLOCK = 128
VMEM_LIMIT = 48 * 1024 * 1024


def vmem_call(kernel, out_shape, in_specs, scratch=(), aliases=None, flops=0, moved=0):
    single = not isinstance(out_shape, (list, tuple))
    whole = pl.BlockSpec(memory_space=pltpu.VMEM)
    return pl.pallas_call(
        kernel,
        out_shape=out_shape,
        in_specs=in_specs,
        out_specs=whole if single else [whole] * len(out_shape),
        scratch_shapes=list(scratch),
        input_output_aliases=aliases or {},
        cost_estimate=pl.CostEstimate(flops=flops, bytes_accessed=moved, transcendentals=0),
        compiler_params=pltpu.CompilerParams(vmem_limit_bytes=VMEM_LIMIT),
    )


VM = pl.BlockSpec(memory_space=pltpu.VMEM)
SM = pl.BlockSpec(memory_space=pltpu.SMEM)


def product(left, right, dims):
    return lax.dot_general(
        left,
        right,
        (dims, ((), ())),
        precision=lax.Precision.HIGHEST,
        preferred_element_type=jnp.float32,
    )


def both_ways(low, high, axis, wrap):
    devices = lax.axis_size(axis)
    up = [(i, (i + 1) % devices) for i in range(devices if wrap else devices - 1)]
    down = [(j, i) for i, j in up]
    return lax.ppermute(high, axis, up), lax.ppermute(low, axis, down)


def pack_kernel(field_ref, first_ref, last_ref):
    comps, depth, rows, lanes = field_ref.shape
    planes = comps * depth
    group = lanes // WIDE
    lane = lax.broadcasted_iota(jnp.int32, (rows, lanes), 1)
    for tile in range(first_ref.shape[0]):
        head = jnp.zeros((rows, lanes), jnp.float32)
        tail = jnp.zeros((rows, lanes), jnp.float32)
        for q in range(min(group, planes - tile * group)):
            c, z = divmod(tile * group + q, depth)
            value = field_ref[c, z]
            here = (lane >= WIDE * q) & (lane < WIDE * (q + 1))
            head = jnp.where(here, pltpu.roll(value, (WIDE * q) % lanes, 1), head)
            tail = jnp.where(here, pltpu.roll(value, (WIDE * (q + 1)) % lanes, 1), tail)
        first_ref[tile] = head
        last_ref[tile] = tail


def parts_of(value, axis):
    size = value.shape[axis]
    return [pltpu.roll(value, shift % size, axis) for shift in (2, 1, -1, -2)]


def derivatives(parts, centre):
    far = parts[0], parts[3]
    first = ((far[0] - far[1]) + 8.0 * (parts[2] - parts[1])) * (1.0 / 12.0)
    second = (16.0 * (parts[1] + parts[2]) - (far[0] + far[1]) - 30.0 * centre) * (1.0 / 12.0)
    return first, second


def sections_kernel(
    assign_ref, row_ref, field_ref, before_ref, after_ref, out_ref, sent_ref, wide_ref, mid_ref, q_ref, place_ref
):
    comps, depth_wide, rows, lanes = field_ref.shape
    depth, across = out_ref.shape[1], out_ref.shape[2]
    group = lanes // WIDE
    lane = lax.broadcasted_iota(jnp.int32, (rows, lanes), 1)

    for c in range(comps):
        for z in range(depth_wide):
            tile, q = divmod(c * depth_wide + z, group)
            after = pltpu.roll(after_ref[tile], (-WIDE * q) % lanes, 1)
            before = pltpu.roll(before_ref[tile], (-WIDE * (q + 1)) % lanes, 1)
            halo = jnp.where(lane < WIDE, after, jnp.where(lane >= lanes - WIDE, before, 0.0))
            wide_ref[c, z, :, 0:lanes] = field_ref[c, z]
            wide_ref[c, z, :, lanes : 2 * lanes] = halo

    edge = lax.broadcasted_iota(jnp.int32, (rows, 2 * lanes), 1)
    outside = ((edge >= lanes + lanes // 2) & (row_ref[0] == 0)) | (
        (edge >= lanes) & (edge < lanes + lanes // 2) & (row_ref[0] == row_ref[1] - 1)
    )

    def tendency(speeds, centre, along_z, along_x, along_y):
        dz_first, dz_second = derivatives(along_z, centre)
        dx_first, dx_second = derivatives(along_x, centre)
        dy_first, dy_second = derivatives(along_y, centre)
        convect = speeds[0] * dx_first + speeds[1] * dy_first + speeds[2] * dz_first
        return viscosity * (dx_second + dy_second + dz_second) - convect

    def first_section(z, _):
        speeds = [wide_ref[c, z] for c in range(comps)]
        for c in range(comps):
            along_z = [wide_ref[c, z + k] for k in (-2, -1, 1, 2)]
            slope = tendency(speeds, speeds[c], along_z, parts_of(speeds[c], 0), parts_of(speeds[c], 1))
            q = step_size * slope
            mid_ref[c, z] = jnp.where(outside, 0.0, speeds[c] + third * q)
            q_ref[c, z] = q[:across, :lanes]
        return 0

    lax.fori_loop(2, depth_wide - 2, first_section, 0)

    def second_section(z, _):
        speeds = [mid_ref[c, z, 0:across, 0:lanes] for c in range(comps)]
        for c in range(comps):
            along_z = [mid_ref[c, z + k, 0:across, 0:lanes] for k in (-2, -1, 1, 2)]
            along_x = [p[:across] for p in parts_of(mid_ref[c, z, :, 0:lanes], 0)]
            along_y = [p[:, :lanes] for p in parts_of(mid_ref[c, z, 0:across, :], 1)]
            slope = tendency(speeds, speeds[c], along_z, along_x, along_y)
            q = carry_back * q_ref[c, z] + step_size * slope
            out_ref[c, z - WIDE] = speeds[c] + second_gain * q
        return 0

    lax.fori_loop(WIDE, WIDE + depth, second_section, 0)

    pieces = sent_ref.shape[0]
    for s in range(pieces):
        place_ref[assign_ref[s]] = s
    pairs = across // 2
    for b in range(pieces):
        c, x = b // pairs, 2 * (b % pairs)
        to = place_ref[b]
        sent_ref[to, :, 0:lanes] = out_ref[c, :, x, :]
        sent_ref[to, :, lanes : 2 * lanes] = out_ref[c, :, x + 1, :]


def pair_index(i, j):
    return i * 4 - (i * (i - 1)) // 2 + (j - i)


def modes_gram_kernel(modes_ref, out_ref):
    count = modes_ref.shape[1] // BLOCK
    for i in range(count):
        for j in range(i, count):
            at = pair_index(i, j) * BLOCK
            out_ref[at : at + BLOCK, :] = product(
                modes_ref[:, i * BLOCK : (i + 1) * BLOCK], modes_ref[:, j * BLOCK : (j + 1) * BLOCK], ((0,), (0,))
            )


def snapshot_gram_kernel(planes_ref, received_ref, modes_ref, packed_in, packed_ref, snap_ref):
    count = snap_ref.shape[0]
    blocks = modes_ref.shape[1] // BLOCK
    base = pair_index(blocks - 1, blocks - 1) * BLOCK + BLOCK
    packed_ref[0:base, :] = packed_in[0:base, :]
    for k in range(count):
        snap_ref[k : k + 1, :] = received_ref[pl.ds(planes_ref[k], 1), :]
    snap = snap_ref[...]
    cross = product(modes_ref[...], snap, ((0,), (1,)))
    for b in range(blocks):
        at, side = base + (b // 2) * BLOCK, (b % 2) * count
        packed_ref[at : at + BLOCK, side : side + count] = cross[b * BLOCK : (b + 1) * BLOCK, :]
    packed_ref[BLOCK - count : BLOCK, 0:count] = product(snap, snap, ((1,), (1,)))


def lanes_of(value, j):
    return jnp.broadcast_to(value[:, j : j + 1], value.shape)


def row_of(value, i):
    return jnp.broadcast_to(value[i : i + 1, :], value.shape)


def total(terms):
    while len(terms) > 1:
        terms = [a + b for a, b in zip(terms[::2], terms[1::2])] + ([terms[-1]] if len(terms) % 2 else [])
    return terms[0]


def eliminate(main, side, upper_ref, inverse_ref, first, last, rows):
    sub = lax.broadcasted_iota(jnp.int32, (8, BLOCK), 0)
    lane = lax.broadcasted_iota(jnp.int32, (8, BLOCK), 1)
    for p in range(first, last):
        top, left = main[p], side[p]
        columns = [lanes_of(top, 8 * p + j) for j in range(8)]
        a = [[row_of(columns[j], i) if j <= i else None for j in range(8)] for i in range(8)]
        scale = [None] * 8
        for j in range(8):
            scale[j] = lax.rsqrt(a[j][j])
            for i in range(j + 1, 8):
                a[i][j] = a[i][j] * scale[j]
            for m in range(j + 1, 8):
                for i in range(m, 8):
                    a[i][m] = a[i][m] - a[i][j] * a[m][j]
        v = [[None] * 8 for _ in range(8)]
        for j in range(8):
            v[j][j] = scale[j]
            for i in range(j + 1, 8):
                v[i][j] = -scale[i] * total([a[i][k] * v[k][j] for k in range(j, i)])
        top_rows = [row_of(top, j) for j in range(8)]
        left_rows = [row_of(left, j) for j in range(8)]
        zero = jnp.zeros((8, BLOCK), jnp.float32)
        down, back = [], []
        for j in range(8):
            column, line = zero, zero
            for i in range(j, 8):
                column = jnp.where(sub == i, v[i][j], column)
            for i in range(j + 1):
                line = jnp.where(sub == i, v[j][i], line)
            down.append(column)
            back.append(line)
        upper = total([down[j] * top_rows[j] for j in range(8)])
        lower = total([down[j] * left_rows[j] for j in range(8)])
        upper_ref[8 * p : 8 * p + 8, :] = jnp.where(lane >= 8 * p + sub, upper, 0.0)
        inverse_ref[8 * p : 8 * p + 8, :] = lower
        if p + 1 == rows:
            break
        upper_rows = [row_of(upper, j) for j in range(8)]
        lower_rows = [row_of(lower, j) for j in range(8)]
        top = total([back[j] * upper_rows[j] for j in range(8)])
        left = total([back[j] * lower_rows[j] for j in range(8)])
        top_rows = [row_of(top, j) for j in range(8)]
        left_rows = [row_of(left, j) for j in range(8)]
        for i in range(p + 1, rows):
            here = [lanes_of(main[i], 8 * p + j) for j in range(8)]
            main[i] = main[i] - total([here[j] * top_rows[j] for j in range(8)])
            side[i] = side[i] - total([here[j] * left_rows[j] for j in range(8)])


def factor_kernel(packed_ref, modes_ref, snap_ref, basis_ref, factor_ref, block_ref, upper_ref, inverse_ref, work_ref, done_ref):
    count = snap_ref.shape[0]
    blocks = modes_ref.shape[1] // BLOCK
    half = BLOCK // 16
    base = pair_index(blocks - 1, blocks - 1) * BLOCK + BLOCK
    wide = blocks + 1
    lane = lax.broadcasted_iota(jnp.int32, (BLOCK, BLOCK), 1)
    sub = lax.broadcasted_iota(jnp.int32, (BLOCK, BLOCK), 0)
    unit = jnp.where(lane == sub, 1.0, 0.0)

    for i in range(blocks):
        for j in range(i, blocks):
            at = pair_index(i, j) * BLOCK
            value = packed_ref[at : at + BLOCK, :]
            if i == j:
                value = jnp.where(lane >= sub, value, value.T)
            block_ref[i * wide + j] = value
        at = base + (i // 2) * BLOCK
        pair = packed_ref[at : at + BLOCK, :]
        if i % 2:
            pair = pltpu.roll(pair, count, 1)
        block_ref[i * wide + blocks] = jnp.where(lane < count, pair, 0.0)
        work_ref[i] = modes_ref[:, i * BLOCK : (i + 1) * BLOCK]
    block_ref[blocks * wide + blocks] = unit
    block_ref[blocks * wide + blocks, 0:count, 0:count] = packed_ref[BLOCK - count : BLOCK, 0:count]
    work_ref[blocks] = jnp.zeros(work_ref.shape[1:], jnp.float32)
    work_ref[blocks, :, 0:count] = snap_ref[...].T

    def one_block(b, _):
        mine = b * wide + b
        rows = BLOCK // 8
        inverse_ref[...] = unit
        upper_ref[...] = unit
        main = [block_ref[mine, 8 * i : 8 * i + 8, :] for i in range(rows)]
        side = [inverse_ref[8 * i : 8 * i + 8, :] for i in range(rows)]
        eliminate(main, side, upper_ref, inverse_ref, 0, half, rows)

        @pl.when(b < blocks)
        def _():
            eliminate(main, side, upper_ref, inverse_ref, half, rows, rows)

        block_ref[mine] = upper_ref[...]
        inverse = inverse_ref[...]
        done = product(work_ref[b], inverse, ((1,), (1,)))
        done_ref[b] = done

        def along(j, _):
            block_ref[b * wide + j] = product(inverse, block_ref[b * wide + j], ((1,), (0,)))
            return 0

        lax.fori_loop(b + 1, wide, along, 0)

        def across(j, _):
            line = block_ref[b * wide + j]
            work_ref[j] = work_ref[j] - product(done, line, ((1,), (0,)))

            def down(i, _):
                block_ref[i * wide + j] = block_ref[i * wide + j] - product(block_ref[b * wide + i], line, ((0,), (0,)))
                return 0

            lax.fori_loop(b + 1, j + 1, down, 0)
            return 0

        lax.fori_loop(b + 1, wide, across, 0)
        return 0

    lax.fori_loop(0, wide, one_block, 0)

    for i in range(blocks):
        basis_ref[:, i * BLOCK : (i + 1) * BLOCK] = done_ref[i]
        for j in range(blocks):
            value = block_ref[i * wide + j] if j >= i else jnp.zeros((BLOCK, BLOCK), jnp.float32)
            factor_ref[i * BLOCK : (i + 1) * BLOCK, j * BLOCK : (j + 1) * BLOCK] = value
        factor_ref[i * BLOCK : (i + 1) * BLOCK, blocks * BLOCK :] = block_ref[i * wide + blocks, :, 0:count]
        factor_ref[blocks * BLOCK :, i * BLOCK : (i + 1) * BLOCK] = jnp.zeros((count, BLOCK), jnp.float32)
    basis_ref[:, blocks * BLOCK :] = done_ref[blocks, :, 0:count]
    factor_ref[blocks * BLOCK :, blocks * BLOCK :] = block_ref[blocks * wide + blocks, 0:count, 0:count]


def f32(*shape):
    return jax.ShapeDtypeStruct(shape, jnp.float32)


def sections(velocity, assign):
    comps, depth, across, height = velocity.shape
    before, after = both_ways(velocity[:, :, :WIDE], velocity[:, :, across - WIDE :], "grp", True)
    field = jnp.concatenate([velocity, after, before], axis=2)
    before, after = both_ways(field[:, :WIDE], field[:, depth - WIDE :], "slab", True)
    field = jnp.concatenate([before, field, after], axis=1)
    shape = field.shape
    tiles = -(-shape[0] * shape[1] * WIDE // height)
    packed = f32(tiles, shape[2], height)
    first, last = vmem_call(pack_kernel, [packed, packed], [VM], moved=4 * field.size)(field)
    before, after = both_ways(first, last, "row", False)
    where = jnp.stack([lax.axis_index("row"), lax.axis_size("row")]).astype(jnp.int32)
    pieces = comps * across // 2
    return vmem_call(
        sections_kernel,
        [f32(*velocity.shape), f32(pieces, depth, 2 * height)],
        [SM, SM, VM, VM, VM],
        scratch=[
            pltpu.VMEM((comps, shape[1], shape[2], 2 * height), jnp.float32),
            pltpu.VMEM((comps, shape[1], shape[2], 2 * height), jnp.float32),
            pltpu.VMEM((comps, shape[1], across, height), jnp.float32),
            pltpu.SMEM((pieces,), jnp.int32),
        ],
        moved=8 * velocity.size,
    )(assign, where, field, before, after)


def on_device(velocity, modes, planes, assign):
    count, rank, held = planes.shape[0], modes.shape[1], modes.shape[0]
    devices = lax.axis_size("grp") * lax.axis_size("slab") * lax.axis_size("row")
    blocks = rank // BLOCK
    rows = (blocks * (blocks + 1) // 2 + blocks // 2) * BLOCK
    packed = vmem_call(modes_gram_kernel, f32(rows, BLOCK), [VM], flops=12 * held * rank * rank, moved=4 * modes.size)(modes)

    advanced, sent = sections(velocity, assign)
    received = lax.all_to_all(sent, "slab", 0, 0, tiled=True).reshape(-1, sent.shape[2])
    packed, snap = vmem_call(
        snapshot_gram_kernel, [f32(rows, BLOCK), f32(count, held)], [SM, VM, VM, VM], aliases={3: 0}
    )(planes, received, modes, packed)

    shares = packed.reshape(devices, rows // devices, BLOCK)
    shares = lax.all_to_all(shares, ALL, 0, 0, tiled=True)
    share = jnp.sum(shares, axis=0, keepdims=True) * (1.0 / float(held * devices))
    gram = lax.all_to_all(jnp.broadcast_to(share, shares.shape), ALL, 0, 0, tiled=True)

    wide = blocks + 1
    basis, factor = vmem_call(
        factor_kernel,
        [f32(held, rank + count), f32(rank + count, rank + count)],
        [VM, VM, VM],
        scratch=[
            pltpu.VMEM((wide * wide, BLOCK, BLOCK), jnp.float32),
            pltpu.VMEM((BLOCK, BLOCK), jnp.float32),
            pltpu.VMEM((BLOCK, BLOCK), jnp.float32),
            pltpu.VMEM((wide, held, BLOCK), jnp.float32),
            pltpu.VMEM((wide, held, BLOCK), jnp.float32),
        ],
    )(gram.reshape(rows, BLOCK), modes, snap)
    return (advanced, basis, factor)


def solution(mesh):
    placed = (P(None, "slab", "grp", "row"), P(("grp", "slab", "row"), None), P(), P())
    return jax.shard_map(
        on_device,
        mesh=mesh,
        in_specs=placed,
        out_specs=(P(None, "slab", "grp", "row"), P(("grp", "slab", "row"), None), P()),
        check_vma=False,
    )
```

time: 931 us -> 240 us (0.26)
  waiting for transfers between devices: 618 us -> 32.4 us
  other arithmetic: 169 us -> 1.86 us
  blocking collectives: 0 us -> 111 us
  Pallas kernels: 0 us -> 45.2 us
  starting transfers between devices: 74.1 us -> 45.6 us
  local copies, waits for them, and re-layouts: 30.1 us -> 2.5 us
  between operations: 18.1 us -> 0.76 us
  matrix products: 15.7 us -> 0 us
    psum x1 -> x0, waiting for transfers between devices: 477 us -> none  [on_device(): summed = lax.psum(product(joined.T, joined), ('grp', 'slab', 'row'))]
    another operation x24 -> x1, other arithmetic: 160 us -> 0.08 us  [sections(): jnp.stack([lax.axis_index('row'), lax.axis_size('row')]).astype(jnp.int32)]
    all_to_all x0 -> x2, blocking collectives: none -> 111 us  [the longest x1 55.8 us: on_device(): lax.all_to_all(jnp.broadcast_to(share, shares.shape), ALL, 0, 0, tiled=True)]
    reduce_scatter x1 -> x0, waiting for transfers between devices: 83.4 us -> none  [on_device(): lax.psum_scatter(arranged.reshape(count, -1), 'slab', scatter_dimension=1...]
    pallas_call x0 -> x5, Pallas kernels: none -> 45.2 us  [the longest x1 31.2 us: on_device(): vmem_call(factor_kernel, [f32(held, rank + count), f32(rank + count, rank...]
    ppermute x12 -> x6, waiting for transfers between devices: 57.9 us -> 16.4 us  [both_ways(): return (lax.ppermute(high, axis, up), lax.ppermute(low, axis, down))]
    ppermute x12 -> x6, starting transfers between devices: 73.6 us -> 36.2 us  [both_ways(): return (lax.ppermute(high, axis, up), lax.ppermute(low, axis, down))]
    all_to_all x0 -> x1, waiting for transfers between devices: none -> 16 us  [on_device(): lax.all_to_all(sent, 'slab', 0, 0, tiled=True).reshape(-1, sent.shape[2])]
  transfers between devices with their start and end apart: 14 -> 7, of which waited for: 5 -> 5; matrix products, arithmetic and copies ran while one was open for 1% -> 0% of each run, Pallas kernels for 0% -> 1%
where the time goes in v1:
time: 240 us
  blocking collectives  111 us (46%)
  starting transfers between devices  45.6 us (19%)
  Pallas kernels  45.2 us (19%)
  waiting for transfers between devices  32.4 us (14%)
  local copies, waits for them, and re-layouts  2.5 us (1%)
    all_to_all x1, blocking collectives, on_device(): lax.all_to_all(jnp.broadcast_to(share, shares.shape), ALL, 0, 0, tiled=True)  55.8 us
    all_to_all x1, blocking collectives, on_device(): shares = lax.all_to_all(shares, ALL, 0, 0, tiled=True)  55.7 us
    ppermute x6, starting transfers between devices, both_ways(): return (lax.ppermute(high, axis, up), lax.ppermute(low, axis, down))  36.2 us
    pallas_call x1, Pallas kernels, on_device(): vmem_call(factor_kernel, [f32(held, rank + count), f32(rank + count, rank...  31.2 us
    ppermute x6, waiting for transfers between devices, both_ways(): return (lax.ppermute(high, axis, up), lax.ppermute(low, axis, down))  16.4 us
    all_to_all x1, waiting for transfers between devices, on_device(): lax.all_to_all(sent, 'slab', 0, 0, tiled=True).reshape(-1, sent.shape[2])  16 us
    pallas_call x1, Pallas kernels, sections(): vmem_call(sections_kernel, [f32(*velocity.shape), f32(pieces, depth, 2 *...  10.7 us
    all_to_all x1, starting transfers between devices, on_device(): lax.all_to_all(sent, 'slab', 0, 0, tiled=True).reshape(-1, sent.shape[2])  9.38 us
  transfers between devices with their start and end apart: 7, of which 5 were waited for; matrix products, arithmetic and copies ran while one was open for 0% of the time, Pallas kernels for 1%

profile of v1, /device:TPU:1, one launch (start us, length us, event | category | flops | bytes accessed | tf_op | source)
XLA Modules:
  0.0 239.8 jit_solution(3606589495389819305)
XLA Ops:
  0.6 1.2 fusion
  1.9 5.9 %collective-permute-start = (f32[3,32,4,128]{3,2,1,0:T(4,128)S(1)}, f32[3,32,4,128]{3,2,1,0:T(4,128)S(1)}, u32[]{:S(2)}, u32[]{:S(2)}) collective-permute-start(f32[3,32,4,128]{3,2,1,0:T(4,128)S(1)} %get-tuple-element.24), channel_id=1, source_target_pairs={{96,0},{192,96},{288,192},{384,288},{480,384},{576,480},{672,576},... | collective-permute-start | bytes 589832 | tf_op jit(solution)/shard_map/ppermute | solution.py:53
  7.8 1.9 collective-permute-start.1
  9.7 0.7 collective-permute-done
  10.4 5.0 %collective-permute-done.1 = f32[3,32,4,128]{3,2,1,0:T(4,128)S(1)} collective-permute-done((f32[3,32,4,128]{3,2,1,0:T(4,128)S(1)}, f32[3,32,4,128]{3,2,1,0:T(4,128)S(1)}, u32[]{:S(2)}, u32[]{:S(2)}) %collective-permute-start.1) | collective-permute-done | bytes 196640 | tf_op jit(solution)/shard_map/ppermute | solution.py:53
  15.4 0.9 pad_maximum_fusion.3
  16.3 6.7 %collective-permute-start.2 = (f32[3,4,16,128]{3,2,1,0:T(8,128)S(1)}, f32[3,4,16,128]{3,2,1,0:T(8,128)S(1)}, u32[]{:S(2)}, u32[]{:S(2)}) collective-permute-start(f32[3,4,16,128]{3,2,1,0:T(8,128)S(1)} %get-tuple-element.22), channel_id=1, source_target_pairs={{0,8},{8,16},{16,24},{24,32},{32,40},{40,48},{48,56},{56,64},{64,7... | collective-permute-start | bytes 294920 | tf_op jit(solution)/shard_map/ppermute | solution.py:53
  23.0 4.8 %collective-permute-start.3 = (f32[3,4,16,128]{3,2,1,0:T(8,128)S(1)}, f32[3,4,16,128]{3,2,1,0:T(8,128)S(1)}, u32[]{:S(2)}, u32[]{:S(2)}) collective-permute-start(f32[3,4,16,128]{3,2,1,0:T(8,128)S(1)} %get-tuple-element.23), channel_id=1, source_target_pairs={{8,0},{16,8},{24,16},{32,24},{40,32},{48,40},{56,48},{64,56},{72,6... | collective-permute-start | bytes 294920 | tf_op jit(solution)/shard_map/ppermute | solution.py:53
  27.8 1.1 collective-permute-done.3
  29.0 0.6 shard_map.67
  29.6 15.6 %collective-permute-start.4 = (f32[4,16,128]{2,1,0:T(8,128)S(1)}, f32[4,16,128]{2,1,0:T(8,128)S(1)}, u32[]{:S(2)}, u32[]{:S(2)}) collective-permute-start(f32[4,16,128]{2,1,0:T(8,128)S(1)} %get-tuple-element.11), channel_id=1, source_target_pairs={{0,1},{1,2},{2,3},{3,4},{4,5},{5,6},{6,7},{8,9},{9,10},{10,11},{11... | collective-permute-start | bytes 98312 | tf_op jit(solution)/shard_map/ppermute | solution.py:53
  45.2 1.3 collective-permute-start.5
  46.6 9.6 %collective-permute-done.5.after_ref = f32[4,16,128]{2,1,0:T(8,128)S(1)} collective-permute-done((f32[4,16,128]{2,1,0:T(8,128)S(1)}, f32[4,16,128]{2,1,0:T(8,128)S(1)}, u32[]{:S(2)}, u32[]{:S(2)}) %collective-permute-start.5) | collective-permute-done | bytes 32800 | tf_op jit(solution)/shard_map/ppermute | solution.py:53
  56.2 10.7 %shard_map.68 = (f32[3,32,8,128]{3,2,1,0:T(8,128)}, f32[12,32,256]{2,1,0:T(8,128)}) custom-call(s32[12]{0:T(128)S(1)} %copy-done.1, s32[2]{0:T(128)S(1)} %pad_add_fusion.row_ref, f32[3,40,16,128]{3,2,1,0:T(8,128)S(1)} %pad_maximum_fusion.field_ref, f32[4,16,128]{2,1,0:T(8,128)S(1)} %collective-permute-done.4.before_ref, ...), custom_call_target="tpu_custom_call" | custom-call | bytes 786432 | tf_op jit(solution)/shard_map/pallas_call | solution.py:340
  66.9 9.4 %all-to-all-start = ((f32[12,32,256]{2,1,0:T(8,128)}), f32[12,32,256]{2,1,0:T(8,128)S(1)}, u32[]{:S(2)}, u32[]{:S(2)}) async-start(f32[12,32,256]{2,1,0:T(8,128)} %get-tuple-element.14), calls=%async_computation | async-start | bytes 786432 | tf_op jit(solution)/shard_map/all_to_all | solution.py:362
  76.3 1.3 shard_map.69.packed_in
  77.6 16.0 %all-to-all-done = f32[12,32,256]{2,1,0:T(8,128)S(1)} async-done(((f32[12,32,256]{2,1,0:T(8,128)}), f32[12,32,256]{2,1,0:T(8,128)S(1)}, u32[]{:S(2)}, u32[]{:S(2)}) %all-to-all-start) | async-done | bytes 393248 | tf_op jit(solution)/shard_map/all_to_all | solution.py:362
  93.6 1.4 shard_map.70
  95.0 55.7 %all_to_all.15 = f32[768,2,128]{2,1,0:T(2,128)S(1)} all-to-all(f32[768,2,128]{2,1,0:T(2,128)S(1)} %bitcast.4), channel_id=1, replica_groups=mesh['grp'=8,'slab'=12,'row'=8] {'grp','slab','row'}, dimensions={0} | all-to-all | bytes 1572864 | tf_op jit(solution)/shard_map/all_to_all | solution.py:368
  150.7 0.8 reduce_sum.9
  151.5 0.2 broadcast_in_dim.2
  151.7 55.8 %all_to_all.16 = f32[768,2,128]{2,1,0:T(2,128)S(1)} all-to-all(f32[768,2,128]{2,1,0:T(2,128)S(1)} %broadcast_in_dim.2), channel_id=1, replica_groups=mesh['grp'=8,'slab'=12,'row'=8] {'grp','slab','row'}, dimensions={0} | all-to-all | bytes 1572864 | tf_op jit(solution)/shard_map/all_to_all | solution.py:370
  207.5 31.2 %shard_map.71 = (f32[256,576]{1,0:T(8,128)S(1)}, f32[576,576]{1,0:T(8,128)}) custom-call(f32[1536,128]{1,0:T(8,128)S(1)} %bitcast.5, f32[256,512]{1,0:T(8,128)S(1)} %copy-done, f32[64,256]{1,0:T(8,128)S(1)} %get-tuple-element.16.snap_ref), custom_call_target="tpu_custom_call" | custom-call | tf_op jit(solution)/shard_map/pallas_call | solution.py:373
  238.7 1.0 copy.8
  (13 shorter events, 0.2 us)
Async XLA Ops:
  0.6 28.3 %copy-start.3 = (f32[3,32,8,128]{3,2,1,0:T(8,128)S(1)}, f32[3,32,8,128]{3,2,1,0:T(8,128)}, u32[]{:S(2)}) copy-start(f32[3,32,8,128]{3,2,1,0:T(8,128)} %param.4) | copy-start | bytes 1179652
  1.9 8.5 %collective-permute-start = (f32[3,32,4,128]{3,2,1,0:T(4,128)S(1)}, f32[3,32,4,128]{3,2,1,0:T(4,128)S(1)}, u32[]{:S(2)}, u32[]{:S(2)}) collective-permute-start(f32[3,32,4,128]{3,2,1,0:T(4,128)S(1)} %get-tuple-element.24), channel_id=1, source_target_pairs={{96,0},{192,96},{288,192},{384,288},{480,384},{576,480},{672,576},... | collective-permute-start | bytes 589832 | tf_op jit(solution)/shard_map/ppermute | solution.py:53
  7.8 7.6 %collective-permute-start.1 = (f32[3,32,4,128]{3,2,1,0:T(4,128)S(1)}, f32[3,32,4,128]{3,2,1,0:T(4,128)S(1)}, u32[]{:S(2)}, u32[]{:S(2)}) collective-permute-start(f32[3,32,4,128]{3,2,1,0:T(4,128)S(1)} %get-tuple-element.25), channel_id=1, source_target_pairs={{0,96},{96,192},{192,288},{288,384},{384,480},{480,576},{576,672},... | collective-permute-start | bytes 589832 | tf_op jit(solution)/shard_map/ppermute | solution.py:53
  16.3 11.5 %collective-permute-start.2 = (f32[3,4,16,128]{3,2,1,0:T(8,128)S(1)}, f32[3,4,16,128]{3,2,1,0:T(8,128)S(1)}, u32[]{:S(2)}, u32[]{:S(2)}) collective-permute-start(f32[3,4,16,128]{3,2,1,0:T(8,128)S(1)} %get-tuple-element.22), channel_id=1, source_target_pairs={{0,8},{8,16},{16,24},{24,32},{32,40},{40,48},{48,56},{56,64},{64,7... | collective-permute-start | bytes 294920 | tf_op jit(solution)/shard_map/ppermute | solution.py:53
  23.0 5.9 %collective-permute-start.3 = (f32[3,4,16,128]{3,2,1,0:T(8,128)S(1)}, f32[3,4,16,128]{3,2,1,0:T(8,128)S(1)}, u32[]{:S(2)}, u32[]{:S(2)}) collective-permute-start(f32[3,4,16,128]{3,2,1,0:T(8,128)S(1)} %get-tuple-element.23), channel_id=1, source_target_pairs={{8,0},{16,8},{24,16},{32,24},{40,32},{48,40},{56,48},{64,56},{72,6... | collective-permute-start | bytes 294920 | tf_op jit(solution)/shard_map/ppermute | solution.py:53
  27.8 28.4 %copy-start.1 = (s32[12]{0:T(128)S(1)}, s32[12]{0:T(128)}, u32[]{:S(2)}) copy-start(s32[12]{0:T(128)} %assign_ref.1) | copy-start | bytes 148
  29.0 47.2 %copy-start = (f32[256,512]{1,0:T(8,128)S(1)}, f32[256,512]{1,0:T(8,128)}, u32[]{:S(2)}) copy-start(f32[256,512]{1,0:T(8,128)} %modes_ref.5) | copy-start | bytes 1572868
  29.6 17.0 %collective-permute-start.4 = (f32[4,16,128]{2,1,0:T(8,128)S(1)}, f32[4,16,128]{2,1,0:T(8,128)S(1)}, u32[]{:S(2)}, u32[]{:S(2)}) collective-permute-start(f32[4,16,128]{2,1,0:T(8,128)S(1)} %get-tuple-element.11), channel_id=1, source_target_pairs={{0,1},{1,2},{2,3},{3,4},{4,5},{5,6},{6,7},{8,9},{9,10},{10,11},{11... | collective-permute-start | bytes 98312 | tf_op jit(solution)/shard_map/ppermute | solution.py:53
  45.2 11.0 %collective-permute-start.5 = (f32[4,16,128]{2,1,0:T(8,128)S(1)}, f32[4,16,128]{2,1,0:T(8,128)S(1)}, u32[]{:S(2)}, u32[]{:S(2)}) collective-permute-start(f32[4,16,128]{2,1,0:T(8,128)S(1)} %get-tuple-element.12), channel_id=1, source_target_pairs={{1,0},{2,1},{3,2},{4,3},{5,4},{6,5},{7,6},{9,8},{10,9},{11,10},{12... | collective-permute-start | bytes 98312 | tf_op jit(solution)/shard_map/ppermute | solution.py:53
  66.9 26.7 %all-to-all-start = ((f32[12,32,256]{2,1,0:T(8,128)}), f32[12,32,256]{2,1,0:T(8,128)S(1)}, u32[]{:S(2)}, u32[]{:S(2)}) async-start(f32[12,32,256]{2,1,0:T(8,128)} %get-tuple-element.14), calls=%async_computation | async-start | bytes 786432 | tf_op jit(solution)/shard_map/all_to_all | solution.py:362
  76.3 17.3 %copy-start.2 = (s32[64]{0:T(128)S(1)}, s32[64]{0:T(128)}, u32[]{:S(2)}) copy-start(s32[64]{0:T(128)} %planes_ref.1) | copy-start | bytes 772

commit v2 on v1

--- a/solution.py
+++ b/solution.py
@@ -162,19 +162,19 @@
             )
 
 
-def snapshot_gram_kernel(planes_ref, received_ref, modes_ref, packed_in, packed_ref, snap_ref):
+def snapshot_gram_kernel(planes_ref, received_ref, modes_ref, packed_ref, snap_ref):
     count = snap_ref.shape[0]
     blocks = modes_ref.shape[1] // BLOCK
-    base = pair_index(blocks - 1, blocks - 1) * BLOCK + BLOCK
-    packed_ref[0:base, :] = packed_in[0:base, :]
     for k in range(count):
         snap_ref[k : k + 1, :] = received_ref[pl.ds(planes_ref[k], 1), :]
     snap = snap_ref[...]
     cross = product(modes_ref[...], snap, ((0,), (1,)))
     for b in range(blocks):
-        at, side = base + (b // 2) * BLOCK, (b % 2) * count
+        at, side = (b // 2) * BLOCK, (b % 2) * count
         packed_ref[at : at + BLOCK, side : side + count] = cross[b * BLOCK : (b + 1) * BLOCK, :]
-    packed_ref[BLOCK - count : BLOCK, 0:count] = product(snap, snap, ((1,), (1,)))
+    base = blocks // 2 * BLOCK
+    packed_ref[base : base + count, :] = jnp.zeros((count, BLOCK), jnp.float32)
+    packed_ref[base : base + count, 0:count] = product(snap, snap, ((1,), (1,)))
 
 
 def lanes_of(value, j):
@@ -241,148 +241,211 @@
             side[i] = side[i] - total([here[j] * left_rows[j] for j in range(8)])
 
 
-def factor_kernel(packed_ref, modes_ref, snap_ref, basis_ref, factor_ref, block_ref, upper_ref, inverse_ref, work_ref, done_ref):
-    count = snap_ref.shape[0]
-    blocks = modes_ref.shape[1] // BLOCK
-    half = BLOCK // 16
-    base = pair_index(blocks - 1, blocks - 1) * BLOCK + BLOCK
-    wide = blocks + 1
+def identity(size):
+    lane = lax.broadcasted_iota(jnp.int32, (size, size), 1)
+    sub = lax.broadcasted_iota(jnp.int32, (size, size), 0)
+    return jnp.where(lane == sub, 1.0, 0.0)
+
+
+def pair_rows(i, j):
+    at = pair_index(i, j) * BLOCK
+    return slice(at, at + BLOCK)
+
+
+def factor_step(b, blocks, gram_ref, side_in, block_ref, side_ref, upper_ref, inverse_ref):
+    rows = BLOCK // 8
     lane = lax.broadcasted_iota(jnp.int32, (BLOCK, BLOCK), 1)
     sub = lax.broadcasted_iota(jnp.int32, (BLOCK, BLOCK), 0)
-    unit = jnp.where(lane == sub, 1.0, 0.0)
-
+    value = gram_ref[pair_rows(b, b), :]
+    value = jnp.where(lane >= sub, value, value.T)
+    unit = identity(BLOCK)
+    main = [value[8 * i : 8 * i + 8, :] for i in range(rows)]
+    side = [unit[8 * i : 8 * i + 8, :] for i in range(rows)]
+    eliminate(main, side, upper_ref, inverse_ref, 0, rows, rows)
+    inverse = inverse_ref[...]
+    for i in range(b):
+        for j in range(i, blocks):
+            block_ref[pair_rows(i, j), :] = gram_ref[pair_rows(i, j), :]
+            if j < b:
+                side_ref[pair_rows(i, j), :] = side_in[pair_rows(i, j), :]
+    block_ref[pair_rows(b, b), :] = upper_ref[...]
+    side_ref[pair_rows(b, b), :] = inverse
+    for j in range(b):
+        side_ref[pair_rows(j, b), :] = product(inverse, side_in[pair_rows(j, b), :], ((1,), (0,)))
+    for j in range(b + 1, blocks):
+        block_ref[pair_rows(b, j), :] = product(inverse, gram_ref[pair_rows(b, j), :], ((1,), (0,)))
+    for i in range(b + 1, blocks):
+        factor = block_ref[pair_rows(b, i), :]
+        for j in range(i, blocks):
+            taken = product(factor, block_ref[pair_rows(b, j), :], ((0,), (0,)))
+            block_ref[pair_rows(i, j), :] = gram_ref[pair_rows(i, j), :] - taken
+        for j in range(b):
+            taken = product(factor, side_ref[pair_rows(j, b), :], ((0,), (0,)))
+            side_ref[pair_rows(j, i), :] = side_in[pair_rows(j, i), :] - taken
+        side_ref[pair_rows(b, i), :] = -product(factor, inverse, ((0,), (0,)))
+
+
+def first_factor_kernel(gram_ref, block_ref, side_ref, upper_ref, inverse_ref):
+    factor_step(0, 4, gram_ref, None, block_ref, side_ref, upper_ref, inverse_ref)
+
+
+def next_factor_kernel(b):
+    def next_factor(gram_ref, side_in, block_ref, side_ref, upper_ref, inverse_ref):
+        factor_step(b, 4, gram_ref, side_in, block_ref, side_ref, upper_ref, inverse_ref)
+
+    return next_factor
+
+
+def last_factor_kernel(gram_ref, side_in, modes_ref, upper_out, inverse_out, done_ref, block_ref, side_ref, upper_ref, inverse_ref):
+    blocks = modes_ref.shape[1] // BLOCK
+    factor_step(blocks - 1, blocks, gram_ref, side_in, block_ref, side_ref, upper_ref, inverse_ref)
+    zero = jnp.zeros((BLOCK, BLOCK), jnp.float32)
     for i in range(blocks):
-        for j in range(i, blocks):
-            at = pair_index(i, j) * BLOCK
-            value = packed_ref[at : at + BLOCK, :]
-            if i == j:
-                value = jnp.where(lane >= sub, value, value.T)
-            block_ref[i * wide + j] = value
-        at = base + (i // 2) * BLOCK
-        pair = packed_ref[at : at + BLOCK, :]
-        if i % 2:
-            pair = pltpu.roll(pair, count, 1)
-        block_ref[i * wide + blocks] = jnp.where(lane < count, pair, 0.0)
-        work_ref[i] = modes_ref[:, i * BLOCK : (i + 1) * BLOCK]
-    block_ref[blocks * wide + blocks] = unit
-    block_ref[blocks * wide + blocks, 0:count, 0:count] = packed_ref[BLOCK - count : BLOCK, 0:count]
-    work_ref[blocks] = jnp.zeros(work_ref.shape[1:], jnp.float32)
-    work_ref[blocks, :, 0:count] = snap_ref[...].T
-
-    def one_block(b, _):
-        mine = b * wide + b
-        rows = BLOCK // 8
-        inverse_ref[...] = unit
-        upper_ref[...] = unit
-        main = [block_ref[mine, 8 * i : 8 * i + 8, :] for i in range(rows)]
-        side = [inverse_ref[8 * i : 8 * i + 8, :] for i in range(rows)]
-        eliminate(main, side, upper_ref, inverse_ref, 0, half, rows)
-
-        @pl.when(b < blocks)
-        def _():
-            eliminate(main, side, upper_ref, inverse_ref, half, rows, rows)
-
-        block_ref[mine] = upper_ref[...]
-        inverse = inverse_ref[...]
-        done = product(work_ref[b], inverse, ((1,), (1,)))
-        done_ref[b] = done
-
-        def along(j, _):
-            block_ref[b * wide + j] = product(inverse, block_ref[b * wide + j], ((1,), (0,)))
-            return 0
-
-        lax.fori_loop(b + 1, wide, along, 0)
-
-        def across(j, _):
-            line = block_ref[b * wide + j]
-            work_ref[j] = work_ref[j] - product(done, line, ((1,), (0,)))
-
-            def down(i, _):
-                block_ref[i * wide + j] = block_ref[i * wide + j] - product(block_ref[b * wide + i], line, ((0,), (0,)))
-                return 0
-
-            lax.fori_loop(b + 1, j + 1, down, 0)
-            return 0
-
-        lax.fori_loop(b + 1, wide, across, 0)
-        return 0
-
-    lax.fori_loop(0, wide, one_block, 0)
-
+        for j in range(blocks):
+            here = (slice(i * BLOCK, (i + 1) * BLOCK), slice(j * BLOCK, (j + 1) * BLOCK))
+            upper_out[here] = block_ref[pair_rows(i, j), :] if i <= j else zero
+            inverse_out[here] = side_ref[pair_rows(j, i), :] if j <= i else zero
     for i in range(blocks):
-        basis_ref[:, i * BLOCK : (i + 1) * BLOCK] = done_ref[i]
-        for j in range(blocks):
-            value = block_ref[i * wide + j] if j >= i else jnp.zeros((BLOCK, BLOCK), jnp.float32)
-            factor_ref[i * BLOCK : (i + 1) * BLOCK, j * BLOCK : (j + 1) * BLOCK] = value
-        factor_ref[i * BLOCK : (i + 1) * BLOCK, blocks * BLOCK :] = block_ref[i * wide + blocks, :, 0:count]
-        factor_ref[blocks * BLOCK :, i * BLOCK : (i + 1) * BLOCK] = jnp.zeros((count, BLOCK), jnp.float32)
-    basis_ref[:, blocks * BLOCK :] = done_ref[blocks, :, 0:count]
-    factor_ref[blocks * BLOCK :, blocks * BLOCK :] = block_ref[blocks * wide + blocks, 0:count, 0:count]
+        size = (i + 1) * BLOCK
+        done_ref[i * BLOCK : size, :] = product(inverse_out[i * BLOCK : size, 0:size], modes_ref[:, 0:size], ((1,), (1,)))
+
+
+def finish_kernel(packed_ref, snap_ref, upper_ref, inverse_ref, done_ref, basis_ref, factor_ref, cross_ref, corner_ref, back_ref):
+    count = snap_ref.shape[0]
+    rank = upper_ref.shape[0]
+    blocks = rank // BLOCK
+    base = blocks // 2 * BLOCK
+    for i in range(blocks):
+        at, side = (i // 2) * BLOCK, (i % 2) * count
+        cross_ref[i * BLOCK : (i + 1) * BLOCK, :] = packed_ref[at : at + BLOCK, side : side + count]
+    cross = product(inverse_ref[...], cross_ref[...], ((1,), (0,)))
+    rows = count // 8
+    corner_ref[...] = jnp.zeros_like(corner_ref)
+    corner_ref[:, 0:count] = packed_ref[base : base + count, 0:count] - product(cross, cross, ((0,), (0,)))
+    unit = identity(BLOCK)
+    main = [corner_ref[8 * i : 8 * i + 8, :] for i in range(rows)]
+    side = [unit[8 * i : 8 * i + 8, :] for i in range(rows)]
+    eliminate(main, side, corner_ref, back_ref, 0, rows, rows)
+    rest = snap_ref[...] - product(cross, done_ref[...], ((0,), (0,)))
+    basis_ref[0:rank, :] = done_ref[...]
+    basis_ref[rank:, :] = product(back_ref[:, 0:count], rest, ((1,), (0,)))
+    factor_ref[0:rank, 0:rank] = upper_ref[...]
+    factor_ref[0:rank, rank:] = cross
+    factor_ref[rank:, 0:rank] = jnp.zeros((count, rank), jnp.float32)
+    factor_ref[rank:, rank:] = corner_ref[:, 0:count]
 
 
 def f32(*shape):
     return jax.ShapeDtypeStruct(shape, jnp.float32)
 
 
-def sections(velocity, assign):
-    comps, depth, across, height = velocity.shape
-    before, after = both_ways(velocity[:, :, :WIDE], velocity[:, :, across - WIDE :], "grp", True)
+def together(*values):
+    return lax.optimization_barrier(values)
+
+
+def halo_field(velocity, first, last, packed):
+    depth = velocity.shape[1]
+    before, after = both_ways(first, last, "grp", True)
+    share = scattered_sum(packed, "grp")
+    before, after, share = together(before, after, share)
     field = jnp.concatenate([velocity, after, before], axis=2)
     before, after = both_ways(field[:, :WIDE], field[:, depth - WIDE :], "slab", True)
+    share = scattered_sum(share, "row")
+    before, after, share = together(before, after, share)
     field = jnp.concatenate([before, field, after], axis=1)
     shape = field.shape
-    tiles = -(-shape[0] * shape[1] * WIDE // height)
-    packed = f32(tiles, shape[2], height)
-    first, last = vmem_call(pack_kernel, [packed, packed], [VM], moved=4 * field.size)(field)
+    tiles = -(-shape[0] * shape[1] * WIDE // shape[3])
+    edge = f32(tiles, shape[2], shape[3])
+    first, last = vmem_call(pack_kernel, [edge, edge], [VM], moved=4 * field.size)(field)
     before, after = both_ways(first, last, "row", False)
+    share = jnp.sum(everyones(share, "slab"), axis=0)
+    return (field,) + tuple(together(before, after, share))
+
+
+def sections(field, before, after, assign, depth, across):
+    comps, height = field.shape[0], field.shape[3]
     where = jnp.stack([lax.axis_index("row"), lax.axis_size("row")]).astype(jnp.int32)
     pieces = comps * across // 2
+    wide = (comps, field.shape[1], field.shape[2], 2 * height)
     return vmem_call(
         sections_kernel,
-        [f32(*velocity.shape), f32(pieces, depth, 2 * height)],
+        [f32(comps, depth, across, height), f32(pieces, depth, 2 * height)],
         [SM, SM, VM, VM, VM],
         scratch=[
-            pltpu.VMEM((comps, shape[1], shape[2], 2 * height), jnp.float32),
-            pltpu.VMEM((comps, shape[1], shape[2], 2 * height), jnp.float32),
-            pltpu.VMEM((comps, shape[1], across, height), jnp.float32),
+            pltpu.VMEM(wide, jnp.float32),
+            pltpu.VMEM(wide, jnp.float32),
+            pltpu.VMEM((comps, field.shape[1], across, height), jnp.float32),
             pltpu.SMEM((pieces,), jnp.int32),
         ],
-        moved=8 * velocity.size,
+        moved=32 * field.size,
     )(assign, where, field, before, after)
+
+
+def scattered_sum(value, axis):
+    shares = value.reshape(lax.axis_size(axis), -1, value.shape[1])
+    return jnp.sum(lax.all_to_all(shares, axis, 0, 0, tiled=True), axis=0)
+
+
+def everyones(value, axis):
+    copies = jnp.broadcast_to(value[None], (lax.axis_size(axis),) + value.shape)
+    return lax.all_to_all(copies, axis, 0, 0, tiled=True)
 
 
 def on_device(velocity, modes, planes, assign):
     count, rank, held = planes.shape[0], modes.shape[1], modes.shape[0]
     devices = lax.axis_size("grp") * lax.axis_size("slab") * lax.axis_size("row")
+    scale = 1.0 / float(held * devices)
     blocks = rank // BLOCK
-    rows = (blocks * (blocks + 1) // 2 + blocks // 2) * BLOCK
+    rows = blocks * (blocks + 1) // 2 * BLOCK
+    tall = blocks // 2 * BLOCK + count
+    block = [pltpu.VMEM((BLOCK, BLOCK), jnp.float32)] * 2
+    state = [f32(rows, BLOCK), f32(rows, BLOCK)]
+    cost = 7 * 1000 * 1000 * 1000
+
+    across = velocity.shape[2]
+    first, last = velocity[:, :, :WIDE], velocity[:, :, across - WIDE :]
     packed = vmem_call(modes_gram_kernel, f32(rows, BLOCK), [VM], flops=12 * held * rank * rank, moved=4 * modes.size)(modes)
-
-    advanced, sent = sections(velocity, assign)
+    field, before, after, share = halo_field(velocity, first, last, packed)
+    share = everyones(share * scale, "row").reshape(-1, BLOCK)
+    advanced, sent = sections(field, before, after, assign, velocity.shape[1], velocity.shape[2])
+    sent, share = together(sent, share)
     received = lax.all_to_all(sent, "slab", 0, 0, tiled=True).reshape(-1, sent.shape[2])
-    packed, snap = vmem_call(
-        snapshot_gram_kernel, [f32(rows, BLOCK), f32(count, held)], [SM, VM, VM, VM], aliases={3: 0}
-    )(planes, received, modes, packed)
-
-    shares = packed.reshape(devices, rows // devices, BLOCK)
-    shares = lax.all_to_all(shares, ALL, 0, 0, tiled=True)
-    share = jnp.sum(shares, axis=0, keepdims=True) * (1.0 / float(held * devices))
-    gram = lax.all_to_all(jnp.broadcast_to(share, shares.shape), ALL, 0, 0, tiled=True)
-
-    wide = blocks + 1
+    packed, snap = vmem_call(snapshot_gram_kernel, [f32(tall, BLOCK), f32(count, held)], [SM, VM, VM])(planes, received, modes)
+
+    groups = lax.axis_size("grp")
+    part = tall // groups
+    copies = jnp.broadcast_to(share[None], (groups,) + share.shape)
+    both = jnp.concatenate([packed.reshape(groups, part, BLOCK), copies], axis=1)
+    both = lax.all_to_all(both, "grp", 0, 0, tiled=True)
+    share = jnp.sum(both[:, :part], axis=0)
+    gram = both[:, part:].reshape(rows, BLOCK)
+
+    lower = vmem_call(first_factor_kernel, state, [VM], scratch=block, flops=cost)(gram)
+    lower = vmem_call(next_factor_kernel(1), state, [VM, VM], scratch=block, flops=cost)(*lower)
+    share = jnp.sum(everyones(share, "row"), axis=0)
+    share, *lower = together(share, *lower)
+    lower = vmem_call(next_factor_kernel(2), state, [VM, VM], scratch=block, flops=cost)(*lower)
+    share = jnp.sum(everyones(share, "slab"), axis=0) * scale
+    share, *lower = together(share, *lower)
+    packed = everyones(share, "grp").reshape(tall, BLOCK)
+    upper, inverse, done = vmem_call(
+        last_factor_kernel,
+        [f32(rank, rank), f32(rank, rank), f32(rank, held)],
+        [VM, VM, VM],
+        scratch=[pltpu.VMEM((rows, BLOCK), jnp.float32)] * 2 + block,
+        flops=cost,
+    )(*lower, modes)
     basis, factor = vmem_call(
-        factor_kernel,
-        [f32(held, rank + count), f32(rank + count, rank + count)],
-        [VM, VM, VM],
+        finish_kernel,
+        [f32(rank + count, held), f32(rank + count, rank + count)],
+        [VM, VM, VM, VM, VM],
         scratch=[
-            pltpu.VMEM((wide * wide, BLOCK, BLOCK), jnp.float32),
-            pltpu.VMEM((BLOCK, BLOCK), jnp.float32),
-            pltpu.VMEM((BLOCK, BLOCK), jnp.float32),
-            pltpu.VMEM((wide, held, BLOCK), jnp.float32),
-            pltpu.VMEM((wide, held, BLOCK), jnp.float32),
+            pltpu.VMEM((rank, count), jnp.float32),
+            pltpu.VMEM((count, BLOCK), jnp.float32),
+            pltpu.VMEM((count, BLOCK), jnp.float32),
         ],
-    )(gram.reshape(rows, BLOCK), modes, snap)
-    return (advanced, basis, factor)
+    )(packed, snap, upper, inverse, done)
+    return (advanced, basis.T, factor)
 
 
 def solution(mesh):

time: 240 us -> 234 us (0.975)
  blocking collectives: 111 us -> 57.1 us
  starting transfers between devices: 45.6 us -> 86.3 us
  local copies, waits for them, and re-layouts: 2.5 us -> 9.11 us
    all_to_all x2, blocking collectives: 111 us -> 57.1 us  [the longest x1 28.9 us: on_device(): both = lax.all_to_all(both, 'grp', 0, 0, tiled=True)]
    all_to_all x1 -> x7, starting transfers between devices: 9.38 us -> 62 us  [the longest x5 35.2 us: everyones(): return lax.all_to_all(copies, axis, 0, 0, tiled=True)]
    ppermute x6, starting transfers between devices: 36.2 us -> 24.4 us  [both_ways(): return (lax.ppermute(high, axis, up), lax.ppermute(low, axis, down))]
    unnamed x9 -> x18, local copies, waits for them, and re-layouts: 1.06 us -> 4.92 us
    broadcast_in_dim x1 -> x6, local copies, waits for them, and re-layouts: 0.21 us -> 3.43 us  [the longest x5 3.39 us: everyones(): copies = jnp.broadcast_to(value[None], (lax.axis_size(axis),) + value.shape)]
    all_to_all x1 -> x7, waiting for transfers between devices: 16 us -> 18.7 us  [the longest x2 12 us: scattered_sum(): return jnp.sum(lax.all_to_all(shares, axis, 0, 0, tiled=True), axis=0)]
    pallas_call x4 -> x8, Pallas kernels: 43.9 us -> 43.4 us  [the longest x1 10.5 us: sections(): vmem_call(sections_kernel, [f32(comps, depth, across, height), f32(pieces...]
  transfers between devices with their start and end apart: 7 -> 13, of which waited for: 5 -> 7; matrix products, arithmetic and copies ran while one was open for 0% -> 0% of each run, Pallas kernels for 1% -> 16%
where the time goes in v2:
time: 234 us; the launch traced here: 233 us
  starting transfers between devices  86.3 us (37%)
  blocking collectives  57.1 us (24%)
  Pallas kernels  45.5 us (19%)
  waiting for transfers between devices  33.6 us (14%)
  local copies, waits for them, and re-layouts  9.11 us (4%)
    all_to_all x5, starting transfers between devices, everyones(): return lax.all_to_all(copies, axis, 0, 0, tiled=True)  35.2 us
    all_to_all x1, blocking collectives, on_device(): both = lax.all_to_all(both, 'grp', 0, 0, tiled=True)  28.9 us
    all_to_all x1, blocking collectives, on_device(): lax.all_to_all(sent, 'slab', 0, 0, tiled=True).reshape(-1, sent.shape[2])  28.1 us
    all_to_all x2, starting transfers between devices, scattered_sum(): return jnp.sum(lax.all_to_all(shares, axis, 0, 0, tiled=True), axis=0)  26.8 us
    ppermute x6, starting transfers between devices, both_ways(): return (lax.ppermute(high, axis, up), lax.ppermute(low, axis, down))  24.4 us
    ppermute x6, waiting for transfers between devices, both_ways(): return (lax.ppermute(high, axis, up), lax.ppermute(low, axis, down))  15 us
    all_to_all x2, waiting for transfers between devices, scattered_sum(): return jnp.sum(lax.all_to_all(shares, axis, 0, 0, tiled=True), axis=0)  12 us
    pallas_call x1, Pallas kernels, sections(): vmem_call(sections_kernel, [f32(comps, depth, across, height), f32(pieces...  10.5 us
  transfers between devices with their start and end apart: 13, of which 7 were waited for; matrix products, arithmetic and copies ran while one was open for 0% of the time, Pallas kernels for 16%

profile of v2, /device:TPU:1, one launch (start us, length us, event | category | flops | bytes accessed | tf_op | source)
XLA Modules:
  0.0 233.0 jit_solution(9545821882222529187)
XLA Ops:
  3.8 7.7 %all-to-all-start = ((f32[8,160,128]{2,1,0:T(8,128)}), f32[8,160,128]{2,1,0:T(8,128)S(1)}, u32[]{:S(2)}, u32[]{:S(2)}) async-start(f32[8,160,128]{2,1,0:T(8,128)} %bitcast.1), calls=%async_computation | async-start | bytes 1310720 | tf_op jit(solution)/shard_map/all_to_all | solution.py:386
  11.6 4.6 %collective-permute-start.1 = (f32[3,32,4,128]{3,2,1,0:T(4,128)S(1)}, f32[3,32,4,128]{3,2,1,0:T(4,128)S(1)}, u32[]{:S(2)}, u32[]{:S(2)}) collective-permute-start(f32[3,32,4,128]{3,2,1,0:T(4,128)S(1)} %get-tuple-element.73), channel_id=1, source_target_pairs={{96,0},{192,96},{288,192},{384,288},{480,384},{576,480},{672,576},... | collective-permute-start | bytes 589832 | tf_op jit(solution)/shard_map/ppermute | solution.py:53
  18.1 7.0 %all-to-all-done = f32[8,160,128]{2,1,0:T(8,128)S(1)} async-done(((f32[8,160,128]{2,1,0:T(8,128)}), f32[8,160,128]{2,1,0:T(8,128)S(1)}, u32[]{:S(2)}, u32[]{:S(2)}) %all-to-all-start) | async-done | bytes 655392 | tf_op jit(solution)/shard_map/all_to_all | solution.py:386
  26.8 3.6 %collective-permute-done = f32[3,32,4,128]{3,2,1,0:T(4,128)S(1)} collective-permute-done((f32[3,32,4,128]{3,2,1,0:T(4,128)S(1)}, f32[3,32,4,128]{3,2,1,0:T(4,128)S(1)}, u32[]{:S(2)}, u32[]{:S(2)}) %collective-permute-start) | collective-permute-done | bytes 196640 | tf_op jit(solution)/shard_map/ppermute | solution.py:53
  31.0 19.1 %all-to-all-start.1 = ((f32[8,20,128]{2,1,0:T(8,128)}), f32[8,20,128]{2,1,0:T(8,128)S(1)}, u32[]{:S(2)}, u32[]{:S(2)}) async-start(f32[8,20,128]{2,1,0:T(8,128)} %reshape.34), calls=%async_computation.1 | async-start | bytes 196608 | tf_op jit(solution)/shard_map/all_to_all | solution.py:386
  50.2 3.6 %collective-permute-start.3 = (f32[3,4,16,128]{3,2,1,0:T(8,128)S(1)}, f32[3,4,16,128]{3,2,1,0:T(8,128)S(1)}, u32[]{:S(2)}, u32[]{:S(2)}) collective-permute-start(f32[3,4,16,128]{3,2,1,0:T(8,128)S(1)} %get-tuple-element.71), channel_id=1, source_target_pairs={{8,0},{16,8},{24,16},{32,24},{40,32},{48,40},{56,48},{64,56},{72,6... | collective-permute-start | bytes 294920 | tf_op jit(solution)/shard_map/ppermute | solution.py:53
  53.8 3.0 %collective-permute-start.2 = (f32[3,4,16,128]{3,2,1,0:T(8,128)S(1)}, f32[3,4,16,128]{3,2,1,0:T(8,128)S(1)}, u32[]{:S(2)}, u32[]{:S(2)}) collective-permute-start(f32[3,4,16,128]{3,2,1,0:T(8,128)S(1)} %get-tuple-element.72), channel_id=1, source_target_pairs={{0,8},{8,16},{16,24},{24,32},{32,40},{40,48},{48,56},{56,64},{64,7... | collective-permute-start | bytes 294920 | tf_op jit(solution)/shard_map/ppermute | solution.py:53
  56.8 5.1 %all-to-all-done.1 = f32[8,20,128]{2,1,0:T(8,128)S(1)} async-done(((f32[8,20,128]{2,1,0:T(8,128)}), f32[8,20,128]{2,1,0:T(8,128)S(1)}, u32[]{:S(2)}, u32[]{:S(2)}) %all-to-all-start.1) | async-done | bytes 81952 | tf_op jit(solution)/shard_map/all_to_all | solution.py:386
  62.6 10.0 %all-to-all-start.2 = ((f32[12,20,128]{2,1,0:T(8,128)}), f32[12,20,128]{2,1,0:T(8,128)S(1)}, u32[]{:S(2)}, u32[]{:S(2)}) async-start(f32[12,20,128]{2,1,0:T(8,128)} %broadcast_in_dim.12), calls=%async_computation.2 | async-start | bytes 294912 | tf_op jit(solution)/shard_map/all_to_all | solution.py:391
  73.3 10.0 %collective-permute-start.4 = (f32[4,16,128]{2,1,0:T(8,128)S(1)}, f32[4,16,128]{2,1,0:T(8,128)S(1)}, u32[]{:S(2)}, u32[]{:S(2)}) collective-permute-start(f32[4,16,128]{2,1,0:T(8,128)S(1)} %get-tuple-element.42), channel_id=1, source_target_pairs={{0,1},{1,2},{2,3},{3,4},{4,5},{5,6},{6,7},{8,9},{9,10},{10,11},{11... | collective-permute-start | bytes 98312 | tf_op jit(solution)/shard_map/ppermute | solution.py:53
  84.6 9.6 %collective-permute-done.5.after_ref = f32[4,16,128]{2,1,0:T(8,128)S(1)} collective-permute-done((f32[4,16,128]{2,1,0:T(8,128)S(1)}, f32[4,16,128]{2,1,0:T(8,128)S(1)}, u32[]{:S(2)}, u32[]{:S(2)}) %collective-permute-start.5) | collective-permute-done | bytes 32800 | tf_op jit(solution)/shard_map/ppermute | solution.py:53
  94.9 4.9 %all-to-all-start.3 = ((f32[8,20,128]{2,1,0:T(8,128)}), f32[8,20,128]{2,1,0:T(8,128)S(1)}, u32[]{:S(2)}, u32[]{:S(2)}) async-start(f32[8,20,128]{2,1,0:T(8,128)} %broadcast_in_dim.13), calls=%async_computation.3 | async-start | bytes 196608 | tf_op jit(solution)/shard_map/all_to_all | solution.py:391
  99.8 10.5 %shard_map.69 = (f32[3,32,8,128]{3,2,1,0:T(8,128)}, f32[12,32,256]{2,1,0:T(8,128)S(1)}) custom-call(s32[12]{0:T(128)S(1)} %copy-done.2, s32[2]{0:T(128)S(1)} %pad_add_fusion.row_ref, f32[3,40,16,128]{3,2,1,0:T(8,128)S(1)} %pad_maximum_fusion.field_ref, f32[4,16,128]{2,1,0:T(8,128)S(1)} %collective-permute-done.4.before_ref, ...), custom_call_target="tpu_custom_call" | custom-call | bytes 7864320 | tf_op jit(solution)/shard_map/pallas_call | solution.py:370
  111.5 28.1 %all_to_all.45 = f32[12,32,256]{2,1,0:T(8,128)S(1)} all-to-all(f32[12,32,256]{2,1,0:T(8,128)S(1)} %get-tuple-element.50), channel_id=1, replica_groups=mesh['grp'=8,'slab'=12,'row'=8] {'slab'}, dimensions={0} | all-to-all | bytes 786432 | tf_op jit(solution)/shard_map/all_to_all | solution.py:412
  141.0 28.9 %all_to_all.46 = f32[8,200,128]{2,1,0:T(8,128)S(1)} all-to-all(f32[8,200,128]{2,1,0:T(8,128)S(1)} %pad_maximum_fusion.1), channel_id=1, replica_groups=mesh['grp'=8,'slab'=12,'row'=8] {'grp'}, dimensions={0} | all-to-all | bytes 1638400 | tf_op jit(solution)/shard_map/all_to_all | solution.py:419
  170.7 8.2 %all-to-all-start.6 = ((f32[8,40,128]{2,1,0:T(8,128)}), f32[8,40,128]{2,1,0:T(8,128)S(1)}, u32[]{:S(2)}, u32[]{:S(2)}) async-start(f32[8,40,128]{2,1,0:T(8,128)} %broadcast_in_dim.15), calls=%async_computation.6 | async-start | bytes 327680 | tf_op jit(solution)/shard_map/all_to_all | solution.py:391
  179.0 6.3 %shard_map.71 = (f32[1280,128]{1,0:T(8,128)S(1)}, f32[1280,128]{1,0:T(8,128)S(1)}) custom-call(f32[1280,128]{1,0:T(8,128)S(1)} %bitcast.9), custom_call_target="tpu_custom_call" | custom-call | flops 7000000000 | tf_op jit(solution)/shard_map/pallas_call | solution.py:423
  185.3 6.2 %shard_map.72 = (f32[1280,128]{1,0:T(8,128)S(1)}, f32[1280,128]{1,0:T(8,128)S(1)}) custom-call(f32[1280,128]{1,0:T(8,128)S(1)} %get-tuple-element.53.gram_ref, f32[1280,128]{1,0:T(8,128)S(1)} %get-tuple-element.54.side_in), custom_call_target="tpu_custom_call" | custom-call | flops 7000000000 | tf_op jit(solution)/shard_map/pallas_call | solution.py:424
  192.3 8.7 %all-to-all-start.7 = ((f32[12,40,128]{2,1,0:T(8,128)}), f32[12,40,128]{2,1,0:T(8,128)S(1)}, u32[]{:S(2)}, u32[]{:S(2)}) async-start(f32[12,40,128]{2,1,0:T(8,128)} %broadcast_in_dim.16), calls=%async_computation.7 | async-start | bytes 491520 | tf_op jit(solution)/shard_map/all_to_all | solution.py:391
  201.1 6.1 %shard_map.73 = (f32[1280,128]{1,0:T(8,128)S(1)}, f32[1280,128]{1,0:T(8,128)S(1)}) custom-call(f32[1280,128]{1,0:T(8,128)S(1)} %get-tuple-element.58.gram_ref, f32[1280,128]{1,0:T(8,128)S(1)} %get-tuple-element.59.side_in), custom_call_target="tpu_custom_call" | custom-call | flops 7000000000 | tf_op jit(solution)/shard_map/pallas_call | solution.py:427
  208.8 5.5 %all-to-all-done.7 = f32[12,40,128]{2,1,0:T(8,128)S(1)} async-done(((f32[12,40,128]{2,1,0:T(8,128)}), f32[12,40,128]{2,1,0:T(8,128)S(1)}, u32[]{:S(2)}, u32[]{:S(2)}) %all-to-all-start.7) | async-done | bytes 245792 | tf_op jit(solution)/shard_map/all_to_all | solution.py:391
  215.1 3.4 %all-to-all-start.8 = ((f32[8,40,128]{2,1,0:T(8,128)}), f32[8,40,128]{2,1,0:T(8,128)S(1)}, u32[]{:S(2)}, u32[]{:S(2)}) async-start(f32[8,40,128]{2,1,0:T(8,128)} %broadcast_in_dim.17), calls=%async_computation.8 | async-start | bytes 327680 | tf_op jit(solution)/shard_map/all_to_all | solution.py:391
  220.7 7.0 %shard_map.74 = (f32[512,512]{1,0:T(8,128)S(1)}, f32[512,512]{1,0:T(8,128)S(1)}, f32[512,256]{1,0:T(8,128)S(1)}) custom-call(f32[1280,128]{1,0:T(8,128)S(1)} %copy-done.5, f32[1280,128]{1,0:T(8,128)S(1)} %copy-done.7, f32[256,512]{1,0:T(8,128)S(1)} %copy-done.1), custom_call_target="tpu_custom_call" | custom-call | flops 7000000000 | tf_op jit(solution)/shard_map/pallas_call | solution.py:431
  227.6 5.3 %shard_map.75 = (f32[576,256]{1,0:T(8,128)}, f32[576,576]{1,0:T(8,128)}) custom-call(f32[320,128]{1,0:T(8,128)S(1)} %bitcast.8, f32[64,256]{1,0:T(8,128)S(1)} %get-tuple-element.63.snap_ref, f32[512,512]{1,0:T(8,128)S(1)} %get-tuple-element.66.upper_ref, f32[512,512]{1,0:T(8,128)S(1)} %get-tuple-element.67.inverse_ref, f32[512,256]{1,0:T(8,128)S(1)} %get-tuple-element.68.done_ref), custom_call_target="tpu_custom_call" | custom-call | tf_op jit(solution)/shard_map/pallas_call | solution.py:438
  (53 shorter events, 19.6 us)
Async XLA Ops:
  0.6 1.0 copy-start
  1.7 9.8 %copy-start.8 = (f32[3,32,8,128]{3,2,1,0:T(8,128)S(1)}, f32[3,32,8,128]{3,2,1,0:T(8,128)}, u32[]{:S(2)}) copy-start(f32[3,32,8,128]{3,2,1,0:T(8,128)} %param.4) | copy-start | bytes 1179652
  3.8 21.2 %all-to-all-start = ((f32[8,160,128]{2,1,0:T(8,128)}), f32[8,160,128]{2,1,0:T(8,128)S(1)}, u32[]{:S(2)}, u32[]{:S(2)}) async-start(f32[8,160,128]{2,1,0:T(8,128)} %bitcast.1), calls=%async_computation | async-start | bytes 1310720 | tf_op jit(solution)/shard_map/all_to_all | solution.py:386
  11.6 15.3 %collective-permute-start.1 = (f32[3,32,4,128]{3,2,1,0:T(4,128)S(1)}, f32[3,32,4,128]{3,2,1,0:T(4,128)S(1)}, u32[]{:S(2)}, u32[]{:S(2)}) collective-permute-start(f32[3,32,4,128]{3,2,1,0:T(4,128)S(1)} %get-tuple-element.73), channel_id=1, source_target_pairs={{96,0},{192,96},{288,192},{384,288},{480,384},{576,480},{672,576},... | collective-permute-start | bytes 589832 | tf_op jit(solution)/shard_map/ppermute | solution.py:53
  16.1 14.2 %collective-permute-start = (f32[3,32,4,128]{3,2,1,0:T(4,128)S(1)}, f32[3,32,4,128]{3,2,1,0:T(4,128)S(1)}, u32[]{:S(2)}, u32[]{:S(2)}) collective-permute-start(f32[3,32,4,128]{3,2,1,0:T(4,128)S(1)} %get-tuple-element.74), channel_id=1, source_target_pairs={{0,96},{96,192},{192,288},{288,384},{384,480},{480,576},{576,672},... | collective-permute-start | bytes 589832 | tf_op jit(solution)/shard_map/ppermute | solution.py:53
  31.0 30.9 %all-to-all-start.1 = ((f32[8,20,128]{2,1,0:T(8,128)}), f32[8,20,128]{2,1,0:T(8,128)S(1)}, u32[]{:S(2)}, u32[]{:S(2)}) async-start(f32[8,20,128]{2,1,0:T(8,128)} %reshape.34), calls=%async_computation.1 | async-start | bytes 196608 | tf_op jit(solution)/shard_map/all_to_all | solution.py:386
  50.2 11.7 %collective-permute-start.3 = (f32[3,4,16,128]{3,2,1,0:T(8,128)S(1)}, f32[3,4,16,128]{3,2,1,0:T(8,128)S(1)}, u32[]{:S(2)}, u32[]{:S(2)}) collective-permute-start(f32[3,4,16,128]{3,2,1,0:T(8,128)S(1)} %get-tuple-element.71), channel_id=1, source_target_pairs={{8,0},{16,8},{24,16},{32,24},{40,32},{48,40},{56,48},{64,56},{72,6... | collective-permute-start | bytes 294920 | tf_op jit(solution)/shard_map/ppermute | solution.py:53
  53.8 8.1 %collective-permute-start.2 = (f32[3,4,16,128]{3,2,1,0:T(8,128)S(1)}, f32[3,4,16,128]{3,2,1,0:T(8,128)S(1)}, u32[]{:S(2)}, u32[]{:S(2)}) collective-permute-start(f32[3,4,16,128]{3,2,1,0:T(8,128)S(1)} %get-tuple-element.72), channel_id=1, source_target_pairs={{0,8},{8,16},{16,24},{24,32},{32,40},{40,48},{48,56},{56,64},{64,7... | collective-permute-start | bytes 294920 | tf_op jit(solution)/shard_map/ppermute | solution.py:53
  62.6 21.9 %all-to-all-start.2 = ((f32[12,20,128]{2,1,0:T(8,128)}), f32[12,20,128]{2,1,0:T(8,128)S(1)}, u32[]{:S(2)}, u32[]{:S(2)}) async-start(f32[12,20,128]{2,1,0:T(8,128)} %broadcast_in_dim.12), calls=%async_computation.2 | async-start | bytes 294912 | tf_op jit(solution)/shard_map/all_to_all | solution.py:391
  72.5 27.3 %copy-start.2 = (s32[12]{0:T(128)S(1)}, s32[12]{0:T(128)}, u32[]{:S(2)}) copy-start(s32[12]{0:T(128)} %assign_ref.1) | copy-start | bytes 148
  73.2 66.4 %copy-start.1 = (f32[256,512]{1,0:T(8,128)S(1)}, f32[256,512]{1,0:T(8,128)}, u32[]{:S(2)}) copy-start(f32[256,512]{1,0:T(8,128)} %modes_ref.5) | copy-start | bytes 1572868
  73.3 66.3 %copy-start.3 = (s32[64]{0:T(128)S(1)}, s32[64]{0:T(128)}, u32[]{:S(2)}) copy-start(s32[64]{0:T(128)} %planes_ref.1) | copy-start | bytes 772
  73.3 11.3 %collective-permute-start.4 = (f32[4,16,128]{2,1,0:T(8,128)S(1)}, f32[4,16,128]{2,1,0:T(8,128)S(1)}, u32[]{:S(2)}, u32[]{:S(2)}) collective-permute-start(f32[4,16,128]{2,1,0:T(8,128)S(1)} %get-tuple-element.42), channel_id=1, source_target_pairs={{0,1},{1,2},{2,3},{3,4},{4,5},{5,6},{6,7},{8,9},{9,10},{10,11},{11... | collective-permute-start | bytes 98312 | tf_op jit(solution)/shard_map/ppermute | solution.py:53
  83.2 11.0 %collective-permute-start.5 = (f32[4,16,128]{2,1,0:T(8,128)S(1)}, f32[4,16,128]{2,1,0:T(8,128)S(1)}, u32[]{:S(2)}, u32[]{:S(2)}) collective-permute-start(f32[4,16,128]{2,1,0:T(8,128)S(1)} %get-tuple-element.43), channel_id=1, source_target_pairs={{1,0},{2,1},{3,2},{4,3},{5,4},{6,5},{7,6},{9,8},{10,9},{11,10},{12... | collective-permute-start | bytes 98312 | tf_op jit(solution)/shard_map/ppermute | solution.py:53
  94.9 16.6 %all-to-all-start.3 = ((f32[8,20,128]{2,1,0:T(8,128)}), f32[8,20,128]{2,1,0:T(8,128)S(1)}, u32[]{:S(2)}, u32[]{:S(2)}) async-start(f32[8,20,128]{2,1,0:T(8,128)} %broadcast_in_dim.13), calls=%async_computation.3 | async-start | bytes 196608 | tf_op jit(solution)/shard_map/all_to_all | solution.py:391
  170.7 20.9 %all-to-all-start.6 = ((f32[8,40,128]{2,1,0:T(8,128)}), f32[8,40,128]{2,1,0:T(8,128)S(1)}, u32[]{:S(2)}, u32[]{:S(2)}) async-start(f32[8,40,128]{2,1,0:T(8,128)} %broadcast_in_dim.15), calls=%async_computation.6 | async-start | bytes 327680 | tf_op jit(solution)/shard_map/all_to_all | solution.py:391
  192.3 22.1 %all-to-all-start.7 = ((f32[12,40,128]{2,1,0:T(8,128)}), f32[12,40,128]{2,1,0:T(8,128)S(1)}, u32[]{:S(2)}, u32[]{:S(2)}) async-start(f32[12,40,128]{2,1,0:T(8,128)} %broadcast_in_dim.16), calls=%async_computation.7 | async-start | bytes 491520 | tf_op jit(solution)/shard_map/all_to_all | solution.py:391
  207.1 0.8 copy-start.4
  208.0 0.9 copy-start.6
  215.1 12.5 %all-to-all-start.8 = ((f32[8,40,128]{2,1,0:T(8,128)}), f32[8,40,128]{2,1,0:T(8,128)S(1)}, u32[]{:S(2)}, u32[]{:S(2)}) async-start(f32[8,40,128]{2,1,0:T(8,128)} %broadcast_in_dim.17), calls=%async_computation.8 | async-start | bytes 327680 | tf_op jit(solution)/shard_map/all_to_all | solution.py:391
  218.5 1.1 copy-start.5
  219.6 1.1 copy-start.7

commit v3 on v2

--- a/solution.py
+++ b/solution.py
@@ -53,12 +53,14 @@
     return lax.ppermute(high, axis, up), lax.ppermute(low, axis, down)
 
 
-def pack_kernel(field_ref, first_ref, last_ref):
+def pack_kernel(row_ref, field_ref, out_ref):
     comps, depth, rows, lanes = field_ref.shape
     planes = comps * depth
     group = lanes // WIDE
     lane = lax.broadcasted_iota(jnp.int32, (rows, lanes), 1)
-    for tile in range(first_ref.shape[0]):
+    row, last = row_ref[0], row_ref[1] - 1
+    heads, tails = [], []
+    for tile in range(out_ref.shape[1]):
         head = jnp.zeros((rows, lanes), jnp.float32)
         tail = jnp.zeros((rows, lanes), jnp.float32)
         for q in range(min(group, planes - tile * group)):
@@ -67,8 +69,18 @@
             here = (lane >= WIDE * q) & (lane < WIDE * (q + 1))
             head = jnp.where(here, pltpu.roll(value, (WIDE * q) % lanes, 1), head)
             tail = jnp.where(here, pltpu.roll(value, (WIDE * (q + 1)) % lanes, 1), tail)
-        first_ref[tile] = head
-        last_ref[tile] = tail
+        heads.append(head)
+        tails.append(tail)
+
+    @pl.when(row > 0)
+    def _():
+        for tile, head in enumerate(heads):
+            out_ref[jnp.maximum(row - 1, 0), tile] = head
+
+    @pl.when(row < last)
+    def _():
+        for tile, tail in enumerate(tails):
+            out_ref[jnp.minimum(row + 1, last), tile] = tail
 
 
 def parts_of(value, axis):
@@ -84,26 +96,29 @@
 
 
 def sections_kernel(
-    assign_ref, row_ref, field_ref, before_ref, after_ref, out_ref, sent_ref, wide_ref, mid_ref, q_ref, place_ref
+    assign_ref, row_ref, field_ref, edges_ref, out_ref, sent_ref, wide_ref, mid_ref, q_ref, place_ref
 ):
     comps, depth_wide, rows, lanes = field_ref.shape
     depth, across = out_ref.shape[1], out_ref.shape[2]
     group = lanes // WIDE
     lane = lax.broadcasted_iota(jnp.int32, (rows, lanes), 1)
 
+    row, last = row_ref[0], row_ref[1] - 1
+    previous, following = jnp.maximum(row - 1, 0), jnp.minimum(row + 1, last)
+    from_next = (lane < WIDE) & (row < last)
+    from_previous = (lane >= lanes - WIDE) & (row > 0)
+
     for c in range(comps):
         for z in range(depth_wide):
             tile, q = divmod(c * depth_wide + z, group)
-            after = pltpu.roll(after_ref[tile], (-WIDE * q) % lanes, 1)
-            before = pltpu.roll(before_ref[tile], (-WIDE * (q + 1)) % lanes, 1)
-            halo = jnp.where(lane < WIDE, after, jnp.where(lane >= lanes - WIDE, before, 0.0))
+            after = pltpu.roll(edges_ref[following, tile], (-WIDE * q) % lanes, 1)
+            before = pltpu.roll(edges_ref[previous, tile], (-WIDE * (q + 1)) % lanes, 1)
+            halo = jnp.where(from_next, after, jnp.where(from_previous, before, 0.0))
             wide_ref[c, z, :, 0:lanes] = field_ref[c, z]
             wide_ref[c, z, :, lanes : 2 * lanes] = halo
 
     edge = lax.broadcasted_iota(jnp.int32, (rows, 2 * lanes), 1)
-    outside = ((edge >= lanes + lanes // 2) & (row_ref[0] == 0)) | (
-        (edge >= lanes) & (edge < lanes + lanes // 2) & (row_ref[0] == row_ref[1] - 1)
-    )
+    outside = ((edge >= lanes + lanes // 2) & (row == 0)) | ((edge >= lanes) & (edge < lanes + lanes // 2) & (row == last))
 
     def tendency(speeds, centre, along_z, along_x, along_y):
         dz_first, dz_second = derivatives(along_z, centre)
@@ -144,8 +159,8 @@
     for b in range(pieces):
         c, x = b // pairs, 2 * (b % pairs)
         to = place_ref[b]
-        sent_ref[to, :, 0:lanes] = out_ref[c, :, x, :]
-        sent_ref[to, :, lanes : 2 * lanes] = out_ref[c, :, x + 1, :]
+        sent_ref[to, 0:depth, :] = out_ref[c, :, x, :]
+        sent_ref[to, depth : 2 * depth, :] = out_ref[c, :, x + 1, :]
 
 
 def pair_index(i, j):
@@ -162,11 +177,18 @@
             )
 
 
-def snapshot_gram_kernel(planes_ref, received_ref, modes_ref, packed_ref, snap_ref):
-    count = snap_ref.shape[0]
+def snapshot_gram_kernel(planes_ref, received_ref, modes_ref, out_ref, snap_ref, packed_ref):
+    count, held = snap_ref.shape
+    slabs = received_ref.shape[0]
     blocks = modes_ref.shape[1] // BLOCK
+    tall = packed_ref.shape[0]
+    groups, share = out_ref.shape[0], tall // out_ref.shape[0]
+    ours = out_ref.shape[1] - share
+    depth = (received_ref.shape[1] - ours) // 2
     for k in range(count):
-        snap_ref[k : k + 1, :] = received_ref[pl.ds(planes_ref[k], 1), :]
+        slab, z = planes_ref[k] // depth, planes_ref[k] % depth
+        snap_ref[k : k + 1, 0:BLOCK] = received_ref[slab, pl.ds(z, 1), :]
+        snap_ref[k : k + 1, BLOCK:held] = received_ref[slab, pl.ds(z + depth, 1), :]
     snap = snap_ref[...]
     cross = product(modes_ref[...], snap, ((0,), (1,)))
     for b in range(blocks):
@@ -175,6 +197,10 @@
     base = blocks // 2 * BLOCK
     packed_ref[base : base + count, :] = jnp.zeros((count, BLOCK), jnp.float32)
     packed_ref[base : base + count, 0:count] = product(snap, snap, ((1,), (1,)))
+    summed = total([received_ref[s, 2 * depth :, :] for s in range(slabs)])
+    for g in range(groups):
+        out_ref[g, 0:share, :] = packed_ref[g * share : (g + 1) * share, :]
+        out_ref[g, share:, :] = summed
 
 
 def lanes_of(value, j):
@@ -252,54 +278,39 @@
     return slice(at, at + BLOCK)
 
 
-def factor_step(b, blocks, gram_ref, side_in, block_ref, side_ref, upper_ref, inverse_ref):
+def modes_factor_kernel(gathered_ref, modes_ref, upper_out, inverse_out, done_ref, block_ref, side_ref, upper_ref, inverse_ref):
+    blocks = modes_ref.shape[1] // BLOCK
+    groups = gathered_ref.shape[0]
+    each = block_ref.shape[0] // groups
     rows = BLOCK // 8
     lane = lax.broadcasted_iota(jnp.int32, (BLOCK, BLOCK), 1)
     sub = lax.broadcasted_iota(jnp.int32, (BLOCK, BLOCK), 0)
-    value = gram_ref[pair_rows(b, b), :]
-    value = jnp.where(lane >= sub, value, value.T)
     unit = identity(BLOCK)
-    main = [value[8 * i : 8 * i + 8, :] for i in range(rows)]
-    side = [unit[8 * i : 8 * i + 8, :] for i in range(rows)]
-    eliminate(main, side, upper_ref, inverse_ref, 0, rows, rows)
-    inverse = inverse_ref[...]
-    for i in range(b):
-        for j in range(i, blocks):
-            block_ref[pair_rows(i, j), :] = gram_ref[pair_rows(i, j), :]
-            if j < b:
-                side_ref[pair_rows(i, j), :] = side_in[pair_rows(i, j), :]
-    block_ref[pair_rows(b, b), :] = upper_ref[...]
-    side_ref[pair_rows(b, b), :] = inverse
-    for j in range(b):
-        side_ref[pair_rows(j, b), :] = product(inverse, side_in[pair_rows(j, b), :], ((1,), (0,)))
-    for j in range(b + 1, blocks):
-        block_ref[pair_rows(b, j), :] = product(inverse, gram_ref[pair_rows(b, j), :], ((1,), (0,)))
-    for i in range(b + 1, blocks):
-        factor = block_ref[pair_rows(b, i), :]
-        for j in range(i, blocks):
-            taken = product(factor, block_ref[pair_rows(b, j), :], ((0,), (0,)))
-            block_ref[pair_rows(i, j), :] = gram_ref[pair_rows(i, j), :] - taken
+    zero = jnp.zeros((BLOCK, BLOCK), jnp.float32)
+    for g in range(groups):
+        block_ref[g * each : (g + 1) * each, :] = gathered_ref[g, gathered_ref.shape[1] - each :, :]
+    for b in range(blocks):
+        value = block_ref[pair_rows(b, b), :]
+        value = jnp.where(lane >= sub, value, value.T)
+        main = [value[8 * i : 8 * i + 8, :] for i in range(rows)]
+        side = [unit[8 * i : 8 * i + 8, :] for i in range(rows)]
+        eliminate(main, side, upper_ref, inverse_ref, 0, rows, rows)
+        inverse = inverse_ref[...]
+        block_ref[pair_rows(b, b), :] = upper_ref[...]
+        side_ref[pair_rows(b, b), :] = inverse
         for j in range(b):
-            taken = product(factor, side_ref[pair_rows(j, b), :], ((0,), (0,)))
-            side_ref[pair_rows(j, i), :] = side_in[pair_rows(j, i), :] - taken
-        side_ref[pair_rows(b, i), :] = -product(factor, inverse, ((0,), (0,)))
-
-
-def first_factor_kernel(gram_ref, block_ref, side_ref, upper_ref, inverse_ref):
-    factor_step(0, 4, gram_ref, None, block_ref, side_ref, upper_ref, inverse_ref)
-
-
-def next_factor_kernel(b):
-    def next_factor(gram_ref, side_in, block_ref, side_ref, upper_ref, inverse_ref):
-        factor_step(b, 4, gram_ref, side_in, block_ref, side_ref, upper_ref, inverse_ref)
-
-    return next_factor
-
-
-def last_factor_kernel(gram_ref, side_in, modes_ref, upper_out, inverse_out, done_ref, block_ref, side_ref, upper_ref, inverse_ref):
-    blocks = modes_ref.shape[1] // BLOCK
-    factor_step(blocks - 1, blocks, gram_ref, side_in, block_ref, side_ref, upper_ref, inverse_ref)
-    zero = jnp.zeros((BLOCK, BLOCK), jnp.float32)
+            side_ref[pair_rows(j, b), :] = product(inverse, side_ref[pair_rows(j, b), :], ((1,), (0,)))
+        for j in range(b + 1, blocks):
+            block_ref[pair_rows(b, j), :] = product(inverse, block_ref[pair_rows(b, j), :], ((1,), (0,)))
+        for i in range(b + 1, blocks):
+            factor = block_ref[pair_rows(b, i), :]
+            for j in range(i, blocks):
+                taken = product(factor, block_ref[pair_rows(b, j), :], ((0,), (0,)))
+                block_ref[pair_rows(i, j), :] = block_ref[pair_rows(i, j), :] - taken
+            for j in range(b):
+                taken = product(factor, side_ref[pair_rows(j, b), :], ((0,), (0,)))
+                side_ref[pair_rows(j, i), :] = side_ref[pair_rows(j, i), :] - taken
+            side_ref[pair_rows(b, i), :] = -product(factor, inverse, ((0,), (0,)))
     for i in range(blocks):
         for j in range(blocks):
             here = (slice(i * BLOCK, (i + 1) * BLOCK), slice(j * BLOCK, (j + 1) * BLOCK))
@@ -339,102 +350,76 @@
     return jax.ShapeDtypeStruct(shape, jnp.float32)
 
 
-def together(*values):
-    return lax.optimization_barrier(values)
-
-
-def halo_field(velocity, first, last, packed):
-    depth = velocity.shape[1]
-    before, after = both_ways(first, last, "grp", True)
-    share = scattered_sum(packed, "grp")
-    before, after, share = together(before, after, share)
+def everyones(value, axis):
+    copies = jnp.broadcast_to(value[None], (lax.axis_size(axis),) + value.shape)
+    return lax.all_to_all(copies, axis, 0, 0, tiled=True)
+
+
+def sections(velocity, assign, extra):
+    comps, depth, across, height = velocity.shape
+    before, after = both_ways(velocity[:, :, :WIDE], velocity[:, :, across - WIDE :], "grp", True)
     field = jnp.concatenate([velocity, after, before], axis=2)
     before, after = both_ways(field[:, :WIDE], field[:, depth - WIDE :], "slab", True)
-    share = scattered_sum(share, "row")
-    before, after, share = together(before, after, share)
     field = jnp.concatenate([before, field, after], axis=1)
-    shape = field.shape
-    tiles = -(-shape[0] * shape[1] * WIDE // shape[3])
-    edge = f32(tiles, shape[2], shape[3])
-    first, last = vmem_call(pack_kernel, [edge, edge], [VM], moved=4 * field.size)(field)
-    before, after = both_ways(first, last, "row", False)
-    share = jnp.sum(everyones(share, "slab"), axis=0)
-    return (field,) + tuple(together(before, after, share))
-
-
-def sections(field, before, after, assign, depth, across):
-    comps, height = field.shape[0], field.shape[3]
+    deep, rows = field.shape[1], field.shape[2]
     where = jnp.stack([lax.axis_index("row"), lax.axis_size("row")]).astype(jnp.int32)
+    tiles = -(-comps * deep * WIDE // height)
+    edges = vmem_call(pack_kernel, f32(lax.axis_size("row"), tiles, rows, height), [SM, VM], moved=4 * field.size)(where, field)
+    edges = lax.all_to_all(edges, "row", 0, 0, tiled=True)
     pieces = comps * across // 2
-    wide = (comps, field.shape[1], field.shape[2], 2 * height)
+    wide = (comps, deep, rows, 2 * height)
     return vmem_call(
         sections_kernel,
-        [f32(comps, depth, across, height), f32(pieces, depth, 2 * height)],
-        [SM, SM, VM, VM, VM],
+        [f32(comps, depth, across, height), f32(pieces, 2 * depth + extra, height)],
+        [SM, SM, VM, VM],
         scratch=[
             pltpu.VMEM(wide, jnp.float32),
             pltpu.VMEM(wide, jnp.float32),
-            pltpu.VMEM((comps, field.shape[1], across, height), jnp.float32),
+            pltpu.VMEM((comps, deep, across, height), jnp.float32),
             pltpu.SMEM((pieces,), jnp.int32),
         ],
         moved=32 * field.size,
-    )(assign, where, field, before, after)
-
-
-def scattered_sum(value, axis):
-    shares = value.reshape(lax.axis_size(axis), -1, value.shape[1])
-    return jnp.sum(lax.all_to_all(shares, axis, 0, 0, tiled=True), axis=0)
-
-
-def everyones(value, axis):
-    copies = jnp.broadcast_to(value[None], (lax.axis_size(axis),) + value.shape)
-    return lax.all_to_all(copies, axis, 0, 0, tiled=True)
+    )(assign, where, field, edges)
 
 
 def on_device(velocity, modes, planes, assign):
     count, rank, held = planes.shape[0], modes.shape[1], modes.shape[0]
-    devices = lax.axis_size("grp") * lax.axis_size("slab") * lax.axis_size("row")
-    scale = 1.0 / float(held * devices)
+    groups, slabs = lax.axis_size("grp"), lax.axis_size("slab")
+    scale = 1.0 / float(held * groups * slabs * lax.axis_size("row"))
     blocks = rank // BLOCK
     rows = blocks * (blocks + 1) // 2 * BLOCK
     tall = blocks // 2 * BLOCK + count
-    block = [pltpu.VMEM((BLOCK, BLOCK), jnp.float32)] * 2
-    state = [f32(rows, BLOCK), f32(rows, BLOCK)]
-    cost = 7 * 1000 * 1000 * 1000
-
-    across = velocity.shape[2]
-    first, last = velocity[:, :, :WIDE], velocity[:, :, across - WIDE :]
+    part = tall // groups
+    each = rows // groups
+    piece = -(-each // (8 * slabs)) * 8
+
     packed = vmem_call(modes_gram_kernel, f32(rows, BLOCK), [VM], flops=12 * held * rank * rank, moved=4 * modes.size)(modes)
-    field, before, after, share = halo_field(velocity, first, last, packed)
-    share = everyones(share * scale, "row").reshape(-1, BLOCK)
-    advanced, sent = sections(field, before, after, assign, velocity.shape[1], velocity.shape[2])
-    sent, share = together(sent, share)
-    received = lax.all_to_all(sent, "slab", 0, 0, tiled=True).reshape(-1, sent.shape[2])
-    packed, snap = vmem_call(snapshot_gram_kernel, [f32(tall, BLOCK), f32(count, held)], [SM, VM, VM])(planes, received, modes)
-
-    groups = lax.axis_size("grp")
-    part = tall // groups
-    copies = jnp.broadcast_to(share[None], (groups,) + share.shape)
-    both = jnp.concatenate([packed.reshape(groups, part, BLOCK), copies], axis=1)
-    both = lax.all_to_all(both, "grp", 0, 0, tiled=True)
+    share = lax.psum_scatter(packed, "grp", scatter_dimension=0, tiled=True)
+    share = jnp.pad(share, ((0, piece * slabs - each), (0, 0))).reshape(slabs, piece, BLOCK)
+
+    advanced, sent = sections(velocity, assign, piece)
+    sent = lax.dynamic_update_slice(sent, share, (0, sent.shape[1] - piece, 0))
+    received = lax.all_to_all(sent, "slab", 0, 0, tiled=True)
+    both, snap = vmem_call(
+        snapshot_gram_kernel,
+        [f32(groups, part + piece, BLOCK), f32(count, held)],
+        [SM, VM, VM],
+        scratch=[pltpu.VMEM((tall, BLOCK), jnp.float32)],
+    )(planes, received, modes)
+    both = jnp.sum(lax.all_to_all(both, "row", 0, 0, tiled=True), axis=0)
+    both = everyones(both, "slab") * scale
+    both = jnp.concatenate([jnp.sum(both[:, :part], axis=0), both[:, part:].reshape(-1, BLOCK)[:each]])
+    both = everyones(both, "grp")
     share = jnp.sum(both[:, :part], axis=0)
-    gram = both[:, part:].reshape(rows, BLOCK)
-
-    lower = vmem_call(first_factor_kernel, state, [VM], scratch=block, flops=cost)(gram)
-    lower = vmem_call(next_factor_kernel(1), state, [VM, VM], scratch=block, flops=cost)(*lower)
-    share = jnp.sum(everyones(share, "row"), axis=0)
-    share, *lower = together(share, *lower)
-    lower = vmem_call(next_factor_kernel(2), state, [VM, VM], scratch=block, flops=cost)(*lower)
-    share = jnp.sum(everyones(share, "slab"), axis=0) * scale
-    share, *lower = together(share, *lower)
-    packed = everyones(share, "grp").reshape(tall, BLOCK)
+    packed = everyones(share, "row").reshape(tall, BLOCK)
+
     upper, inverse, done = vmem_call(
-        last_factor_kernel,
+        modes_factor_kernel,
         [f32(rank, rank), f32(rank, rank), f32(rank, held)],
-        [VM, VM, VM],
-        scratch=[pltpu.VMEM((rows, BLOCK), jnp.float32)] * 2 + block,
-        flops=cost,
-    )(*lower, modes)
+        [VM, VM],
+        scratch=[pltpu.VMEM((rows, BLOCK), jnp.float32)] * 2 + [pltpu.VMEM((BLOCK, BLOCK), jnp.float32)] * 2,
+        flops=28 * 1000 * 1000 * 1000,
+    )(both, modes)
     basis, factor = vmem_call(
         finish_kernel,
         [f32(rank + count, held), f32(rank + count, rank + count)],

time: 234 us -> 226 us (0.966)
  blocking collectives: 57.1 us -> 130 us
  starting transfers between devices: 86.3 us -> 22.9 us
  waiting for transfers between devices: 33.6 us -> 6.75 us
  between operations: 0.9 us -> 14.2 us
  local copies, waits for them, and re-layouts: 9.11 us -> 5.65 us
    all_to_all x2 -> x5, blocking collectives: 57.1 us -> 130 us  [the longest x2 52.9 us: everyones(): return lax.all_to_all(copies, axis, 0, 0, tiled=True)]
    all_to_all x5 -> x1, starting transfers between devices: 35.2 us -> 3.56 us  [everyones(): return lax.all_to_all(copies, axis, 0, 0, tiled=True)]
    all_to_all x2 -> x0, starting transfers between devices: 26.8 us -> none  [scattered_sum(): return jnp.sum(lax.all_to_all(shares, axis, 0, 0, tiled=True), axis=0)]
    all_to_all x2 -> x0, waiting for transfers between devices: 12 us -> none  [scattered_sum(): return jnp.sum(lax.all_to_all(shares, axis, 0, 0, tiled=True), axis=0)]
    ppermute x6 -> x4, waiting for transfers between devices: 15 us -> 6.73 us  [both_ways(): return (lax.ppermute(high, axis, up), lax.ppermute(low, axis, down))]
    all_to_all x5 -> x1, waiting for transfers between devices: 6.64 us -> 0.01 us  [everyones(): return lax.all_to_all(copies, axis, 0, 0, tiled=True)]
    ppermute x6 -> x4, starting transfers between devices: 24.4 us -> 19.3 us  [both_ways(): return (lax.ppermute(high, axis, up), lax.ppermute(low, axis, down))]
    broadcast_in_dim x5 -> x3, local copies, waits for them, and re-layouts: 3.39 us -> 0.76 us  [everyones(): copies = jnp.broadcast_to(value[None], (lax.axis_size(axis),) + value.shape)]
  transfers between devices with their start and end apart: 13 -> 6, of which waited for: 7 -> 3; matrix products, arithmetic and copies ran while one was open for 0% -> 0% of each run, Pallas kernels for 16% -> 16%
where the time goes in v3:
time: 226 us
  blocking collectives  130 us (58%)
  Pallas kernels  45.5 us (20%)
  starting transfers between devices  22.9 us (10%)
  between operations  14.2 us (6%)
  waiting for transfers between devices  6.75 us (3%)
  local copies, waits for them, and re-layouts  5.65 us (2%)
    all_to_all x2, blocking collectives, everyones(): return lax.all_to_all(copies, axis, 0, 0, tiled=True)  52.9 us
    all_to_all x1, blocking collectives, on_device(): received = lax.all_to_all(sent, 'slab', 0, 0, tiled=True)  30.8 us
    all_to_all x1, blocking collectives, sections(): edges = lax.all_to_all(edges, 'row', 0, 0, tiled=True)  30.5 us
    pallas_call x1, Pallas kernels, on_device(): vmem_call(modes_factor_kernel, [f32(rank, rank), f32(rank, rank), f32(ran...  24.8 us
    ppermute x4, starting transfers between devices, both_ways(): return (lax.ppermute(high, axis, up), lax.ppermute(low, axis, down))  19.3 us
    all_to_all x1, blocking collectives, on_device(): both = jnp.sum(lax.all_to_all(both, 'row', 0, 0, tiled=True), axis=0)  16 us
    pallas_call x1, Pallas kernels, sections(): vmem_call(sections_kernel, [f32(comps, depth, across, height), f32(pieces...  10.5 us
    ppermute x4, waiting for transfers between devices, both_ways(): return (lax.ppermute(high, axis, up), lax.ppermute(low, axis, down))  6.73 us
  transfers between devices with their start and end apart: 6, of which 3 were waited for; matrix products, arithmetic and copies ran while one was open for 0% of the time, Pallas kernels for 16%

profile of v3, /device:TPU:1, one launch (start us, length us, event | category | flops | bytes accessed | tf_op | source)
XLA Modules:
  0.0 225.7 jit_solution(2464112728104064439)
XLA Ops:
  7.2 1.0 copy-done
  8.3 2.2 shard_map.69
  10.5 5.9 %collective-permute-start = (f32[3,32,4,128]{3,2,1,0:T(4,128)S(1)}, f32[3,32,4,128]{3,2,1,0:T(4,128)S(1)}, u32[]{:S(2)}, u32[]{:S(2)}) collective-permute-start(f32[3,32,4,128]{3,2,1,0:T(4,128)S(1)} %get-tuple-element.23), channel_id=1, source_target_pairs={{96,0},{192,96},{288,192},{384,288},{480,384},{576,480},{672,576},... | collective-permute-start | bytes 589832 | tf_op jit(solution)/shard_map/ppermute | solution.py:53
  16.4 1.9 collective-permute-start.1
  19.0 5.0 %collective-permute-done.1 = f32[3,32,4,128]{3,2,1,0:T(4,128)S(1)} collective-permute-done((f32[3,32,4,128]{3,2,1,0:T(4,128)S(1)}, f32[3,32,4,128]{3,2,1,0:T(4,128)S(1)}, u32[]{:S(2)}, u32[]{:S(2)}) %collective-permute-start.1) | collective-permute-done | bytes 196640 | tf_op jit(solution)/shard_map/ppermute | solution.py:53
  24.1 6.7 %collective-permute-start.2 = (f32[3,4,16,128]{3,2,1,0:T(8,128)S(1)}, f32[3,4,16,128]{3,2,1,0:T(8,128)S(1)}, u32[]{:S(2)}, u32[]{:S(2)}) collective-permute-start(f32[3,4,16,128]{3,2,1,0:T(8,128)S(1)} %get-tuple-element.21), channel_id=1, source_target_pairs={{0,8},{8,16},{16,24},{24,32},{32,40},{40,48},{48,56},{56,64},{64,7... | collective-permute-start | bytes 294920 | tf_op jit(solution)/shard_map/ppermute | solution.py:53
  30.8 4.8 %collective-permute-start.3 = (f32[3,4,16,128]{3,2,1,0:T(8,128)S(1)}, f32[3,4,16,128]{3,2,1,0:T(8,128)S(1)}, u32[]{:S(2)}, u32[]{:S(2)}) collective-permute-start(f32[3,4,16,128]{3,2,1,0:T(8,128)S(1)} %get-tuple-element.22), channel_id=1, source_target_pairs={{8,0},{16,8},{24,16},{32,24},{40,32},{48,40},{56,48},{64,56},{72,6... | collective-permute-start | bytes 294920 | tf_op jit(solution)/shard_map/ppermute | solution.py:53
  35.7 1.0 collective-permute-done.3
  36.8 1.1 shard_map.67
  38.0 30.5 %all_to_all.30.edges_ref = f32[8,4,16,128]{3,2,1,0:T(8,128)S(1)} all-to-all(f32[8,4,16,128]{3,2,1,0:T(8,128)S(1)} %shard_map.67), channel_id=1, replica_groups=mesh['grp'=8,'slab'=12,'row'=8] {'row'}, dimensions={0} | all-to-all | bytes 524288 | tf_op jit(solution)/shard_map/all_to_all | solution.py:368
  68.5 10.5 %shard_map.68 = (f32[3,32,8,128]{3,2,1,0:T(8,128)}, f32[12,80,128]{2,1,0:T(8,128)S(1)}) custom-call(s32[12]{0:T(128)S(1)} %copy-done.6, s32[2]{0:T(128)S(1)} %pad_add_fusion.row_ref, f32[3,40,16,128]{3,2,1,0:T(8,128)S(1)} %pad_maximum_fusion.field_ref, f32[8,4,16,128]{3,2,1,0:T(8,128)S(1)} %all_to_all.30.edges_ref), custom_call_target="tpu_custom_call" | custom-call | bytes 7864320 | tf_op jit(solution)/shard_map/pallas_call | solution.py:371
  79.1 0.9 pad.4
  80.0 30.8 %all_to_all.31.received_ref = f32[12,80,128]{2,1,0:T(8,128)S(1)} all-to-all(f32[12,80,128]{2,1,0:T(8,128)S(1)} %constant_dynamic-update-slice_fusion), channel_id=1, replica_groups=mesh['grp'=8,'slab'=12,'row'=8] {'slab'}, dimensions={0} | all-to-all | bytes 983040 | tf_op jit(solution)/shard_map/all_to_all | solution.py:402
  110.8 1.6 shard_map.70
  112.4 16.0 %all_to_all.32 = f32[8,56,128]{2,1,0:T(8,128)S(1)} all-to-all(f32[8,56,128]{2,1,0:T(8,128)S(1)} %get-tuple-element.14), channel_id=1, replica_groups=mesh['grp'=8,'slab'=12,'row'=8] {'row'}, dimensions={0} | all-to-all | bytes 458752 | tf_op jit(solution)/shard_map/all_to_all | solution.py:409
  128.5 25.4 %all_to_all.33 = f32[12,56,128]{2,1,0:T(8,128)S(1)} all-to-all(f32[12,56,128]{2,1,0:T(8,128)S(1)} %broadcast_in_dim.6), channel_id=1, replica_groups=mesh['grp'=8,'slab'=12,'row'=8] {'slab'}, dimensions={0} | all-to-all | bytes 688128 | tf_op jit(solution)/shard_map/all_to_all | solution.py:355
  154.1 27.5 %all_to_all.34.gathered_ref = f32[8,200,128]{2,1,0:T(8,128)S(1)} all-to-all(f32[8,200,128]{2,1,0:T(8,128)S(1)} %broadcast_in_dim.7), channel_id=1, replica_groups=mesh['grp'=8,'slab'=12,'row'=8] {'grp'}, dimensions={0} | all-to-all | bytes 1638400 | tf_op jit(solution)/shard_map/all_to_all | solution.py:355
  181.6 0.7 broadcast_in_dim.8
  182.3 3.6 %all-to-all-start.5 = ((f32[8,40,128]{2,1,0:T(8,128)}), f32[8,40,128]{2,1,0:T(8,128)S(1)}, u32[]{:S(2)}, u32[]{:S(2)}) async-start(f32[8,40,128]{2,1,0:T(8,128)} %broadcast_in_dim.8), calls=%async_computation.6 | async-start | bytes 327680 | tf_op jit(solution)/shard_map/all_to_all | solution.py:355
  185.9 1.0 copy-done.2
  186.9 24.8 %shard_map.71 = (f32[512,512]{1,0:T(8,128)S(1)}, f32[512,512]{1,0:T(8,128)S(1)}, f32[512,256]{1,0:T(8,128)S(1)}) custom-call(f32[8,200,128]{2,1,0:T(8,128)S(1)} %all_to_all.34.gathered_ref, f32[256,512]{1,0:T(8,128)S(1)} %copy-done.2), custom_call_target="tpu_custom_call" | custom-call | flops 28000000000 | tf_op jit(solution)/shard_map/pallas_call | solution.py:416
  211.7 0.8 copy-done.3
  212.5 1.0 copy-done.4
  213.5 5.3 %shard_map.72 = (f32[576,256]{1,0:T(8,128)}, f32[576,576]{1,0:T(8,128)}) custom-call(f32[320,128]{1,0:T(8,128)S(1)} %bitcast.5, f32[64,256]{1,0:T(8,128)S(1)} %get-tuple-element.15.snap_ref, f32[512,512]{1,0:T(8,128)S(1)} %get-tuple-element.16.upper_ref, f32[512,512]{1,0:T(8,128)S(1)} %get-tuple-element.17.inverse_ref, f32[512,256]{1,0:T(8,128)S(1)} %copy-done.4), custom_call_target="tpu_custom_call" | custom-call | tf_op jit(solution)/shard_map/pallas_call | solution.py:423
  (31 shorter events, 1.2 us)
Async XLA Ops:
  7.2 71.9 %reduce-scatter.2.cloned.1.call-start = ((), (), s32[]{:S(2)}) async-start(), calls=%async_computation.7 | async-start | bytes 737280 | tf_op jit(solution)/shard_map/reduce_scatter | solution.py:397
  7.2 1.0 copy-start
  8.3 2.2 copy-start.7
  10.5 8.5 %collective-permute-start = (f32[3,32,4,128]{3,2,1,0:T(4,128)S(1)}, f32[3,32,4,128]{3,2,1,0:T(4,128)S(1)}, u32[]{:S(2)}, u32[]{:S(2)}) collective-permute-start(f32[3,32,4,128]{3,2,1,0:T(4,128)S(1)} %get-tuple-element.23), channel_id=1, source_target_pairs={{96,0},{192,96},{288,192},{384,288},{480,384},{576,480},{672,576},... | collective-permute-start | bytes 589832 | tf_op jit(solution)/shard_map/ppermute | solution.py:53
  16.4 7.6 %collective-permute-start.1 = (f32[3,32,4,128]{3,2,1,0:T(4,128)S(1)}, f32[3,32,4,128]{3,2,1,0:T(4,128)S(1)}, u32[]{:S(2)}, u32[]{:S(2)}) collective-permute-start(f32[3,32,4,128]{3,2,1,0:T(4,128)S(1)} %get-tuple-element.24), channel_id=1, source_target_pairs={{0,96},{96,192},{192,288},{288,384},{384,480},{480,576},{576,672},... | collective-permute-start | bytes 589832 | tf_op jit(solution)/shard_map/ppermute | solution.py:53
  24.1 11.6 %collective-permute-start.2 = (f32[3,4,16,128]{3,2,1,0:T(8,128)S(1)}, f32[3,4,16,128]{3,2,1,0:T(8,128)S(1)}, u32[]{:S(2)}, u32[]{:S(2)}) collective-permute-start(f32[3,4,16,128]{3,2,1,0:T(8,128)S(1)} %get-tuple-element.21), channel_id=1, source_target_pairs={{0,8},{8,16},{16,24},{24,32},{32,40},{40,48},{48,56},{56,64},{64,7... | collective-permute-start | bytes 294920 | tf_op jit(solution)/shard_map/ppermute | solution.py:53
  30.8 5.9 %collective-permute-start.3 = (f32[3,4,16,128]{3,2,1,0:T(8,128)S(1)}, f32[3,4,16,128]{3,2,1,0:T(8,128)S(1)}, u32[]{:S(2)}, u32[]{:S(2)}) collective-permute-start(f32[3,4,16,128]{3,2,1,0:T(8,128)S(1)} %get-tuple-element.22), channel_id=1, source_target_pairs={{8,0},{16,8},{24,16},{32,24},{40,32},{48,40},{56,48},{64,56},{72,6... | collective-permute-start | bytes 294920 | tf_op jit(solution)/shard_map/ppermute | solution.py:53
  35.7 32.8 %copy-start.6 = (s32[12]{0:T(128)S(1)}, s32[12]{0:T(128)}, u32[]{:S(2)}) copy-start(s32[12]{0:T(128)} %assign_ref.1) | copy-start | bytes 148
  38.0 72.8 %copy-start.1 = (f32[256,512]{1,0:T(8,128)S(1)}, f32[256,512]{1,0:T(8,128)}, u32[]{:S(2)}) copy-start(f32[256,512]{1,0:T(8,128)} %modes_ref.5) | copy-start | bytes 1572868
  38.0 72.8 %copy-start.5 = (s32[64]{0:T(128)S(1)}, s32[64]{0:T(128)}, u32[]{:S(2)}) copy-start(s32[64]{0:T(128)} %planes_ref.1) | copy-start | bytes 772
  182.3 30.2 %all-to-all-start.5 = ((f32[8,40,128]{2,1,0:T(8,128)}), f32[8,40,128]{2,1,0:T(8,128)S(1)}, u32[]{:S(2)}, u32[]{:S(2)}) async-start(f32[8,40,128]{2,1,0:T(8,128)} %broadcast_in_dim.8), calls=%async_computation.6 | async-start | bytes 327680 | tf_op jit(solution)/shard_map/all_to_all | solution.py:355
  185.9 1.0 copy-start.2
  211.7 0.8 copy-start.3
  212.5 1.0 copy-start.4
Sparse Core Ops, SparseCore 0:
  11.7 45.3 reduce-scatter.1

commit v4 on v3

--- a/solution.py
+++ b/solution.py
@@ -1,3 +1,5 @@
+import functools
+
 import jax
 import jax.numpy as jnp
 from jax import lax
@@ -14,7 +16,7 @@
 ALL = ("grp", "slab", "row")
 WIDE = 4
 BLOCK = 128
-VMEM_LIMIT = 48 * 1024 * 1024
+VMEM_LIMIT = 20 * 1024 * 1024
 
 
 def vmem_call(kernel, out_shape, in_specs, scratch=(), aliases=None, flops=0, moved=0):
@@ -46,6 +48,12 @@
     )
 
 
+def total(terms):
+    while len(terms) > 1:
+        terms = [a + b for a, b in zip(terms[::2], terms[1::2])] + ([terms[-1]] if len(terms) % 2 else [])
+    return terms[0]
+
+
 def both_ways(low, high, axis, wrap):
     devices = lax.axis_size(axis)
     up = [(i, (i + 1) % devices) for i in range(devices if wrap else devices - 1)]
@@ -53,14 +61,19 @@
     return lax.ppermute(high, axis, up), lax.ppermute(low, axis, down)
 
 
-def pack_kernel(row_ref, field_ref, out_ref):
+def pack_kernel(row_ref, field_ref, share_ref, out_ref):
     comps, depth, rows, lanes = field_ref.shape
     planes = comps * depth
     group = lanes // WIDE
     lane = lax.broadcasted_iota(jnp.int32, (rows, lanes), 1)
     row, last = row_ref[0], row_ref[1] - 1
     heads, tails = [], []
-    for tile in range(out_ref.shape[1]):
+    tiles = -(-planes // group)
+    summed = total([share_ref[g] for g in range(share_ref.shape[0])])
+    each = summed.shape[0] // out_ref.shape[0]
+    for slot in range(out_ref.shape[0]):
+        out_ref[slot, tiles * rows : tiles * rows + each, :] = summed[slot * each : (slot + 1) * each]
+    for tile in range(tiles):
         head = jnp.zeros((rows, lanes), jnp.float32)
         tail = jnp.zeros((rows, lanes), jnp.float32)
         for q in range(min(group, planes - tile * group)):
@@ -75,12 +88,12 @@
     @pl.when(row > 0)
     def _():
         for tile, head in enumerate(heads):
-            out_ref[jnp.maximum(row - 1, 0), tile] = head
+            out_ref[jnp.maximum(row - 1, 0), tile * rows : (tile + 1) * rows, :] = head
 
     @pl.when(row < last)
     def _():
         for tile, tail in enumerate(tails):
-            out_ref[jnp.minimum(row + 1, last), tile] = tail
+            out_ref[jnp.minimum(row + 1, last), tile * rows : (tile + 1) * rows, :] = tail
 
 
 def parts_of(value, axis):
@@ -89,9 +102,8 @@
 
 
 def derivatives(parts, centre):
-    far = parts[0], parts[3]
-    first = ((far[0] - far[1]) + 8.0 * (parts[2] - parts[1])) * (1.0 / 12.0)
-    second = (16.0 * (parts[1] + parts[2]) - (far[0] + far[1]) - 30.0 * centre) * (1.0 / 12.0)
+    first = (parts[0] - parts[3]) + 8.0 * (parts[2] - parts[1])
+    second = 16.0 * (parts[1] + parts[2]) - (parts[0] + parts[3])
     return first, second
 
 
@@ -111,8 +123,8 @@
     for c in range(comps):
         for z in range(depth_wide):
             tile, q = divmod(c * depth_wide + z, group)
-            after = pltpu.roll(edges_ref[following, tile], (-WIDE * q) % lanes, 1)
-            before = pltpu.roll(edges_ref[previous, tile], (-WIDE * (q + 1)) % lanes, 1)
+            after = pltpu.roll(edges_ref[following, tile * rows : (tile + 1) * rows, :], (-WIDE * q) % lanes, 1)
+            before = pltpu.roll(edges_ref[previous, tile * rows : (tile + 1) * rows, :], (-WIDE * (q + 1)) % lanes, 1)
             halo = jnp.where(from_next, after, jnp.where(from_previous, before, 0.0))
             wide_ref[c, z, :, 0:lanes] = field_ref[c, z]
             wide_ref[c, z, :, lanes : 2 * lanes] = halo
@@ -125,14 +137,14 @@
         dx_first, dx_second = derivatives(along_x, centre)
         dy_first, dy_second = derivatives(along_y, centre)
         convect = speeds[0] * dx_first + speeds[1] * dy_first + speeds[2] * dz_first
-        return viscosity * (dx_second + dy_second + dz_second) - convect
+        return viscosity * ((dx_second + dy_second) + (dz_second - 90.0 * centre)) - convect
 
     def first_section(z, _):
         speeds = [wide_ref[c, z] for c in range(comps)]
         for c in range(comps):
             along_z = [wide_ref[c, z + k] for k in (-2, -1, 1, 2)]
             slope = tendency(speeds, speeds[c], along_z, parts_of(speeds[c], 0), parts_of(speeds[c], 1))
-            q = step_size * slope
+            q = (step_size / 12.0) * slope
             mid_ref[c, z] = jnp.where(outside, 0.0, speeds[c] + third * q)
             q_ref[c, z] = q[:across, :lanes]
         return 0
@@ -146,11 +158,17 @@
             along_x = [p[:across] for p in parts_of(mid_ref[c, z, :, 0:lanes], 0)]
             along_y = [p[:, :lanes] for p in parts_of(mid_ref[c, z, 0:across, :], 1)]
             slope = tendency(speeds, speeds[c], along_z, along_x, along_y)
-            q = carry_back * q_ref[c, z] + step_size * slope
+            q = carry_back * q_ref[c, z] + (step_size / 12.0) * slope
             out_ref[c, z - WIDE] = speeds[c] + second_gain * q
         return 0
 
     lax.fori_loop(WIDE, WIDE + depth, second_section, 0)
+
+    tiles = -(-comps * depth_wide // group)
+    each = edges_ref.shape[1] - tiles * rows
+    summed = total([edges_ref[r, tiles * rows :, :] for r in range(edges_ref.shape[0])])
+    for s in range(sent_ref.shape[0]):
+        sent_ref[s, 2 * depth : 2 * depth + each, :] = summed
 
     pieces = sent_ref.shape[0]
     for s in range(pieces):
@@ -203,6 +221,16 @@
         out_ref[g, share:, :] = summed
 
 
+def merge_kernel(scale, part, received_ref, out_ref):
+    slots = received_ref.shape[0]
+    each = (out_ref.shape[1] - part) // slots
+    summed = total([received_ref[r, 0:part, :] for r in range(slots)]) * scale
+    rows = [received_ref[r, part : part + each, :] * scale for r in range(slots)]
+    whole = jnp.concatenate([summed] + rows, axis=0)
+    for g in range(out_ref.shape[0]):
+        out_ref[g] = whole
+
+
 def lanes_of(value, j):
     return jnp.broadcast_to(value[:, j : j + 1], value.shape)
 
@@ -211,56 +239,42 @@
     return jnp.broadcast_to(value[i : i + 1, :], value.shape)
 
 
-def total(terms):
-    while len(terms) > 1:
-        terms = [a + b for a, b in zip(terms[::2], terms[1::2])] + ([terms[-1]] if len(terms) % 2 else [])
-    return terms[0]
-
-
-def eliminate(main, side, upper_ref, inverse_ref, first, last, rows):
+def eliminate(main, side, upper_ref, inverse_ref, rows):
     sub = lax.broadcasted_iota(jnp.int32, (8, BLOCK), 0)
     lane = lax.broadcasted_iota(jnp.int32, (8, BLOCK), 1)
-    for p in range(first, last):
+    for p in range(rows):
         top, left = main[p], side[p]
         columns = [lanes_of(top, 8 * p + j) for j in range(8)]
         a = [[row_of(columns[j], i) if j <= i else None for j in range(8)] for i in range(8)]
-        scale = [None] * 8
+        upper = [row_of(top, j) for j in range(8)]
+        lower = [row_of(left, j) for j in range(8)]
+        v = [[None] * 8 for _ in range(8)]
         for j in range(8):
-            scale[j] = lax.rsqrt(a[j][j])
-            for i in range(j + 1, 8):
-                a[i][j] = a[i][j] * scale[j]
+            scale = lax.rsqrt(a[j][j])
+            below = {i: a[i][j] * scale for i in range(j + 1, 8)}
             for m in range(j + 1, 8):
                 for i in range(m, 8):
-                    a[i][m] = a[i][m] - a[i][j] * a[m][j]
-        v = [[None] * 8 for _ in range(8)]
-        for j in range(8):
-            v[j][j] = scale[j]
-            for i in range(j + 1, 8):
-                v[i][j] = -scale[i] * total([a[i][k] * v[k][j] for k in range(j, i)])
-        top_rows = [row_of(top, j) for j in range(8)]
-        left_rows = [row_of(left, j) for j in range(8)]
-        zero = jnp.zeros((8, BLOCK), jnp.float32)
-        down, back = [], []
-        for j in range(8):
-            column, line = zero, zero
-            for i in range(j, 8):
-                column = jnp.where(sub == i, v[i][j], column)
-            for i in range(j + 1):
-                line = jnp.where(sub == i, v[j][i], line)
-            down.append(column)
-            back.append(line)
-        upper = total([down[j] * top_rows[j] for j in range(8)])
-        lower = total([down[j] * left_rows[j] for j in range(8)])
-        upper_ref[8 * p : 8 * p + 8, :] = jnp.where(lane >= 8 * p + sub, upper, 0.0)
-        inverse_ref[8 * p : 8 * p + 8, :] = lower
+                    a[i][m] = a[i][m] - below[i] * below[m]
+            upper[j], lower[j] = upper[j] * scale, lower[j] * scale
+            v[j][j] = scale
+            for k in range(j):
+                v[j][k] = v[j][k] * scale
+            for m in range(j + 1, 8):
+                upper[m] = upper[m] - below[m] * upper[j]
+                lower[m] = lower[m] - below[m] * lower[j]
+                for k in range(j + 1):
+                    taken = below[m] * v[j][k]
+                    v[m][k] = -taken if v[m][k] is None else v[m][k] - taken
+        factor, inverse = upper[7], lower[7]
+        for j in range(7):
+            factor = jnp.where(sub == j, upper[j], factor)
+            inverse = jnp.where(sub == j, lower[j], inverse)
+        upper_ref[8 * p : 8 * p + 8, :] = jnp.where(lane >= 8 * p + sub, factor, 0.0)
+        inverse_ref[8 * p : 8 * p + 8, :] = inverse
         if p + 1 == rows:
             break
-        upper_rows = [row_of(upper, j) for j in range(8)]
-        lower_rows = [row_of(lower, j) for j in range(8)]
-        top = total([back[j] * upper_rows[j] for j in range(8)])
-        left = total([back[j] * lower_rows[j] for j in range(8)])
-        top_rows = [row_of(top, j) for j in range(8)]
-        left_rows = [row_of(left, j) for j in range(8)]
+        top_rows = [total([v[i][j] * upper[i] for i in range(j, 8)]) for j in range(8)]
+        left_rows = [total([v[i][j] * lower[i] for i in range(j, 8)]) for j in range(8)]
         for i in range(p + 1, rows):
             here = [lanes_of(main[i], 8 * p + j) for j in range(8)]
             main[i] = main[i] - total([here[j] * top_rows[j] for j in range(8)])
@@ -294,7 +308,7 @@
         value = jnp.where(lane >= sub, value, value.T)
         main = [value[8 * i : 8 * i + 8, :] for i in range(rows)]
         side = [unit[8 * i : 8 * i + 8, :] for i in range(rows)]
-        eliminate(main, side, upper_ref, inverse_ref, 0, rows, rows)
+        eliminate(main, side, upper_ref, inverse_ref, rows)
         inverse = inverse_ref[...]
         block_ref[pair_rows(b, b), :] = upper_ref[...]
         side_ref[pair_rows(b, b), :] = inverse
@@ -336,7 +350,7 @@
     unit = identity(BLOCK)
     main = [corner_ref[8 * i : 8 * i + 8, :] for i in range(rows)]
     side = [unit[8 * i : 8 * i + 8, :] for i in range(rows)]
-    eliminate(main, side, corner_ref, back_ref, 0, rows, rows)
+    eliminate(main, side, corner_ref, back_ref, rows)
     rest = snap_ref[...] - product(cross, done_ref[...], ((0,), (0,)))
     basis_ref[0:rank, :] = done_ref[...]
     basis_ref[rank:, :] = product(back_ref[:, 0:count], rest, ((1,), (0,)))
@@ -355,22 +369,27 @@
     return lax.all_to_all(copies, axis, 0, 0, tiled=True)
 
 
-def sections(velocity, assign, extra):
+def sections(velocity, assign, shares):
     comps, depth, across, height = velocity.shape
     before, after = both_ways(velocity[:, :, :WIDE], velocity[:, :, across - WIDE :], "grp", True)
+    before, after, shares = lax.optimization_barrier((before, after, shares))
     field = jnp.concatenate([velocity, after, before], axis=2)
     before, after = both_ways(field[:, :WIDE], field[:, depth - WIDE :], "slab", True)
     field = jnp.concatenate([before, field, after], axis=1)
     deep, rows = field.shape[1], field.shape[2]
-    where = jnp.stack([lax.axis_index("row"), lax.axis_size("row")]).astype(jnp.int32)
+    places = lax.axis_size("row")
+    each = shares.shape[1] // places
+    where = jnp.stack([lax.axis_index("row"), places]).astype(jnp.int32)
     tiles = -(-comps * deep * WIDE // height)
-    edges = vmem_call(pack_kernel, f32(lax.axis_size("row"), tiles, rows, height), [SM, VM], moved=4 * field.size)(where, field)
+    edges = vmem_call(pack_kernel, f32(places, tiles * rows + each, height), [SM, VM, VM], moved=4 * field.size)(
+        where, field, shares
+    )
     edges = lax.all_to_all(edges, "row", 0, 0, tiled=True)
     pieces = comps * across // 2
     wide = (comps, deep, rows, 2 * height)
     return vmem_call(
         sections_kernel,
-        [f32(comps, depth, across, height), f32(pieces, 2 * depth + extra, height)],
+        [f32(comps, depth, across, height), f32(pieces, 2 * depth + each, height)],
         [SM, SM, VM, VM],
         scratch=[
             pltpu.VMEM(wide, jnp.float32),
@@ -384,42 +403,38 @@
 
 def on_device(velocity, modes, planes, assign):
     count, rank, held = planes.shape[0], modes.shape[1], modes.shape[0]
-    groups, slabs = lax.axis_size("grp"), lax.axis_size("slab")
-    scale = 1.0 / float(held * groups * slabs * lax.axis_size("row"))
+    groups, slabs, places = lax.axis_size("grp"), lax.axis_size("slab"), lax.axis_size("row")
+    scale = 1.0 / float(held * groups * slabs * places)
     blocks = rank // BLOCK
     rows = blocks * (blocks + 1) // 2 * BLOCK
     tall = blocks // 2 * BLOCK + count
-    part = tall // groups
-    each = rows // groups
-    piece = -(-each // (8 * slabs)) * 8
+    part = tall // places
 
     packed = vmem_call(modes_gram_kernel, f32(rows, BLOCK), [VM], flops=12 * held * rank * rank, moved=4 * modes.size)(modes)
-    share = lax.psum_scatter(packed, "grp", scatter_dimension=0, tiled=True)
-    share = jnp.pad(share, ((0, piece * slabs - each), (0, 0))).reshape(slabs, piece, BLOCK)
-
-    advanced, sent = sections(velocity, assign, piece)
-    sent = lax.dynamic_update_slice(sent, share, (0, sent.shape[1] - piece, 0))
+    shares = lax.all_to_all(packed.reshape(groups, -1, BLOCK), "grp", 0, 0, tiled=True)
+    advanced, sent = sections(velocity, assign, shares)
     received = lax.all_to_all(sent, "slab", 0, 0, tiled=True)
+    each = rows // groups // places
     both, snap = vmem_call(
         snapshot_gram_kernel,
-        [f32(groups, part + piece, BLOCK), f32(count, held)],
+        [f32(places, part + each, BLOCK), f32(count, held)],
         [SM, VM, VM],
         scratch=[pltpu.VMEM((tall, BLOCK), jnp.float32)],
     )(planes, received, modes)
-    both = jnp.sum(lax.all_to_all(both, "row", 0, 0, tiled=True), axis=0)
-    both = everyones(both, "slab") * scale
-    both = jnp.concatenate([jnp.sum(both[:, :part], axis=0), both[:, part:].reshape(-1, BLOCK)[:each]])
-    both = everyones(both, "grp")
-    share = jnp.sum(both[:, :part], axis=0)
-    packed = everyones(share, "row").reshape(tall, BLOCK)
+    both = lax.all_to_all(both, "row", 0, 0, tiled=True)
+    both = vmem_call(functools.partial(merge_kernel, scale, part), f32(groups, part + rows // groups, BLOCK), [VM])(both)
+    both = lax.all_to_all(both, "grp", 0, 0, tiled=True)
+    share = everyones(jnp.sum(both[:, :part], axis=0), "slab")
 
     upper, inverse, done = vmem_call(
         modes_factor_kernel,
         [f32(rank, rank), f32(rank, rank), f32(rank, held)],
         [VM, VM],
         scratch=[pltpu.VMEM((rows, BLOCK), jnp.float32)] * 2 + [pltpu.VMEM((BLOCK, BLOCK), jnp.float32)] * 2,
-        flops=28 * 1000 * 1000 * 1000,
+        flops=20 * 1000 * 1000 * 1000,
     )(both, modes)
+    share, upper = lax.optimization_barrier((share, upper))
+    packed = everyones(jnp.sum(share, axis=0), "row").reshape(tall, BLOCK)
     basis, factor = vmem_call(
         finish_kernel,
         [f32(rank + count, held), f32(rank + count, rank + count)],

time: 226 us -> 226 us (level)
  between operations: 14.2 us -> 0.77 us
  starting transfers between devices: 22.9 us -> 36.2 us
  waiting for transfers between devices: 6.75 us -> 16.2 us
  blocking collectives: 130 us -> 122 us
    all_to_all x2 -> x1, blocking collectives: 52.9 us -> 15.1 us  [everyones(): return lax.all_to_all(copies, axis, 0, 0, tiled=True)]
    all_to_all x1 -> x2, blocking collectives: 16 us -> 40.6 us  [the longest x1 24.8 us: on_device(): both = lax.all_to_all(both, 'grp', 0, 0, tiled=True)]
    ppermute x4, waiting for transfers between devices: 6.73 us -> 16.2 us  [both_ways(): return (lax.ppermute(high, axis, up), lax.ppermute(low, axis, down))]
    all_to_all x1, starting transfers between devices: 3.56 us -> 12.4 us  [everyones(): return lax.all_to_all(copies, axis, 0, 0, tiled=True)]
    all_to_all x0 -> x1, starting transfers between devices: none -> 7.65 us  [on_device(): lax.all_to_all(packed.reshape(groups, -1, BLOCK), 'grp', 0, 0, tiled=True)]
    all_to_all x1, blocking collectives: 30.8 us -> 35.3 us  [on_device(): received = lax.all_to_all(sent, 'slab', 0, 0, tiled=True)]
    ppermute x4, starting transfers between devices: 19.3 us -> 16.2 us  [both_ways(): return (lax.ppermute(high, axis, up), lax.ppermute(low, axis, down))]
  transfers between devices with their start and end apart: 6 -> 6, of which waited for: 3 -> 3; matrix products, arithmetic and copies ran while one was open for 0% -> 0% of each run, Pallas kernels for 16% -> 11%
where the time goes in v4:
time: 226 us; the launch traced here: 224 us
  blocking collectives  122 us (54%)
  Pallas kernels  44.5 us (20%)
  starting transfers between devices  36.2 us (16%)
  waiting for transfers between devices  16.2 us (7%)
  local copies, waits for them, and re-layouts  3.67 us (2%)
    all_to_all x1, blocking collectives, on_device(): received = lax.all_to_all(sent, 'slab', 0, 0, tiled=True)  35.3 us
    all_to_all x1, blocking collectives, sections(): edges = lax.all_to_all(edges, 'row', 0, 0, tiled=True)  30.8 us
    all_to_all x1, blocking collectives, on_device(): both = lax.all_to_all(both, 'grp', 0, 0, tiled=True)  24.8 us
    pallas_call x1, Pallas kernels, on_device(): vmem_call(modes_factor_kernel, [f32(rank, rank), f32(rank, rank), f32(ran...  24.1 us
    ppermute x4, waiting for transfers between devices, both_ways(): return (lax.ppermute(high, axis, up), lax.ppermute(low, axis, down))  16.2 us
    ppermute x4, starting transfers between devices, both_ways(): return (lax.ppermute(high, axis, up), lax.ppermute(low, axis, down))  16.2 us
    all_to_all x1, blocking collectives, on_device(): both = lax.all_to_all(both, 'row', 0, 0, tiled=True)  15.8 us
    all_to_all x1, blocking collectives, everyones(): return lax.all_to_all(copies, axis, 0, 0, tiled=True)  15.1 us
  transfers between devices with their start and end apart: 6, of which 3 were waited for; matrix products, arithmetic and copies ran while one was open for 0% of the time, Pallas kernels for 11%

profile of v4, /device:TPU:1, one launch (start us, length us, event | category | flops | bytes accessed | tf_op | source)
XLA Modules:
  0.0 224.5 jit_solution(14239190686113967281)
XLA Ops:
  0.6 1.0 copy-done
  1.7 2.2 shard_map.67
  3.8 7.7 %all-to-all-start = ((f32[8,160,128]{2,1,0:T(8,128)}), f32[8,160,128]{2,1,0:T(8,128)S(1)}, u32[]{:S(2)}, u32[]{:S(2)}) async-start(f32[8,160,128]{2,1,0:T(8,128)} %bitcast.1), calls=%async_computation | async-start | bytes 1310720 | tf_op jit(solution)/shard_map/all_to_all | solution.py:414
  11.6 4.6 %collective-permute-start.1 = (f32[3,32,4,128]{3,2,1,0:T(4,128)S(1)}, f32[3,32,4,128]{3,2,1,0:T(4,128)S(1)}, u32[]{:S(2)}, u32[]{:S(2)}) collective-permute-start(f32[3,32,4,128]{3,2,1,0:T(4,128)S(1)} %get-tuple-element.33), channel_id=1, source_target_pairs={{96,0},{192,96},{288,192},{384,288},{480,384},{576,480},{672,576},... | collective-permute-start | bytes 589832 | tf_op jit(solution)/shard_map/ppermute | solution.py:61
  16.1 1.9 collective-permute-start
  18.1 8.7 %collective-permute-done.1 = f32[3,32,4,128]{3,2,1,0:T(4,128)S(1)} collective-permute-done((f32[3,32,4,128]{3,2,1,0:T(4,128)S(1)}, f32[3,32,4,128]{3,2,1,0:T(4,128)S(1)}, u32[]{:S(2)}, u32[]{:S(2)}) %collective-permute-start.1) | collective-permute-done | bytes 196640 | tf_op jit(solution)/shard_map/ppermute | solution.py:61
  26.8 3.6 %collective-permute-done = f32[3,32,4,128]{3,2,1,0:T(4,128)S(1)} collective-permute-done((f32[3,32,4,128]{3,2,1,0:T(4,128)S(1)}, f32[3,32,4,128]{3,2,1,0:T(4,128)S(1)}, u32[]{:S(2)}, u32[]{:S(2)}) %collective-permute-start) | collective-permute-done | bytes 196640 | tf_op jit(solution)/shard_map/ppermute | solution.py:61
  30.4 7.8 %collective-permute-start.2 = (f32[3,4,16,128]{3,2,1,0:T(8,128)S(1)}, f32[3,4,16,128]{3,2,1,0:T(8,128)S(1)}, u32[]{:S(2)}, u32[]{:S(2)}) collective-permute-start(f32[3,4,16,128]{3,2,1,0:T(8,128)S(1)} %get-tuple-element.31), channel_id=1, source_target_pairs={{0,8},{8,16},{16,24},{24,32},{32,40},{40,48},{48,56},{56,64},{64,7... | collective-permute-start | bytes 294920 | tf_op jit(solution)/shard_map/ppermute | solution.py:61
  38.2 1.9 collective-permute-start.3
  40.2 3.9 %collective-permute-done.3 = f32[3,4,16,128]{3,2,1,0:T(8,128)S(1)} collective-permute-done((f32[3,4,16,128]{3,2,1,0:T(8,128)S(1)}, f32[3,4,16,128]{3,2,1,0:T(8,128)S(1)}, u32[]{:S(2)}, u32[]{:S(2)}) %collective-permute-start.3) | collective-permute-done | bytes 98336 | tf_op jit(solution)/shard_map/ppermute | solution.py:61
  44.3 1.1 shard_map.68
  45.4 30.8 %all_to_all.35.edges_ref = f32[8,84,128]{2,1,0:T(8,128)S(1)} all-to-all(f32[8,84,128]{2,1,0:T(8,128)S(1)} %shard_map.68), channel_id=1, replica_groups=mesh['grp'=8,'slab'=12,'row'=8] {'row'}, dimensions={0} | all-to-all | bytes 688128 | tf_op jit(solution)/shard_map/all_to_all | solution.py:387
  76.2 10.1 %shard_map.69 = (f32[3,32,8,128]{3,2,1,0:T(8,128)}, f32[12,84,128]{2,1,0:T(8,128)S(1)}) custom-call(s32[12]{0:T(128)S(1)} %copy-done.4, s32[2]{0:T(128)S(1)} %pad_add_fusion.row_ref, f32[3,40,16,128]{3,2,1,0:T(8,128)S(1)} %pad_maximum_fusion.field_ref, f32[8,84,128]{2,1,0:T(8,128)S(1)} %all_to_all.35.edges_ref), custom_call_target="tpu_custom_call" | custom-call | bytes 7864320 | tf_op jit(solution)/shard_map/pallas_call | solution.py:390
  86.4 35.3 %all_to_all.36.received_ref = f32[12,84,128]{2,1,0:T(8,128)S(1)} all-to-all(f32[12,84,128]{2,1,0:T(8,128)S(1)} %get-tuple-element.21), channel_id=1, replica_groups=mesh['grp'=8,'slab'=12,'row'=8] {'slab'}, dimensions={0} | all-to-all | bytes 1032192 | tf_op jit(solution)/shard_map/all_to_all | solution.py:416
  121.7 1.6 shard_map.70
  123.3 15.8 %all_to_all.37.received_ref = f32[8,60,128]{2,1,0:T(8,128)S(1)} all-to-all(f32[8,60,128]{2,1,0:T(8,128)S(1)} %get-tuple-element.22), channel_id=1, replica_groups=mesh['grp'=8,'slab'=12,'row'=8] {'row'}, dimensions={0} | all-to-all | bytes 491520 | tf_op jit(solution)/shard_map/all_to_all | solution.py:424
  139.2 24.8 %all_to_all.38.gathered_ref = f32[8,200,128]{2,1,0:T(8,128)S(1)} all-to-all(f32[8,200,128]{2,1,0:T(8,128)S(1)} %shard_map.71), channel_id=1, replica_groups=mesh['grp'=8,'slab'=12,'row'=8] {'grp'}, dimensions={0} | all-to-all | bytes 1638400 | tf_op jit(solution)/shard_map/all_to_all | solution.py:426
  164.7 12.4 %all-to-all-start.5 = ((f32[12,40,128]{2,1,0:T(8,128)}), f32[12,40,128]{2,1,0:T(8,128)}, u32[]{:S(2)}, u32[]{:S(2)}) async-start(f32[12,40,128]{2,1,0:T(8,128)} %broadcast_in_dim.4), calls=%async_computation.5 | async-start | bytes 491520 | tf_op jit(solution)/shard_map/all_to_all | solution.py:369
  177.1 24.1 %shard_map.72 = (f32[512,512]{1,0:T(8,128)S(1)}, f32[512,512]{1,0:T(8,128)S(1)}, f32[512,256]{1,0:T(8,128)S(1)}) custom-call(f32[8,200,128]{2,1,0:T(8,128)S(1)} %all_to_all.38.gathered_ref, f32[256,512]{1,0:T(8,128)S(1)} %copy-done.1), custom_call_target="tpu_custom_call" | custom-call | flops 20000000000 | tf_op jit(solution)/shard_map/pallas_call | solution.py:429
  201.2 0.8 copy-done.2
  202.0 1.0 reduce_sum.19
  203.0 15.1 %all_to_all.39 = f32[8,40,128]{2,1,0:T(8,128)S(1)} all-to-all(f32[8,40,128]{2,1,0:T(8,128)S(1)} %broadcast_in_dim.5), channel_id=1, replica_groups=mesh['grp'=8,'slab'=12,'row'=8] {'row'}, dimensions={0} | all-to-all | bytes 327680 | tf_op jit(solution)/shard_map/all_to_all | solution.py:369
  218.1 1.0 copy-done.3
  219.2 5.3 %shard_map.73 = (f32[576,256]{1,0:T(8,128)}, f32[576,576]{1,0:T(8,128)}) custom-call(f32[320,128]{1,0:T(8,128)S(1)} %bitcast.4, f32[64,256]{1,0:T(8,128)S(1)} %get-tuple-element.25.snap_ref, f32[512,512]{1,0:T(8,128)S(1)} %get-tuple-element.26.upper_ref, f32[512,512]{1,0:T(8,128)S(1)} %get-tuple-element.27.inverse_ref, f32[512,256]{1,0:T(8,128)S(1)} %copy-done.3), custom_call_target="tpu_custom_call" | custom-call | tf_op jit(solution)/shard_map/pallas_call | solution.py:438
  (22 shorter events, 1.1 us)
Async XLA Ops:
  0.6 1.0 copy-start
  1.7 9.8 %copy-start.6 = (f32[3,32,8,128]{3,2,1,0:T(8,128)S(1)}, f32[3,32,8,128]{3,2,1,0:T(8,128)}, u32[]{:S(2)}) copy-start(f32[3,32,8,128]{3,2,1,0:T(8,128)} %param.4) | copy-start | bytes 1179652
  3.8 26.5 %all-to-all-start = ((f32[8,160,128]{2,1,0:T(8,128)}), f32[8,160,128]{2,1,0:T(8,128)S(1)}, u32[]{:S(2)}, u32[]{:S(2)}) async-start(f32[8,160,128]{2,1,0:T(8,128)} %bitcast.1), calls=%async_computation | async-start | bytes 1310720 | tf_op jit(solution)/shard_map/all_to_all | solution.py:414
  11.6 15.3 %collective-permute-start.1 = (f32[3,32,4,128]{3,2,1,0:T(4,128)S(1)}, f32[3,32,4,128]{3,2,1,0:T(4,128)S(1)}, u32[]{:S(2)}, u32[]{:S(2)}) collective-permute-start(f32[3,32,4,128]{3,2,1,0:T(4,128)S(1)} %get-tuple-element.33), channel_id=1, source_target_pairs={{96,0},{192,96},{288,192},{384,288},{480,384},{576,480},{672,576},... | collective-permute-start | bytes 589832 | tf_op jit(solution)/shard_map/ppermute | solution.py:61
  16.1 14.2 %collective-permute-start = (f32[3,32,4,128]{3,2,1,0:T(4,128)S(1)}, f32[3,32,4,128]{3,2,1,0:T(4,128)S(1)}, u32[]{:S(2)}, u32[]{:S(2)}) collective-permute-start(f32[3,32,4,128]{3,2,1,0:T(4,128)S(1)} %get-tuple-element.34), channel_id=1, source_target_pairs={{0,96},{96,192},{192,288},{288,384},{384,480},{480,576},{576,672},... | collective-permute-start | bytes 589832 | tf_op jit(solution)/shard_map/ppermute | solution.py:61
  30.4 9.8 %collective-permute-start.2 = (f32[3,4,16,128]{3,2,1,0:T(8,128)S(1)}, f32[3,4,16,128]{3,2,1,0:T(8,128)S(1)}, u32[]{:S(2)}, u32[]{:S(2)}) collective-permute-start(f32[3,4,16,128]{3,2,1,0:T(8,128)S(1)} %get-tuple-element.31), channel_id=1, source_target_pairs={{0,8},{8,16},{16,24},{24,32},{32,40},{40,48},{48,56},{56,64},{64,7... | collective-permute-start | bytes 294920 | tf_op jit(solution)/shard_map/ppermute | solution.py:61
  38.2 5.9 %collective-permute-start.3 = (f32[3,4,16,128]{3,2,1,0:T(8,128)S(1)}, f32[3,4,16,128]{3,2,1,0:T(8,128)S(1)}, u32[]{:S(2)}, u32[]{:S(2)}) collective-permute-start(f32[3,4,16,128]{3,2,1,0:T(8,128)S(1)} %get-tuple-element.32), channel_id=1, source_target_pairs={{8,0},{16,8},{24,16},{32,24},{40,32},{48,40},{56,48},{64,56},{72,6... | collective-permute-start | bytes 294920 | tf_op jit(solution)/shard_map/ppermute | solution.py:61
  44.2 32.0 %copy-start.4 = (s32[12]{0:T(128)S(1)}, s32[12]{0:T(128)}, u32[]{:S(2)}) copy-start(s32[12]{0:T(128)} %assign_ref.1) | copy-start | bytes 148
  45.4 76.3 %copy-start.1 = (f32[256,512]{1,0:T(8,128)S(1)}, f32[256,512]{1,0:T(8,128)}, u32[]{:S(2)}) copy-start(f32[256,512]{1,0:T(8,128)} %modes_ref.5) | copy-start | bytes 1572868
  45.4 76.3 %copy-start.5 = (s32[64]{0:T(128)S(1)}, s32[64]{0:T(128)}, u32[]{:S(2)}) copy-start(s32[64]{0:T(128)} %planes_ref.1) | copy-start | bytes 772
  164.7 37.3 %all-to-all-start.5 = ((f32[12,40,128]{2,1,0:T(8,128)}), f32[12,40,128]{2,1,0:T(8,128)}, u32[]{:S(2)}, u32[]{:S(2)}) async-start(f32[12,40,128]{2,1,0:T(8,128)} %broadcast_in_dim.4), calls=%async_computation.5 | async-start | bytes 491520 | tf_op jit(solution)/shard_map/all_to_all | solution.py:369
  201.2 0.8 copy-start.2
  218.1 1.0 copy-start.3

commit v5 on v4

--- a/solution.py
+++ b/solution.py
@@ -107,6 +107,18 @@
     return first, second
 
 
+def planes_each(section, first, last, unroll):
+    while (last - first) % unroll:
+        unroll -= 1
+
+    def step(i, _):
+        for k in range(unroll):
+            section(first + i * unroll + k)
+        return 0
+
+    lax.fori_loop(0, (last - first) // unroll, step, 0)
+
+
 def sections_kernel(
     assign_ref, row_ref, field_ref, edges_ref, out_ref, sent_ref, wide_ref, mid_ref, q_ref, place_ref
 ):
@@ -139,7 +151,7 @@
         convect = speeds[0] * dx_first + speeds[1] * dy_first + speeds[2] * dz_first
         return viscosity * ((dx_second + dy_second) + (dz_second - 90.0 * centre)) - convect
 
-    def first_section(z, _):
+    def first_section(z):
         speeds = [wide_ref[c, z] for c in range(comps)]
         for c in range(comps):
             along_z = [wide_ref[c, z + k] for k in (-2, -1, 1, 2)]
@@ -147,11 +159,10 @@
             q = (step_size / 12.0) * slope
             mid_ref[c, z] = jnp.where(outside, 0.0, speeds[c] + third * q)
             q_ref[c, z] = q[:across, :lanes]
-        return 0
-
-    lax.fori_loop(2, depth_wide - 2, first_section, 0)
-
-    def second_section(z, _):
+
+    planes_each(first_section, 2, depth_wide - 2, 3)
+
+    def second_section(z):
         speeds = [mid_ref[c, z, 0:across, 0:lanes] for c in range(comps)]
         for c in range(comps):
             along_z = [mid_ref[c, z + k, 0:across, 0:lanes] for k in (-2, -1, 1, 2)]
@@ -160,9 +171,8 @@
             slope = tendency(speeds, speeds[c], along_z, along_x, along_y)
             q = carry_back * q_ref[c, z] + (step_size / 12.0) * slope
             out_ref[c, z - WIDE] = speeds[c] + second_gain * q
-        return 0
-
-    lax.fori_loop(WIDE, WIDE + depth, second_section, 0)
+
+    planes_each(second_section, WIDE, WIDE + depth, 8)
 
     tiles = -(-comps * depth_wide // group)
     each = edges_ref.shape[1] - tiles * rows
@@ -292,39 +302,55 @@
     return slice(at, at + BLOCK)
 
 
-def modes_factor_kernel(gathered_ref, modes_ref, upper_out, inverse_out, done_ref, block_ref, side_ref, upper_ref, inverse_ref):
-    blocks = modes_ref.shape[1] // BLOCK
-    groups = gathered_ref.shape[0]
-    each = block_ref.shape[0] // groups
+def factor_step(b, blocks, block_ref, side_ref, upper_ref, inverse_ref):
     rows = BLOCK // 8
     lane = lax.broadcasted_iota(jnp.int32, (BLOCK, BLOCK), 1)
     sub = lax.broadcasted_iota(jnp.int32, (BLOCK, BLOCK), 0)
     unit = identity(BLOCK)
-    zero = jnp.zeros((BLOCK, BLOCK), jnp.float32)
+    value = block_ref[pair_rows(b, b), :]
+    value = jnp.where(lane >= sub, value, value.T)
+    main = [value[8 * i : 8 * i + 8, :] for i in range(rows)]
+    side = [unit[8 * i : 8 * i + 8, :] for i in range(rows)]
+    eliminate(main, side, upper_ref, inverse_ref, rows)
+    inverse = inverse_ref[...]
+    block_ref[pair_rows(b, b), :] = upper_ref[...]
+    side_ref[pair_rows(b, b), :] = inverse
+    for j in range(b):
+        side_ref[pair_rows(j, b), :] = product(inverse, side_ref[pair_rows(j, b), :], ((1,), (0,)))
+    for j in range(b + 1, blocks):
+        block_ref[pair_rows(b, j), :] = product(inverse, block_ref[pair_rows(b, j), :], ((1,), (0,)))
+    for i in range(b + 1, blocks):
+        factor = block_ref[pair_rows(b, i), :]
+        for j in range(i, blocks):
+            taken = product(factor, block_ref[pair_rows(b, j), :], ((0,), (0,)))
+            block_ref[pair_rows(i, j), :] = block_ref[pair_rows(i, j), :] - taken
+        for j in range(b):
+            taken = product(factor, side_ref[pair_rows(j, b), :], ((0,), (0,)))
+            side_ref[pair_rows(j, i), :] = side_ref[pair_rows(j, i), :] - taken
+        side_ref[pair_rows(b, i), :] = -product(factor, inverse, ((0,), (0,)))
+
+
+def first_factor_kernel(steps, blocks, gathered_ref, block_ref, side_ref, upper_ref, inverse_ref):
+    groups = gathered_ref.shape[0]
+    each = block_ref.shape[0] // groups
     for g in range(groups):
         block_ref[g * each : (g + 1) * each, :] = gathered_ref[g, gathered_ref.shape[1] - each :, :]
-    for b in range(blocks):
-        value = block_ref[pair_rows(b, b), :]
-        value = jnp.where(lane >= sub, value, value.T)
-        main = [value[8 * i : 8 * i + 8, :] for i in range(rows)]
-        side = [unit[8 * i : 8 * i + 8, :] for i in range(rows)]
-        eliminate(main, side, upper_ref, inverse_ref, rows)
-        inverse = inverse_ref[...]
-        block_ref[pair_rows(b, b), :] = upper_ref[...]
-        side_ref[pair_rows(b, b), :] = inverse
-        for j in range(b):
-            side_ref[pair_rows(j, b), :] = product(inverse, side_ref[pair_rows(j, b), :], ((1,), (0,)))
-        for j in range(b + 1, blocks):
-            block_ref[pair_rows(b, j), :] = product(inverse, block_ref[pair_rows(b, j), :], ((1,), (0,)))
-        for i in range(b + 1, blocks):
-            factor = block_ref[pair_rows(b, i), :]
-            for j in range(i, blocks):
-                taken = product(factor, block_ref[pair_rows(b, j), :], ((0,), (0,)))
-                block_ref[pair_rows(i, j), :] = block_ref[pair_rows(i, j), :] - taken
-            for j in range(b):
-                taken = product(factor, side_ref[pair_rows(j, b), :], ((0,), (0,)))
-                side_ref[pair_rows(j, i), :] = side_ref[pair_rows(j, i), :] - taken
-            side_ref[pair_rows(b, i), :] = -product(factor, inverse, ((0,), (0,)))
+    for b in range(steps, blocks):
+        for j in range(b, blocks):
+            side_ref[pair_rows(b, j), :] = jnp.zeros((BLOCK, BLOCK), jnp.float32)
+    for b in range(steps):
+        factor_step(b, blocks, block_ref, side_ref, upper_ref, inverse_ref)
+
+
+def last_factor_kernel(
+    steps, block_in, side_in, modes_ref, upper_out, inverse_out, done_ref, block_ref, side_ref, upper_ref, inverse_ref
+):
+    blocks = modes_ref.shape[1] // BLOCK
+    zero = jnp.zeros((BLOCK, BLOCK), jnp.float32)
+    block_ref[...] = block_in[...]
+    side_ref[...] = side_in[...]
+    for b in range(steps, blocks):
+        factor_step(b, blocks, block_ref, side_ref, upper_ref, inverse_ref)
     for i in range(blocks):
         for j in range(blocks):
             here = (slice(i * BLOCK, (i + 1) * BLOCK), slice(j * BLOCK, (j + 1) * BLOCK))
@@ -426,15 +452,21 @@
     both = lax.all_to_all(both, "grp", 0, 0, tiled=True)
     share = everyones(jnp.sum(both[:, :part], axis=0), "slab")
 
+    steps = blocks // 2
+    pair = [pltpu.VMEM((BLOCK, BLOCK), jnp.float32)] * 2
+    cost = 10 * 1000 * 1000 * 1000
+    lower = vmem_call(
+        functools.partial(first_factor_kernel, steps, blocks), [f32(rows, BLOCK)] * 2, [VM], scratch=pair, flops=cost
+    )(both)
+    share, *lower = lax.optimization_barrier((share, *lower))
+    packed = everyones(jnp.sum(share, axis=0), "row").reshape(tall, BLOCK)
     upper, inverse, done = vmem_call(
-        modes_factor_kernel,
+        functools.partial(last_factor_kernel, steps),
         [f32(rank, rank), f32(rank, rank), f32(rank, held)],
-        [VM, VM],
-        scratch=[pltpu.VMEM((rows, BLOCK), jnp.float32)] * 2 + [pltpu.VMEM((BLOCK, BLOCK), jnp.float32)] * 2,
-        flops=20 * 1000 * 1000 * 1000,
-    )(both, modes)
-    share, upper = lax.optimization_barrier((share, upper))
-    packed = everyones(jnp.sum(share, axis=0), "row").reshape(tall, BLOCK)
+        [VM, VM, VM],
+        scratch=[pltpu.VMEM((rows, BLOCK), jnp.float32)] * 2 + pair,
+        flops=cost,
+    )(*lower, modes)
     basis, factor = vmem_call(
         finish_kernel,
         [f32(rank + count, held), f32(rank + count, rank + count)],

time: 226 us -> 212 us (0.938)
  blocking collectives: 122 us -> 107 us
  starting transfers between devices: 36.2 us -> 39.8 us
  Pallas kernels: 44.5 us -> 41.1 us
    all_to_all x1 -> x0, blocking collectives: 15.1 us -> none  [everyones(): return lax.all_to_all(copies, axis, 0, 0, tiled=True)]
    pallas_call x1, Pallas kernels: 10.1 us -> 6.45 us  [sections(): vmem_call(sections_kernel, [f32(comps, depth, across, height), f32(pieces...]
    all_to_all x1 -> x2, starting transfers between devices: 12.4 us -> 16 us  [everyones(): return lax.all_to_all(copies, axis, 0, 0, tiled=True)]
    pallas_call x1 -> x2, Pallas kernels: 24.1 us -> 24.4 us  [the longest x1 12.6 us: on_device(): vmem_call(functools.partial(last_factor_kernel, steps), [f32(rank, rank),...]
  transfers between devices with their start and end apart: 6 -> 7, of which waited for: 3 -> 4; matrix products, arithmetic and copies ran while one was open for 0% -> 0% of each run, Pallas kernels for 11% -> 12%
where the time goes in v5:
time: 212 us; the launch traced here: 211 us
  blocking collectives  107 us (50%)
  Pallas kernels  41.1 us (19%)
  starting transfers between devices  39.8 us (19%)
  waiting for transfers between devices  16.9 us (8%)
  local copies, waits for them, and re-layouts  5.52 us (3%)
    all_to_all x1, blocking collectives, on_device(): received = lax.all_to_all(sent, 'slab', 0, 0, tiled=True)  35.3 us
    all_to_all x1, blocking collectives, sections(): edges = lax.all_to_all(edges, 'row', 0, 0, tiled=True)  30.8 us
    all_to_all x1, blocking collectives, on_device(): both = lax.all_to_all(both, 'grp', 0, 0, tiled=True)  24.8 us
    ppermute x4, waiting for transfers between devices, both_ways(): return (lax.ppermute(high, axis, up), lax.ppermute(low, axis, down))  16.2 us
    ppermute x4, starting transfers between devices, both_ways(): return (lax.ppermute(high, axis, up), lax.ppermute(low, axis, down))  16.2 us
    all_to_all x2, starting transfers between devices, everyones(): return lax.all_to_all(copies, axis, 0, 0, tiled=True)  16 us
    all_to_all x1, blocking collectives, on_device(): both = lax.all_to_all(both, 'row', 0, 0, tiled=True)  15.8 us
    pallas_call x1, Pallas kernels, on_device(): vmem_call(functools.partial(last_factor_kernel, steps), [f32(rank, rank),...  12.6 us
  transfers between devices with their start and end apart: 7, of which 4 were waited for; matrix products, arithmetic and copies ran while one was open for 0% of the time, Pallas kernels for 12%

profile of v5, /device:TPU:1, one launch (start us, length us, event | category | flops | bytes accessed | tf_op | source)
XLA Modules:
  0.0 211.1 jit_solution(15776646148565516014)
XLA Ops:
  0.6 1.0 copy-done
  1.7 2.2 %shard_map.67 = f32[1280,128]{1,0:T(8,128)} custom-call(f32[256,512]{1,0:T(8,128)S(1)} %copy-done), custom_call_target="tpu_custom_call" | custom-call | flops 805306368 | bytes 524288 | tf_op jit(solution)/shard_map/pallas_call | solution.py:439
  3.8 7.7 %all-to-all-start = ((f32[8,160,128]{2,1,0:T(8,128)}), f32[8,160,128]{2,1,0:T(8,128)S(1)}, u32[]{:S(2)}, u32[]{:S(2)}) async-start(f32[8,160,128]{2,1,0:T(8,128)} %bitcast.1), calls=%async_computation | async-start | bytes 1310720 | tf_op jit(solution)/shard_map/all_to_all | solution.py:440
  11.6 4.6 %collective-permute-start.1 = (f32[3,32,4,128]{3,2,1,0:T(4,128)S(1)}, f32[3,32,4,128]{3,2,1,0:T(4,128)S(1)}, u32[]{:S(2)}, u32[]{:S(2)}) collective-permute-start(f32[3,32,4,128]{3,2,1,0:T(4,128)S(1)} %get-tuple-element.39), channel_id=1, source_target_pairs={{96,0},{192,96},{288,192},{384,288},{480,384},{576,480},{672,576},... | collective-permute-start | bytes 589832 | tf_op jit(solution)/shard_map/ppermute | solution.py:61
  16.1 1.9 collective-permute-start
  18.1 8.7 %collective-permute-done.1 = f32[3,32,4,128]{3,2,1,0:T(4,128)S(1)} collective-permute-done((f32[3,32,4,128]{3,2,1,0:T(4,128)S(1)}, f32[3,32,4,128]{3,2,1,0:T(4,128)S(1)}, u32[]{:S(2)}, u32[]{:S(2)}) %collective-permute-start.1) | collective-permute-done | bytes 196640 | tf_op jit(solution)/shard_map/ppermute | solution.py:61
  26.8 3.6 %collective-permute-done = f32[3,32,4,128]{3,2,1,0:T(4,128)S(1)} collective-permute-done((f32[3,32,4,128]{3,2,1,0:T(4,128)S(1)}, f32[3,32,4,128]{3,2,1,0:T(4,128)S(1)}, u32[]{:S(2)}, u32[]{:S(2)}) %collective-permute-start) | collective-permute-done | bytes 196640 | tf_op jit(solution)/shard_map/ppermute | solution.py:61
  30.4 7.8 %collective-permute-start.2 = (f32[3,4,16,128]{3,2,1,0:T(8,128)S(1)}, f32[3,4,16,128]{3,2,1,0:T(8,128)S(1)}, u32[]{:S(2)}, u32[]{:S(2)}) collective-permute-start(f32[3,4,16,128]{3,2,1,0:T(8,128)S(1)} %get-tuple-element.37), channel_id=1, source_target_pairs={{0,8},{8,16},{16,24},{24,32},{32,40},{40,48},{48,56},{56,64},{64,7... | collective-permute-start | bytes 294920 | tf_op jit(solution)/shard_map/ppermute | solution.py:61
  38.2 1.9 collective-permute-start.3
  40.2 3.9 %collective-permute-done.3 = f32[3,4,16,128]{3,2,1,0:T(8,128)S(1)} collective-permute-done((f32[3,4,16,128]{3,2,1,0:T(8,128)S(1)}, f32[3,4,16,128]{3,2,1,0:T(8,128)S(1)}, u32[]{:S(2)}, u32[]{:S(2)}) %collective-permute-start.3) | collective-permute-done | bytes 98336 | tf_op jit(solution)/shard_map/ppermute | solution.py:61
  44.3 1.1 shard_map.68
  45.4 30.8 %all_to_all.35.edges_ref = f32[8,84,128]{2,1,0:T(8,128)S(1)} all-to-all(f32[8,84,128]{2,1,0:T(8,128)S(1)} %shard_map.68), channel_id=1, replica_groups=mesh['grp'=8,'slab'=12,'row'=8] {'row'}, dimensions={0} | all-to-all | bytes 688128 | tf_op jit(solution)/shard_map/all_to_all | solution.py:413
  76.2 6.4 %shard_map.69 = (f32[3,32,8,128]{3,2,1,0:T(8,128)}, f32[12,84,128]{2,1,0:T(8,128)S(1)}) custom-call(s32[12]{0:T(128)S(1)} %copy-done.2, s32[2]{0:T(128)S(1)} %pad_add_fusion.row_ref, f32[3,40,16,128]{3,2,1,0:T(8,128)S(1)} %pad_maximum_fusion.field_ref, f32[8,84,128]{2,1,0:T(8,128)S(1)} %all_to_all.35.edges_ref), custom_call_target="tpu_custom_call" | custom-call | bytes 7864320 | tf_op jit(solution)/shard_map/pallas_call | solution.py:416
  82.7 35.3 %all_to_all.36.received_ref = f32[12,84,128]{2,1,0:T(8,128)S(1)} all-to-all(f32[12,84,128]{2,1,0:T(8,128)S(1)} %get-tuple-element.24), channel_id=1, replica_groups=mesh['grp'=8,'slab'=12,'row'=8] {'slab'}, dimensions={0} | all-to-all | bytes 1032192 | tf_op jit(solution)/shard_map/all_to_all | solution.py:442
  118.0 1.6 shard_map.70
  119.6 15.8 %all_to_all.37.received_ref = f32[8,60,128]{2,1,0:T(8,128)S(1)} all-to-all(f32[8,60,128]{2,1,0:T(8,128)S(1)} %get-tuple-element.25), channel_id=1, replica_groups=mesh['grp'=8,'slab'=12,'row'=8] {'row'}, dimensions={0} | all-to-all | bytes 491520 | tf_op jit(solution)/shard_map/all_to_all | solution.py:450
  135.5 24.8 %all_to_all.38.gathered_ref = f32[8,200,128]{2,1,0:T(8,128)S(1)} all-to-all(f32[8,200,128]{2,1,0:T(8,128)S(1)} %shard_map.71), channel_id=1, replica_groups=mesh['grp'=8,'slab'=12,'row'=8] {'grp'}, dimensions={0} | all-to-all | bytes 1638400 | tf_op jit(solution)/shard_map/all_to_all | solution.py:452
  161.0 12.4 %all-to-all-start.5 = ((f32[12,40,128]{2,1,0:T(8,128)}), f32[12,40,128]{2,1,0:T(8,128)S(1)}, u32[]{:S(2)}, u32[]{:S(2)}) async-start(f32[12,40,128]{2,1,0:T(8,128)} %broadcast_in_dim.4), calls=%async_computation.5 | async-start | bytes 491520 | tf_op jit(solution)/shard_map/all_to_all | solution.py:395
  173.4 11.8 %shard_map.72 = (f32[1280,128]{1,0:T(8,128)S(1)}, f32[1280,128]{1,0:T(8,128)S(1)}) custom-call(f32[8,200,128]{2,1,0:T(8,128)S(1)} %all_to_all.38.gathered_ref), custom_call_target="tpu_custom_call" | custom-call | flops 10000000000 | tf_op jit(solution)/shard_map/pallas_call | solution.py:458
  187.4 3.6 %all-to-all-start.6 = ((f32[8,40,128]{2,1,0:T(8,128)}), f32[8,40,128]{2,1,0:T(8,128)S(1)}, u32[]{:S(2)}, u32[]{:S(2)}) async-start(f32[8,40,128]{2,1,0:T(8,128)} %broadcast_in_dim.5), calls=%async_computation.6 | async-start | bytes 327680 | tf_op jit(solution)/shard_map/all_to_all | solution.py:395
  191.1 1.1 copy-done.5
  192.1 1.1 copy-done.7
  193.2 12.6 %shard_map.73 = (f32[512,512]{1,0:T(8,128)S(1)}, f32[512,512]{1,0:T(8,128)S(1)}, f32[512,256]{1,0:T(8,128)S(1)}) custom-call(f32[1280,128]{1,0:T(8,128)S(1)} %copy-done.5, f32[1280,128]{1,0:T(8,128)S(1)} %copy-done.7, f32[256,512]{1,0:T(8,128)S(1)} %copy-done.1), custom_call_target="tpu_custom_call" | custom-call | flops 10000000000 | tf_op jit(solution)/shard_map/pallas_call | solution.py:463
  205.8 5.3 %shard_map.74 = (f32[576,256]{1,0:T(8,128)}, f32[576,576]{1,0:T(8,128)}) custom-call(f32[320,128]{1,0:T(8,128)S(1)} %bitcast.4, f32[64,256]{1,0:T(8,128)S(1)} %get-tuple-element.29.snap_ref, f32[512,512]{1,0:T(8,128)S(1)} %get-tuple-element.32.upper_ref, f32[512,512]{1,0:T(8,128)S(1)} %get-tuple-element.33.inverse_ref, f32[512,256]{1,0:T(8,128)S(1)} %get-tuple-element.34.done_ref), custom_call_target="tpu_custom_call" | custom-call | tf_op jit(solution)/shard_map/pallas_call | solution.py:470
  (28 shorter events, 3.3 us)
Async XLA Ops:
  0.6 1.0 copy-start
  1.7 9.8 %copy-start.8 = (f32[3,32,8,128]{3,2,1,0:T(8,128)S(1)}, f32[3,32,8,128]{3,2,1,0:T(8,128)}, u32[]{:S(2)}) copy-start(f32[3,32,8,128]{3,2,1,0:T(8,128)} %param.4) | copy-start | bytes 1179652
  3.8 26.5 %all-to-all-start = ((f32[8,160,128]{2,1,0:T(8,128)}), f32[8,160,128]{2,1,0:T(8,128)S(1)}, u32[]{:S(2)}, u32[]{:S(2)}) async-start(f32[8,160,128]{2,1,0:T(8,128)} %bitcast.1), calls=%async_computation | async-start | bytes 1310720 | tf_op jit(solution)/shard_map/all_to_all | solution.py:440
  11.6 15.3 %collective-permute-start.1 = (f32[3,32,4,128]{3,2,1,0:T(4,128)S(1)}, f32[3,32,4,128]{3,2,1,0:T(4,128)S(1)}, u32[]{:S(2)}, u32[]{:S(2)}) collective-permute-start(f32[3,32,4,128]{3,2,1,0:T(4,128)S(1)} %get-tuple-element.39), channel_id=1, source_target_pairs={{96,0},{192,96},{288,192},{384,288},{480,384},{576,480},{672,576},... | collective-permute-start | bytes 589832 | tf_op jit(solution)/shard_map/ppermute | solution.py:61
  16.1 14.2 %collective-permute-start = (f32[3,32,4,128]{3,2,1,0:T(4,128)S(1)}, f32[3,32,4,128]{3,2,1,0:T(4,128)S(1)}, u32[]{:S(2)}, u32[]{:S(2)}) collective-permute-start(f32[3,32,4,128]{3,2,1,0:T(4,128)S(1)} %get-tuple-element.40), channel_id=1, source_target_pairs={{0,96},{96,192},{192,288},{288,384},{384,480},{480,576},{576,672},... | collective-permute-start | bytes 589832 | tf_op jit(solution)/shard_map/ppermute | solution.py:61
  30.4 9.8 %collective-permute-start.2 = (f32[3,4,16,128]{3,2,1,0:T(8,128)S(1)}, f32[3,4,16,128]{3,2,1,0:T(8,128)S(1)}, u32[]{:S(2)}, u32[]{:S(2)}) collective-permute-start(f32[3,4,16,128]{3,2,1,0:T(8,128)S(1)} %get-tuple-element.37), channel_id=1, source_target_pairs={{0,8},{8,16},{16,24},{24,32},{32,40},{40,48},{48,56},{56,64},{64,7... | collective-permute-start | bytes 294920 | tf_op jit(solution)/shard_map/ppermute | solution.py:61
  38.2 5.9 %collective-permute-start.3 = (f32[3,4,16,128]{3,2,1,0:T(8,128)S(1)}, f32[3,4,16,128]{3,2,1,0:T(8,128)S(1)}, u32[]{:S(2)}, u32[]{:S(2)}) collective-permute-start(f32[3,4,16,128]{3,2,1,0:T(8,128)S(1)} %get-tuple-element.38), channel_id=1, source_target_pairs={{8,0},{16,8},{24,16},{32,24},{40,32},{48,40},{56,48},{64,56},{72,6... | collective-permute-start | bytes 294920 | tf_op jit(solution)/shard_map/ppermute | solution.py:61
  44.2 32.0 %copy-start.2 = (s32[12]{0:T(128)S(1)}, s32[12]{0:T(128)}, u32[]{:S(2)}) copy-start(s32[12]{0:T(128)} %assign_ref.1) | copy-start | bytes 148
  45.4 72.6 %copy-start.1 = (f32[256,512]{1,0:T(8,128)S(1)}, f32[256,512]{1,0:T(8,128)}, u32[]{:S(2)}) copy-start(f32[256,512]{1,0:T(8,128)} %modes_ref.5) | copy-start | bytes 1572868
  45.4 72.6 %copy-start.3 = (s32[64]{0:T(128)S(1)}, s32[64]{0:T(128)}, u32[]{:S(2)}) copy-start(s32[64]{0:T(128)} %planes_ref.1) | copy-start | bytes 772
  161.0 25.7 %all-to-all-start.5 = ((f32[12,40,128]{2,1,0:T(8,128)}), f32[12,40,128]{2,1,0:T(8,128)S(1)}, u32[]{:S(2)}, u32[]{:S(2)}) async-start(f32[12,40,128]{2,1,0:T(8,128)} %broadcast_in_dim.4), calls=%async_computation.5 | async-start | bytes 491520 | tf_op jit(solution)/shard_map/all_to_all | solution.py:395
  185.2 0.8 copy-start.6
  186.0 1.4 copy-start.4
  187.4 18.4 %all-to-all-start.6 = ((f32[8,40,128]{2,1,0:T(8,128)}), f32[8,40,128]{2,1,0:T(8,128)S(1)}, u32[]{:S(2)}, u32[]{:S(2)}) async-start(f32[8,40,128]{2,1,0:T(8,128)} %broadcast_in_dim.5), calls=%async_computation.6 | async-start | bytes 327680 | tf_op jit(solution)/shard_map/all_to_all | solution.py:395
  191.0 1.1 copy-start.5
  192.1 1.1 copy-start.7

commit v6 on v5

--- a/solution.py
+++ b/solution.py
@@ -160,7 +160,7 @@
             mid_ref[c, z] = jnp.where(outside, 0.0, speeds[c] + third * q)
             q_ref[c, z] = q[:across, :lanes]
 
-    planes_each(first_section, 2, depth_wide - 2, 3)
+    planes_each(first_section, 2, depth_wide - 2, 6)
 
     def second_section(z):
         speeds = [mid_ref[c, z, 0:across, 0:lanes] for c in range(comps)]
@@ -172,7 +172,7 @@
             q = carry_back * q_ref[c, z] + (step_size / 12.0) * slope
             out_ref[c, z - WIDE] = speeds[c] + second_gain * q
 
-    planes_each(second_section, WIDE, WIDE + depth, 8)
+    planes_each(second_section, WIDE, WIDE + depth, 16)
 
     tiles = -(-comps * depth_wide // group)
     each = edges_ref.shape[1] - tiles * rows
@@ -335,9 +335,6 @@
     each = block_ref.shape[0] // groups
     for g in range(groups):
         block_ref[g * each : (g + 1) * each, :] = gathered_ref[g, gathered_ref.shape[1] - each :, :]
-    for b in range(steps, blocks):
-        for j in range(b, blocks):
-            side_ref[pair_rows(b, j), :] = jnp.zeros((BLOCK, BLOCK), jnp.float32)
     for b in range(steps):
         factor_step(b, blocks, block_ref, side_ref, upper_ref, inverse_ref)
 
@@ -348,7 +345,7 @@
     blocks = modes_ref.shape[1] // BLOCK
     zero = jnp.zeros((BLOCK, BLOCK), jnp.float32)
     block_ref[...] = block_in[...]
-    side_ref[...] = side_in[...]
+    side_ref[0 : side_in.shape[0], :] = side_in[...]
     for b in range(steps, blocks):
         factor_step(b, blocks, block_ref, side_ref, upper_ref, inverse_ref)
     for i in range(blocks):
@@ -456,7 +453,11 @@
     pair = [pltpu.VMEM((BLOCK, BLOCK), jnp.float32)] * 2
     cost = 10 * 1000 * 1000 * 1000
     lower = vmem_call(
-        functools.partial(first_factor_kernel, steps, blocks), [f32(rows, BLOCK)] * 2, [VM], scratch=pair, flops=cost
+        functools.partial(first_factor_kernel, steps, blocks),
+        [f32(rows, BLOCK), f32(pair_index(steps, steps) * BLOCK, BLOCK)],
+        [VM],
+        scratch=pair,
+        flops=cost,
     )(both)
     share, *lower = lax.optimization_barrier((share, *lower))
     packed = everyones(jnp.sum(share, axis=0), "row").reshape(tall, BLOCK)

time: 212 us -> 212 us (level)
  no operation moved by 1% of the time
where the time goes in v6:
time: 212 us; the launch traced here: 211 us
  blocking collectives  107 us (50%)
  Pallas kernels  40.8 us (19%)
  starting transfers between devices  39.8 us (19%)
  waiting for transfers between devices  17 us (8%)
  local copies, waits for them, and re-layouts  5.36 us (3%)
    all_to_all x1, blocking collectives, on_device(): received = lax.all_to_all(sent, 'slab', 0, 0, tiled=True)  35.3 us
    all_to_all x1, blocking collectives, sections(): edges = lax.all_to_all(edges, 'row', 0, 0, tiled=True)  30.8 us
    all_to_all x1, blocking collectives, on_device(): both = lax.all_to_all(both, 'grp', 0, 0, tiled=True)  24.8 us
    ppermute x4, waiting for transfers between devices, both_ways(): return (lax.ppermute(high, axis, up), lax.ppermute(low, axis, down))  16.2 us
    ppermute x4, starting transfers between devices, both_ways(): return (lax.ppermute(high, axis, up), lax.ppermute(low, axis, down))  16.2 us
    all_to_all x2, starting transfers between devices, everyones(): return lax.all_to_all(copies, axis, 0, 0, tiled=True)  16 us
    all_to_all x1, blocking collectives, on_device(): both = lax.all_to_all(both, 'row', 0, 0, tiled=True)  15.8 us
    pallas_call x1, Pallas kernels, on_device(): vmem_call(functools.partial(last_factor_kernel, steps), [f32(rank, rank),...  12.6 us
  transfers between devices with their start and end apart: 7, of which 4 were waited for; matrix products, arithmetic and copies ran while one was open for 0% of the time, Pallas kernels for 12%

profile of v6, /device:TPU:1, one launch (start us, length us, event | category | flops | bytes accessed | tf_op | source)
XLA Modules:
  0.0 210.8 jit_solution(6454605942635032312)
XLA Ops:
  0.6 1.0 copy-done
  1.7 2.2 %shard_map.67 = f32[1280,128]{1,0:T(8,128)} custom-call(f32[256,512]{1,0:T(8,128)S(1)} %copy-done), custom_call_target="tpu_custom_call" | custom-call | flops 805306368 | bytes 524288 | tf_op jit(solution)/shard_map/pallas_call | solution.py:436
  3.8 7.7 %all-to-all-start = ((f32[8,160,128]{2,1,0:T(8,128)}), f32[8,160,128]{2,1,0:T(8,128)S(1)}, u32[]{:S(2)}, u32[]{:S(2)}) async-start(f32[8,160,128]{2,1,0:T(8,128)} %bitcast.1), calls=%async_computation | async-start | bytes 1310720 | tf_op jit(solution)/shard_map/all_to_all | solution.py:437
  11.6 4.6 %collective-permute-start.1 = (f32[3,32,4,128]{3,2,1,0:T(4,128)S(1)}, f32[3,32,4,128]{3,2,1,0:T(4,128)S(1)}, u32[]{:S(2)}, u32[]{:S(2)}) collective-permute-start(f32[3,32,4,128]{3,2,1,0:T(4,128)S(1)} %get-tuple-element.39), channel_id=1, source_target_pairs={{96,0},{192,96},{288,192},{384,288},{480,384},{576,480},{672,576},... | collective-permute-start | bytes 589832 | tf_op jit(solution)/shard_map/ppermute | solution.py:61
  16.1 1.9 collective-permute-start
  18.1 8.7 %collective-permute-done.1 = f32[3,32,4,128]{3,2,1,0:T(4,128)S(1)} collective-permute-done((f32[3,32,4,128]{3,2,1,0:T(4,128)S(1)}, f32[3,32,4,128]{3,2,1,0:T(4,128)S(1)}, u32[]{:S(2)}, u32[]{:S(2)}) %collective-permute-start.1) | collective-permute-done | bytes 196640 | tf_op jit(solution)/shard_map/ppermute | solution.py:61
  26.8 3.6 %collective-permute-done = f32[3,32,4,128]{3,2,1,0:T(4,128)S(1)} collective-permute-done((f32[3,32,4,128]{3,2,1,0:T(4,128)S(1)}, f32[3,32,4,128]{3,2,1,0:T(4,128)S(1)}, u32[]{:S(2)}, u32[]{:S(2)}) %collective-permute-start) | collective-permute-done | bytes 196640 | tf_op jit(solution)/shard_map/ppermute | solution.py:61
  30.4 7.8 %collective-permute-start.2 = (f32[3,4,16,128]{3,2,1,0:T(8,128)S(1)}, f32[3,4,16,128]{3,2,1,0:T(8,128)S(1)}, u32[]{:S(2)}, u32[]{:S(2)}) collective-permute-start(f32[3,4,16,128]{3,2,1,0:T(8,128)S(1)} %get-tuple-element.37), channel_id=1, source_target_pairs={{0,8},{8,16},{16,24},{24,32},{32,40},{40,48},{48,56},{56,64},{64,7... | collective-permute-start | bytes 294920 | tf_op jit(solution)/shard_map/ppermute | solution.py:61
  38.2 1.9 collective-permute-start.3
  40.2 3.9 %collective-permute-done.3 = f32[3,4,16,128]{3,2,1,0:T(8,128)S(1)} collective-permute-done((f32[3,4,16,128]{3,2,1,0:T(8,128)S(1)}, f32[3,4,16,128]{3,2,1,0:T(8,128)S(1)}, u32[]{:S(2)}, u32[]{:S(2)}) %collective-permute-start.3) | collective-permute-done | bytes 98336 | tf_op jit(solution)/shard_map/ppermute | solution.py:61
  44.3 1.1 shard_map.68
  45.4 30.8 %all_to_all.35.edges_ref = f32[8,84,128]{2,1,0:T(8,128)S(1)} all-to-all(f32[8,84,128]{2,1,0:T(8,128)S(1)} %shard_map.68), channel_id=1, replica_groups=mesh['grp'=8,'slab'=12,'row'=8] {'row'}, dimensions={0} | all-to-all | bytes 688128 | tf_op jit(solution)/shard_map/all_to_all | solution.py:410
  76.2 6.2 %shard_map.69 = (f32[3,32,8,128]{3,2,1,0:T(8,128)}, f32[12,84,128]{2,1,0:T(8,128)S(1)}) custom-call(s32[12]{0:T(128)S(1)} %copy-done.2, s32[2]{0:T(128)S(1)} %pad_add_fusion.row_ref, f32[3,40,16,128]{3,2,1,0:T(8,128)S(1)} %pad_maximum_fusion.field_ref, f32[8,84,128]{2,1,0:T(8,128)S(1)} %all_to_all.35.edges_ref), custom_call_target="tpu_custom_call" | custom-call | bytes 7864320 | tf_op jit(solution)/shard_map/pallas_call | solution.py:413
  82.4 35.3 %all_to_all.36.received_ref = f32[12,84,128]{2,1,0:T(8,128)S(1)} all-to-all(f32[12,84,128]{2,1,0:T(8,128)S(1)} %get-tuple-element.24), channel_id=1, replica_groups=mesh['grp'=8,'slab'=12,'row'=8] {'slab'}, dimensions={0} | all-to-all | bytes 1032192 | tf_op jit(solution)/shard_map/all_to_all | solution.py:439
  117.7 1.6 shard_map.70
  119.3 15.8 %all_to_all.37.received_ref = f32[8,60,128]{2,1,0:T(8,128)S(1)} all-to-all(f32[8,60,128]{2,1,0:T(8,128)S(1)} %get-tuple-element.25), channel_id=1, replica_groups=mesh['grp'=8,'slab'=12,'row'=8] {'row'}, dimensions={0} | all-to-all | bytes 491520 | tf_op jit(solution)/shard_map/all_to_all | solution.py:447
  135.2 24.8 %all_to_all.38.gathered_ref = f32[8,200,128]{2,1,0:T(8,128)S(1)} all-to-all(f32[8,200,128]{2,1,0:T(8,128)S(1)} %shard_map.71), channel_id=1, replica_groups=mesh['grp'=8,'slab'=12,'row'=8] {'grp'}, dimensions={0} | all-to-all | bytes 1638400 | tf_op jit(solution)/shard_map/all_to_all | solution.py:449
  160.8 12.4 %all-to-all-start.5 = ((f32[12,40,128]{2,1,0:T(8,128)}), f32[12,40,128]{2,1,0:T(8,128)S(1)}, u32[]{:S(2)}, u32[]{:S(2)}) async-start(f32[12,40,128]{2,1,0:T(8,128)} %broadcast_in_dim.4), calls=%async_computation.5 | async-start | bytes 491520 | tf_op jit(solution)/shard_map/all_to_all | solution.py:392
  173.1 11.8 %shard_map.72 = (f32[1280,128]{1,0:T(8,128)S(1)}, f32[896,128]{1,0:T(8,128)S(1)}) custom-call(f32[8,200,128]{2,1,0:T(8,128)S(1)} %all_to_all.38.gathered_ref), custom_call_target="tpu_custom_call" | custom-call | flops 10000000000 | tf_op jit(solution)/shard_map/pallas_call | solution.py:455
  187.2 3.6 %all-to-all-start.6 = ((f32[8,40,128]{2,1,0:T(8,128)}), f32[8,40,128]{2,1,0:T(8,128)S(1)}, u32[]{:S(2)}, u32[]{:S(2)}) async-start(f32[8,40,128]{2,1,0:T(8,128)} %broadcast_in_dim.5), calls=%async_computation.6 | async-start | bytes 327680 | tf_op jit(solution)/shard_map/all_to_all | solution.py:392
  190.8 1.1 copy-done.5
  191.9 1.0 copy-done.7
  192.9 12.6 %shard_map.73 = (f32[512,512]{1,0:T(8,128)S(1)}, f32[512,512]{1,0:T(8,128)S(1)}, f32[512,256]{1,0:T(8,128)S(1)}) custom-call(f32[1280,128]{1,0:T(8,128)S(1)} %copy-done.5, f32[896,128]{1,0:T(8,128)S(1)} %copy-done.7, f32[256,512]{1,0:T(8,128)S(1)} %copy-done.1), custom_call_target="tpu_custom_call" | custom-call | flops 10000000000 | tf_op jit(solution)/shard_map/pallas_call | solution.py:464
  205.5 5.3 %shard_map.74 = (f32[576,256]{1,0:T(8,128)}, f32[576,576]{1,0:T(8,128)}) custom-call(f32[320,128]{1,0:T(8,128)S(1)} %bitcast.4, f32[64,256]{1,0:T(8,128)S(1)} %get-tuple-element.29.snap_ref, f32[512,512]{1,0:T(8,128)S(1)} %get-tuple-element.32.upper_ref, f32[512,512]{1,0:T(8,128)S(1)} %get-tuple-element.33.inverse_ref, f32[512,256]{1,0:T(8,128)S(1)} %get-tuple-element.34.done_ref), custom_call_target="tpu_custom_call" | custom-call | tf_op jit(solution)/shard_map/pallas_call | solution.py:471
  (28 shorter events, 3.3 us)
Async XLA Ops:
  0.6 1.0 copy-start
  1.7 9.8 %copy-start.8 = (f32[3,32,8,128]{3,2,1,0:T(8,128)S(1)}, f32[3,32,8,128]{3,2,1,0:T(8,128)}, u32[]{:S(2)}) copy-start(f32[3,32,8,128]{3,2,1,0:T(8,128)} %param.4) | copy-start | bytes 1179652
  3.8 26.5 %all-to-all-start = ((f32[8,160,128]{2,1,0:T(8,128)}), f32[8,160,128]{2,1,0:T(8,128)S(1)}, u32[]{:S(2)}, u32[]{:S(2)}) async-start(f32[8,160,128]{2,1,0:T(8,128)} %bitcast.1), calls=%async_computation | async-start | bytes 1310720 | tf_op jit(solution)/shard_map/all_to_all | solution.py:437
  11.6 15.3 %collective-permute-start.1 = (f32[3,32,4,128]{3,2,1,0:T(4,128)S(1)}, f32[3,32,4,128]{3,2,1,0:T(4,128)S(1)}, u32[]{:S(2)}, u32[]{:S(2)}) collective-permute-start(f32[3,32,4,128]{3,2,1,0:T(4,128)S(1)} %get-tuple-element.39), channel_id=1, source_target_pairs={{96,0},{192,96},{288,192},{384,288},{480,384},{576,480},{672,576},... | collective-permute-start | bytes 589832 | tf_op jit(solution)/shard_map/ppermute | solution.py:61
  16.1 14.2 %collective-permute-start = (f32[3,32,4,128]{3,2,1,0:T(4,128)S(1)}, f32[3,32,4,128]{3,2,1,0:T(4,128)S(1)}, u32[]{:S(2)}, u32[]{:S(2)}) collective-permute-start(f32[3,32,4,128]{3,2,1,0:T(4,128)S(1)} %get-tuple-element.40), channel_id=1, source_target_pairs={{0,96},{96,192},{192,288},{288,384},{384,480},{480,576},{576,672},... | collective-permute-start | bytes 589832 | tf_op jit(solution)/shard_map/ppermute | solution.py:61
  30.4 9.8 %collective-permute-start.2 = (f32[3,4,16,128]{3,2,1,0:T(8,128)S(1)}, f32[3,4,16,128]{3,2,1,0:T(8,128)S(1)}, u32[]{:S(2)}, u32[]{:S(2)}) collective-permute-start(f32[3,4,16,128]{3,2,1,0:T(8,128)S(1)} %get-tuple-element.37), channel_id=1, source_target_pairs={{0,8},{8,16},{16,24},{24,32},{32,40},{40,48},{48,56},{56,64},{64,7... | collective-permute-start | bytes 294920 | tf_op jit(solution)/shard_map/ppermute | solution.py:61
  38.2 5.9 %collective-permute-start.3 = (f32[3,4,16,128]{3,2,1,0:T(8,128)S(1)}, f32[3,4,16,128]{3,2,1,0:T(8,128)S(1)}, u32[]{:S(2)}, u32[]{:S(2)}) collective-permute-start(f32[3,4,16,128]{3,2,1,0:T(8,128)S(1)} %get-tuple-element.38), channel_id=1, source_target_pairs={{8,0},{16,8},{24,16},{32,24},{40,32},{48,40},{56,48},{64,56},{72,6... | collective-permute-start | bytes 294920 | tf_op jit(solution)/shard_map/ppermute | solution.py:61
  44.2 32.0 %copy-start.2 = (s32[12]{0:T(128)S(1)}, s32[12]{0:T(128)}, u32[]{:S(2)}) copy-start(s32[12]{0:T(128)} %assign_ref.1) | copy-start | bytes 148
  45.4 72.3 %copy-start.1 = (f32[256,512]{1,0:T(8,128)S(1)}, f32[256,512]{1,0:T(8,128)}, u32[]{:S(2)}) copy-start(f32[256,512]{1,0:T(8,128)} %modes_ref.5) | copy-start | bytes 1572868
  45.4 72.3 %copy-start.3 = (s32[64]{0:T(128)S(1)}, s32[64]{0:T(128)}, u32[]{:S(2)}) copy-start(s32[64]{0:T(128)} %planes_ref.1) | copy-start | bytes 772
  160.8 25.7 %all-to-all-start.5 = ((f32[12,40,128]{2,1,0:T(8,128)}), f32[12,40,128]{2,1,0:T(8,128)S(1)}, u32[]{:S(2)}, u32[]{:S(2)}) async-start(f32[12,40,128]{2,1,0:T(8,128)} %broadcast_in_dim.4), calls=%async_computation.5 | async-start | bytes 491520 | tf_op jit(solution)/shard_map/all_to_all | solution.py:392
  184.9 0.8 copy-start.6
  185.7 1.5 copy-start.4
  187.2 18.3 %all-to-all-start.6 = ((f32[8,40,128]{2,1,0:T(8,128)}), f32[8,40,128]{2,1,0:T(8,128)S(1)}, u32[]{:S(2)}, u32[]{:S(2)}) async-start(f32[8,40,128]{2,1,0:T(8,128)} %broadcast_in_dim.5), calls=%async_computation.6 | async-start | bytes 327680 | tf_op jit(solution)/shard_map/all_to_all | solution.py:392
  190.8 1.1 copy-start.5
  191.9 1.0 copy-start.7
